TPU v7x, 256 devices: a whole 4x4x8 slice. The times are simulated.
256 devices in a mesh: blk: 64 (over z, y, x_lo), hop: 4 (over x_hi, core).
Axes of the slice: x: 4 (x_hi: 2, x_lo: 2; x = x_hi * 2 + x_lo), y: 4, z: 8, core: 2. Of those that a mesh axis runs over, the one named last changes fastest.
Arguments:
- user_factors: float32 [196608, 256], P(('blk', 'hop')), may hold values from -1.5 to 1.5
- item_factors: float32 [131072, 256], P(('blk', 'hop')), may hold values from -1.5 to 1.5
- ratings: bfloat16 [196608, 5, 512], P(('blk', 'hop')), may hold values from -4 to 4, as said below
- block_mask: int32 [1536, 5, 4], P(('blk', 'hop')), may hold values from 0 to 1, as said below
Outputs:
- new_users: float32 [196608, 256], P(('blk', 'hop'))
- new_items: float32 [131072, 256], P(('blk', 'hop'))
Inputs may be any that keep to these rules, and one draw needn't show every extreme that they name: `ratings`: zero marks a rating that is not observed; every other entry has magnitude 0.05 or more. `block_mask`: 1 marks a 128-square block that holds ratings; in every stratum some user shard has all of its blocks marked.
All inputs are finite; a program needn't handle non-finite values.
Results may differ from a plain program's by a relative error of at most 0.0024.
Values sent between devices are 32-bit elements; how exact they have to be, the bound alone decides.
A program may use at most 64 MiB of HBM per device.

v0:
```python
import jax
import jax.numpy as jnp
from jax import lax
from jax.sharding import PartitionSpec as P

CLIP_LIMIT = 3.0
DECAY = 0.03
RATE = 4.0


def from_behind(block, axis, distance):
    devices = range(lax.axis_size(axis))
    route = [((i - distance) % len(devices), i) for i in devices]
    return lax.ppermute(block, axis, route)


def errors(user_bf, item_bf, tile_rates, observed):
    predicted = jnp.einsum("ik,jk->ij", user_bf, item_bf, preferred_element_type=jnp.float32)
    misfit = jnp.clip(tile_rates.astype(jnp.float32) - predicted, -CLIP_LIMIT, CLIP_LIMIT)
    return jnp.where(observed, misfit, 0.0).astype(jnp.bfloat16)


def expand(tile_rates, tile_flags):
    row_blocks, col_blocks = tile_flags.shape
    block_side = tile_rates.shape[0] // row_blocks
    nonzero = tile_rates.reshape(row_blocks, block_side, col_blocks, block_side) != 0
    return (nonzero & (tile_flags[:, None, :, None] > 0)).reshape(tile_rates.shape)


def user_pass(user_rows, item_bf, tile_rates, observed, user_rate):
    user_bf = user_rows.astype(jnp.bfloat16)
    misfit = errors(user_bf, item_bf, tile_rates, observed)
    gradient = jnp.dot(misfit, item_bf, preferred_element_type=jnp.float32)
    return (1.0 - DECAY) * user_rows + user_rate * gradient


def item_pass(user_bf, item_rows, item_bf, tile_rates, observed, item_rate):
    misfit = errors(user_bf, item_bf, tile_rates, observed)
    gradient = jnp.einsum("ij,ik->jk", misfit, user_bf, preferred_element_type=jnp.float32)
    return (1.0 - DECAY) * item_rows + item_rate * gradient


def move_whole(updated, stratum, strata):
    if stratum < strata - 2:
        return from_behind(updated, "blk", 1)
    if stratum == strata - 2:
        return from_behind(updated, "hop", 1)
    return updated


def body(user_factors, item_factors, ratings, block_mask):
    row_count = user_factors.shape[0]
    item_count = item_factors.shape[0]
    strata = ratings.shape[1]
    user_rate = RATE / item_count
    item_rate = RATE / row_count
    user_rows = user_factors
    item_rows = item_factors
    for stratum in range(strata):
        tile_rates = ratings[:, stratum, :]
        tile_flags = block_mask[:, stratum, :]
        observed = expand(tile_rates, tile_flags)
        item_bf = item_rows.astype(jnp.bfloat16)
        user_rows = user_pass(user_rows, item_bf, tile_rates, observed, user_rate)
        user_bf = user_rows.astype(jnp.bfloat16)
        updated = item_pass(user_bf, item_rows, item_bf, tile_rates, observed, item_rate)
        item_rows = move_whole(updated, stratum, strata)
    returned = from_behind(item_rows, "blk", -(strata - 2))
    returned = from_behind(returned, "hop", -1)
    return (user_rows, returned)


def solution(mesh):
    in_specs = (
        P(("blk", "hop"), None),
        P(("blk", "hop"), None),
        P(("blk", "hop"), None, None),
        P(("blk", "hop"), None, None),
    )
    out_specs = (P(("blk", "hop"), None), P(("blk", "hop"), None))
    return jax.shard_map(body, mesh=mesh, in_specs=in_specs, out_specs=out_specs, check_vma=False)
```

profile of v0, /device:TPU:1, one launch (start us, length us, event | category | flops | bytes accessed | tf_op | source)
XLA Modules:
  0.0 125.3 jit_solution(2294547212663777257)
XLA Ops:
  0.6 0.8 fusion.151
  1.4 0.1 copy.6
  1.5 0.3 and.55
  1.8 0.0 copy-start
  1.8 2.8 %fusion.46 = f32[768,256]{1,0:T(8,128)S(1)} fusion(f32[768,256]{1,0:T(8,128)} %param.4, bf16[768,5,512]{2,0,1:T(8,128)(2,1)} %param.6, f32[512,256]{1,0:T(8,128)} %param.5, pred[96,8,4,128]{3,2,1,0:T(4,128)(4,1)S(1)} %bitcast.172), kind=kOutput, calls=%fused_computation.61 | convolution fusion | flops 407240704 | bytes 4587520 | tf_op jit(solution)/shard_map/dot_general | solution.py:33
  4.6 0.0 copy-done
  4.6 2.2 %fusion.48 = f32[512,256]{1,0:T(8,128)S(1)} fusion(bf16[768,5,512]{2,0,1:T(8,128)(2,1)} %param.6, f32[512,256]{1,0:T(8,128)S(1)} %copy-done, f32[768,256]{1,0:T(8,128)S(1)} %fusion.46, pred[96,8,4,128]{3,2,1,0:T(4,128)(4,1)S(1)} %bitcast.173), kind=kOutput, calls=%fused_computation.63 | convolution fusion | flops 407109632 | bytes 4325376 | tf_op jit(solution)/shard_map/ij,ik->jk/dot_general | solution.py:39
  6.8 2.1 %collective-permute-start = (f32[512,256]{1,0:T(8,128)S(1)}, f32[512,256]{1,0:T(8,128)S(1)}, u32[]{:S(2)}, u32[]{:S(2)}) collective-permute-start(f32[512,256]{1,0:T(8,128)S(1)} %fusion.48), channel_id=1, source_target_pairs={{252,0},{0,4},{4,8},{8,12},{12,16},{16,20},{20,24},{24,28},{28,32}... | collective-permute-start | bytes 1572872 | tf_op jit(solution)/shard_map/ppermute | solution.py:14
  8.9 0.1 copy.7
  9.0 19.3 %collective-permute-done = f32[512,256]{1,0:T(8,128)S(1)} collective-permute-done((f32[512,256]{1,0:T(8,128)S(1)}, f32[512,256]{1,0:T(8,128)S(1)}, u32[]{:S(2)}, u32[]{:S(2)}) %collective-permute-start) | collective-permute-done | bytes 524320 | tf_op jit(solution)/shard_map/ppermute | solution.py:14
  28.3 0.3 and.58
  28.6 2.0 %fusion.42 = f32[768,256]{1,0:T(8,128)S(1)} fusion(f32[768,256]{1,0:T(8,128)S(1)} %fusion.46, bf16[768,5,512]{2,0,1:T(8,128)(2,1)} %param.6, f32[512,256]{1,0:T(8,128)S(1)} %collective-permute-done, pred[96,8,4,128]{3,2,1,0:T(4,128)(4,1)S(1)} %bitcast.164), kind=kOutput, calls=%fused_computation.57 | convolution fusion | flops 407240704 | bytes 4587520 | tf_op jit(solution)/shard_map/dot_general | solution.py:33
  30.5 2.2 %multiply_add_fusion.6 = f32[512,256]{1,0:T(8,128)S(1)} fusion(f32[512,256]{1,0:T(8,128)S(1)} %collective-permute-done, bf16[768,5,512]{2,0,1:T(8,128)(2,1)} %param.6, f32[768,256]{1,0:T(8,128)S(1)} %fusion.42, pred[96,8,4,128]{3,2,1,0:T(4,128)(4,1)S(1)} %bitcast.165), kind=kOutput, calls=%fused_computation.124 | convolution fusion | flops 407109632 | bytes 4325376 | tf_op jit(solution)/shard_map/ij,ik->jk/dot_general | solution.py:39
  32.7 0.1 collective-permute-start.1
  32.8 0.1 copy.8
  32.9 16.3 %collective-permute-done.1 = f32[512,256]{1,0:T(8,128)S(1)} collective-permute-done((f32[512,256]{1,0:T(8,128)S(1)}, f32[512,256]{1,0:T(8,128)S(1)}, u32[]{:S(2)}, u32[]{:S(2)}) %collective-permute-start.1) | collective-permute-done | bytes 524320 | tf_op jit(solution)/shard_map/ppermute | solution.py:14
  49.3 0.3 and.61
  49.5 2.0 %multiply_add_fusion.2 = f32[768,256]{1,0:T(8,128)S(1)} fusion(f32[768,256]{1,0:T(8,128)S(1)} %fusion.42, bf16[768,5,512]{2,0,1:T(8,128)(2,1)} %param.6, f32[512,256]{1,0:T(8,128)S(1)} %collective-permute-done.1, pred[96,8,4,128]{3,2,1,0:T(4,128)(4,1)S(1)} %bitcast.166), kind=kOutput, calls=%fused_computation.80 | convolution fusion | flops 407240704 | bytes 4587520 | tf_op jit(solution)/shard_map/dot_general | solution.py:33
  51.5 2.2 %multiply_add_fusion.5 = f32[512,256]{1,0:T(8,128)S(1)} fusion(f32[512,256]{1,0:T(8,128)S(1)} %collective-permute-done.1, bf16[768,5,512]{2,0,1:T(8,128)(2,1)} %param.6, f32[768,256]{1,0:T(8,128)S(1)} %multiply_add_fusion.2, pred[96,8,4,128]{3,2,1,0:T(4,128)(4,1)S(1)} %bitcast.167), kind=kOutput, calls=%fused_computation.123 | convolution fusion | flops 407109632 | bytes 4325376 | tf_op jit(solution)/shard_map/ij,ik->jk/dot_general | solution.py:39
  53.7 0.1 collective-permute-start.2
  53.8 0.1 copy.9
  53.9 15.5 %collective-permute-done.2 = f32[512,256]{1,0:T(8,128)S(1)} collective-permute-done((f32[512,256]{1,0:T(8,128)S(1)}, f32[512,256]{1,0:T(8,128)S(1)}, u32[]{:S(2)}, u32[]{:S(2)}) %collective-permute-start.2) | collective-permute-done | bytes 524320 | tf_op jit(solution)/shard_map/ppermute | solution.py:14
  69.4 0.3 and.64
  69.7 2.0 %multiply_add_fusion.1 = f32[768,256]{1,0:T(8,128)S(1)} fusion(f32[768,256]{1,0:T(8,128)S(1)} %multiply_add_fusion.2, bf16[768,5,512]{2,0,1:T(8,128)(2,1)} %param.6, f32[512,256]{1,0:T(8,128)S(1)} %collective-permute-done.2, pred[96,8,4,128]{3,2,1,0:T(4,128)(4,1)S(1)} %bitcast.168), kind=kOutput, calls=%fused_computation.79 | convolution fusion | flops 407240704 | bytes 4587520 | tf_op jit(solution)/shard_map/dot_general | solution.py:33
  71.6 2.2 %multiply_add_fusion.4 = f32[512,256]{1,0:T(8,128)S(1)} fusion(f32[512,256]{1,0:T(8,128)S(1)} %collective-permute-done.2, bf16[768,5,512]{2,0,1:T(8,128)(2,1)} %param.6, f32[768,256]{1,0:T(8,128)S(1)} %multiply_add_fusion.1, pred[96,8,4,128]{3,2,1,0:T(4,128)(4,1)S(1)} %bitcast.169), kind=kOutput, calls=%fused_computation.122 | convolution fusion | flops 407109632 | bytes 4325376 | tf_op jit(solution)/shard_map/ij,ik->jk/dot_general | solution.py:39
  73.8 5.6 %collective-permute-start.3 = (f32[512,256]{1,0:T(8,128)S(1)}, f32[512,256]{1,0:T(8,128)S(1)}, u32[]{:S(2)}, u32[]{:S(2)}) collective-permute-start(f32[512,256]{1,0:T(8,128)S(1)} %multiply_add_fusion.4), channel_id=1, source_target_pairs={{3,0},{0,1},{1,2},{2,3},{7,4},{4,5},{5,6},{6,7},{11,8},{8,9},{9,10... | collective-permute-start | bytes 1572872 | tf_op jit(solution)/shard_map/ppermute | solution.py:14
  79.4 0.1 copy.10
  79.5 17.3 %collective-permute-done.3 = f32[512,256]{1,0:T(8,128)S(1)} collective-permute-done((f32[512,256]{1,0:T(8,128)S(1)}, f32[512,256]{1,0:T(8,128)S(1)}, u32[]{:S(2)}, u32[]{:S(2)}) %collective-permute-start.3) | collective-permute-done | bytes 524320 | tf_op jit(solution)/shard_map/ppermute | solution.py:14
  96.8 0.3 and.67
  97.1 2.0 %multiply_add_fusion = f32[768,256]{1,0:T(8,128)S(1)} fusion(f32[768,256]{1,0:T(8,128)S(1)} %multiply_add_fusion.1, bf16[768,5,512]{2,0,1:T(8,128)(2,1)} %param.6, f32[512,256]{1,0:T(8,128)S(1)} %collective-permute-done.3, pred[96,8,4,128]{3,2,1,0:T(4,128)(4,1)S(1)} %bitcast.170), kind=kOutput, calls=%fused_computation.78 | convolution fusion | flops 407240704 | bytes 4587520 | tf_op jit(solution)/shard_map/dot_general | solution.py:33
  99.0 0.0 copy-start.1
  99.0 2.5 %multiply_add_fusion.3 = f32[512,256]{1,0:T(8,128)S(1)} fusion(f32[512,256]{1,0:T(8,128)S(1)} %collective-permute-done.3, f32[768,256]{1,0:T(8,128)S(1)} %multiply_add_fusion, bf16[768,5,512]{2,0,1:T(8,128)(2,1)} %param.6, pred[96,8,4,128]{3,2,1,0:T(4,128)(4,1)S(1)} %bitcast.171), kind=kOutput, calls=%fused_computation.121 | convolution fusion | flops 407109632 | bytes 4325376 | tf_op jit(solution)/shard_map/ij,ik->jk/dot_general | solution.py:39
  101.5 0.0 copy-done.1
  101.6 0.1 collective-permute-start.4
  101.6 12.8 %collective-permute-done.4 = f32[512,256]{1,0:T(8,128)S(1)} collective-permute-done((f32[512,256]{1,0:T(8,128)S(1)}, f32[512,256]{1,0:T(8,128)S(1)}, u32[]{:S(2)}, u32[]{:S(2)}) %collective-permute-start.4) | collective-permute-done | bytes 524320 | tf_op jit(solution)/shard_map/ppermute | solution.py:14
  114.4 2.5 %collective-permute-start.5 = (f32[512,256]{1,0:T(8,128)S(1)}, f32[512,256]{1,0:T(8,128)S(1)}, u32[]{:S(2)}, u32[]{:S(2)}) collective-permute-start(f32[512,256]{1,0:T(8,128)S(1)} %collective-permute-done.4), channel_id=1, source_target_pairs={{1,0},{2,1},{3,2},{0,3},{5,4},{6,5},{7,6},{4,7},{9,8},{10,9},{11,1... | collective-permute-start | bytes 1572872 | tf_op jit(solution)/shard_map/ppermute | solution.py:14
  116.9 7.6 %collective-permute-done.5 = f32[512,256]{1,0:T(8,128)S(1)} collective-permute-done((f32[512,256]{1,0:T(8,128)S(1)}, f32[512,256]{1,0:T(8,128)S(1)}, u32[]{:S(2)}, u32[]{:S(2)}) %collective-permute-start.5) | collective-permute-done | bytes 524320 | tf_op jit(solution)/shard_map/ppermute | solution.py:14
  124.5 0.8 copy.52
Async XLA Ops:
  1.8 2.8 %copy-start = (f32[512,256]{1,0:T(8,128)S(1)}, f32[512,256]{1,0:T(8,128)}, u32[]{:S(2)}) copy-start(f32[512,256]{1,0:T(8,128)} %param.5) | copy-start | bytes 1572868
  6.8 21.5 %collective-permute-start = (f32[512,256]{1,0:T(8,128)S(1)}, f32[512,256]{1,0:T(8,128)S(1)}, u32[]{:S(2)}, u32[]{:S(2)}) collective-permute-start(f32[512,256]{1,0:T(8,128)S(1)} %fusion.48), channel_id=1, source_target_pairs={{252,0},{0,4},{4,8},{8,12},{12,16},{16,20},{20,24},{24,28},{28,32}... | collective-permute-start | bytes 1572872 | tf_op jit(solution)/shard_map/ppermute | solution.py:14
  32.7 16.5 %collective-permute-start.1 = (f32[512,256]{1,0:T(8,128)S(1)}, f32[512,256]{1,0:T(8,128)S(1)}, u32[]{:S(2)}, u32[]{:S(2)}) collective-permute-start(f32[512,256]{1,0:T(8,128)S(1)} %multiply_add_fusion.6), channel_id=1, source_target_pairs={{252,0},{0,4},{4,8},{8,12},{12,16},{16,20},{20,24},{24,28},{28,32}... | collective-permute-start | bytes 1572872 | tf_op jit(solution)/shard_map/ppermute | solution.py:14
  53.7 15.7 %collective-permute-start.2 = (f32[512,256]{1,0:T(8,128)S(1)}, f32[512,256]{1,0:T(8,128)S(1)}, u32[]{:S(2)}, u32[]{:S(2)}) collective-permute-start(f32[512,256]{1,0:T(8,128)S(1)} %multiply_add_fusion.5), channel_id=1, source_target_pairs={{252,0},{0,4},{4,8},{8,12},{12,16},{16,20},{20,24},{24,28},{28,32}... | collective-permute-start | bytes 1572872 | tf_op jit(solution)/shard_map/ppermute | solution.py:14
  73.8 22.9 %collective-permute-start.3 = (f32[512,256]{1,0:T(8,128)S(1)}, f32[512,256]{1,0:T(8,128)S(1)}, u32[]{:S(2)}, u32[]{:S(2)}) collective-permute-start(f32[512,256]{1,0:T(8,128)S(1)} %multiply_add_fusion.4), channel_id=1, source_target_pairs={{3,0},{0,1},{1,2},{2,3},{7,4},{4,5},{5,6},{6,7},{11,8},{8,9},{9,10... | collective-permute-start | bytes 1572872 | tf_op jit(solution)/shard_map/ppermute | solution.py:14
  99.0 2.5 %copy-start.1 = (f32[768,256]{1,0:T(8,128)}, f32[768,256]{1,0:T(8,128)S(1)}, u32[]{:S(2)}) copy-start(f32[768,256]{1,0:T(8,128)S(1)} %multiply_add_fusion) | copy-start | bytes 2359300
  101.6 12.8 %collective-permute-start.4 = (f32[512,256]{1,0:T(8,128)S(1)}, f32[512,256]{1,0:T(8,128)S(1)}, u32[]{:S(2)}, u32[]{:S(2)}) collective-permute-start(f32[512,256]{1,0:T(8,128)S(1)} %multiply_add_fusion.3), channel_id=1, source_target_pairs={{12,0},{16,4},{20,8},{24,12},{28,16},{32,20},{36,24},{40,28},{44,3... | collective-permute-start | bytes 1572872 | tf_op jit(solution)/shard_map/ppermute | solution.py:14
  114.4 10.1 %collective-permute-start.5 = (f32[512,256]{1,0:T(8,128)S(1)}, f32[512,256]{1,0:T(8,128)S(1)}, u32[]{:S(2)}, u32[]{:S(2)}) collective-permute-start(f32[512,256]{1,0:T(8,128)S(1)} %collective-permute-done.4), channel_id=1, source_target_pairs={{1,0},{2,1},{3,2},{0,3},{5,4},{6,5},{7,6},{4,7},{9,8},{10,9},{11,1... | collective-permute-start | bytes 1572872 | tf_op jit(solution)/shard_map/ppermute | solution.py:14
where the time goes:
time: 126 us; the launch traced here: 125 us
  waiting for transfers between devices  88.7 us (70%)
  matrix products  21.9 us (17%)
  starting transfers between devices  10.4 us (8%)
  local copies, waits for them, and re-layouts  2.71 us (2%)
    ppermute x6, waiting for transfers between devices, from_behind(): return lax.ppermute(block, axis, route)  88.7 us
    dot_general x5, matrix products, item_pass(): jnp.einsum('ij,ik->jk', misfit, user_bf, preferred_element_type=jnp.float32)  11.3 us
    dot_general x5, matrix products, user_pass(): gradient = jnp.dot(misfit, item_bf, preferred_element_type=jnp.float32)  10.6 us
    ppermute x6, starting transfers between devices, from_behind(): return lax.ppermute(block, axis, route)  10.4 us
  transfers between devices with their start and end apart: 6, of which 6 were waited for; matrix products, arithmetic and copies ran while one was open for 0% of the time, Pallas kernels for 0%

commit v1 on v0

v1 whole, which is shorter than its diff:
```python
import jax
import jax.numpy as jnp
from jax import lax
from jax.sharding import PartitionSpec as P

CLIP_LIMIT = 3.0
DECAY = 0.03
RATE = 4.0
CHUNK = 128


def shift(block, axes, sizes, offsets):
    total = 1
    for size in sizes:
        total *= size
    route = []
    for src in range(total):
        coords = []
        rem = src
        for size in reversed(sizes):
            coords.append(rem % size)
            rem //= size
        coords = coords[::-1]
        dst = 0
        for c, size, off in zip(coords, sizes, offsets):
            dst = dst * size + (c + off) % size
        route.append((src, dst))
    return lax.ppermute(block, axes, route)


def errors(user_bf, item_bf, tile_rates, observed):
    predicted = jnp.einsum("ik,jk->ij", user_bf, item_bf, preferred_element_type=jnp.float32)
    misfit = jnp.clip(tile_rates.astype(jnp.float32) - predicted, -CLIP_LIMIT, CLIP_LIMIT)
    return jnp.where(observed, misfit, 0.0).astype(jnp.bfloat16)


def expand(tile_rates, tile_flags):
    row_blocks, col_blocks = tile_flags.shape
    block_side = tile_rates.shape[0] // row_blocks
    col_side = tile_rates.shape[1] // col_blocks
    nonzero = tile_rates.reshape(row_blocks, block_side, col_blocks, col_side) != 0
    return (nonzero & (tile_flags[:, None, :, None] > 0)).reshape(tile_rates.shape)


def body(user_factors, item_factors, ratings, block_mask):
    row_count = user_factors.shape[0]
    item_count = item_factors.shape[0]
    strata = ratings.shape[1]
    user_rate = RATE / item_count
    item_rate = RATE / row_count
    n_blk = lax.axis_size("blk")
    n_hop = lax.axis_size("hop")
    n_chunks = item_count // CHUNK
    flag_cols = block_mask.shape[2] // n_chunks
    user_rows = user_factors
    chunks = [item_factors[k * CHUNK:(k + 1) * CHUNK] for k in range(n_chunks)]
    for stratum in range(strata):
        tile_rates = ratings[:, stratum, :]
        tile_flags = block_mask[:, stratum, :]
        rates_k = [tile_rates[:, k * CHUNK:(k + 1) * CHUNK] for k in range(n_chunks)]
        observed_k = [
            expand(rates_k[k], tile_flags[:, k * flag_cols:(k + 1) * flag_cols]) for k in range(n_chunks)
        ]
        items_bf = [c.astype(jnp.bfloat16) for c in chunks]
        user_bf = user_rows.astype(jnp.bfloat16)
        gradient = None
        for k in range(n_chunks):
            misfit = errors(user_bf, items_bf[k], rates_k[k], observed_k[k])
            part = jnp.dot(misfit, items_bf[k], preferred_element_type=jnp.float32)
            gradient = part if gradient is None else gradient + part
        user_rows = (1.0 - DECAY) * user_rows + user_rate * gradient
        user_bf = user_rows.astype(jnp.bfloat16)
        updated = []
        for k in range(n_chunks):
            misfit = errors(user_bf, items_bf[k], rates_k[k], observed_k[k])
            grad_k = jnp.einsum("ij,ik->jk", misfit, user_bf, preferred_element_type=jnp.float32)
            new_k = (1.0 - DECAY) * chunks[k] + item_rate * grad_k
            if stratum < strata - 2:
                new_k = shift(new_k, "blk", (n_blk,), (1,))
            elif stratum == strata - 2:
                new_k = shift(new_k, "hop", (n_hop,), (1,))
            updated.append(new_k)
        chunks = updated
    back = strata - 2
    returned = [shift(c, ("blk", "hop"), (n_blk, n_hop), (-back, -1)) for c in chunks]
    return (user_rows, jnp.concatenate(returned, axis=0))


def solution(mesh):
    in_specs = (
        P(("blk", "hop"), None),
        P(("blk", "hop"), None),
        P(("blk", "hop"), None, None),
        P(("blk", "hop"), None, None),
    )
    out_specs = (P(("blk", "hop"), None), P(("blk", "hop"), None))
    return jax.shard_map(body, mesh=mesh, in_specs=in_specs, out_specs=out_specs, check_vma=False)
```

time: 126 us -> 135 us (1.071); the launches traced: 125 us -> 133 us
  waiting for transfers between devices: 88.7 us -> 33.7 us
  matrix products: 21.9 us -> 63.3 us
  local copies, waits for them, and re-layouts: 2.71 us -> 13.7 us
  starting transfers between devices: 10.4 us -> 20 us
    ppermute x6 -> x20, waiting for transfers between devices: 88.7 us -> 33.7 us  [shift(): return lax.ppermute(block, axes, route)]
    dot_general x10 -> x40, matrix products: 21.9 us -> 63.3 us  [the longest x20 36.3 us: body(): jnp.einsum('ij,ik->jk', misfit, user_bf, preferred_element_type=jnp.float32)]
    ppermute x6 -> x20, starting transfers between devices: 10.4 us -> 20 us  [shift(): return lax.ppermute(block, axes, route)]
    and x5 -> x18, local copies, waits for them, and re-layouts: 1.36 us -> 7.03 us  [expand(): nonzero & (tile_flags[:, None, :, None] > 0)]
    squeeze x0 -> x2, local copies, waits for them, and re-layouts: none -> 4.67 us  [the longest x1 3.91 us: body(): tile_rates = ratings[:, stratum, :]]
  transfers between devices with their start and end apart: 6 -> 20, of which waited for: 6 -> 10; matrix products, arithmetic and copies ran while one was open for 0% -> 32% of each run, Pallas kernels for 0% -> 0%
where the time goes in v1:
time: 135 us; the launch traced here: 133 us
  matrix products  63.3 us (47%)
  waiting for transfers between devices  33.7 us (25%)
  starting transfers between devices  20 us (15%)
  local copies, waits for them, and re-layouts  13.7 us (10%)
    dot_general x20, matrix products, body(): jnp.einsum('ij,ik->jk', misfit, user_bf, preferred_element_type=jnp.float32)  36.3 us
    ppermute x20, waiting for transfers between devices, shift(): return lax.ppermute(block, axes, route)  33.7 us
    dot_general x20, matrix products, body(): part = jnp.dot(misfit, items_bf[k], preferred_element_type=jnp.float32)  27 us
    ppermute x20, starting transfers between devices, shift(): return lax.ppermute(block, axes, route)  20 us
    and x18, local copies, waits for them, and re-layouts, expand(): nonzero & (tile_flags[:, None, :, None] > 0)  7.03 us
    squeeze x1, local copies, waits for them, and re-layouts, body(): tile_rates = ratings[:, stratum, :]  3.91 us
  transfers between devices with their start and end apart: 20, of which 10 were waited for; matrix products, arithmetic and copies ran while one was open for 32% of the time, Pallas kernels for 0%

profile of v1, /device:TPU:1, one launch (start us, length us, event | category | flops | bytes accessed | tf_op | source)
XLA Modules:
  0.0 132.8 jit_solution(1795070613239085476)
XLA Ops:
  0.6 0.8 slice_bitcast_fusion.5
  1.4 3.9 %slice_bitcast_fusion = (bf16[768,512]{1,0:T(8,128)(2,1)}, bf16[768,512]{1,0:T(8,128)(2,1)}, bf16[768,512]{1,0:T(8,128)(2,1)}, bf16[768,512]{1,0:T(8,128)(2,1)S(1)}, bf16[768,512]{1,0:T(8,128)(2,1)}) fusion(bf16[768,5,512]{2,0,1:T(8,128)(2,1)} %param.6), kind=kLoop, calls=%fused_computation.242 | loop fusion | bytes 7864320 | tf_op jit(solution)/shard_map/squeeze | solution.py:58
  5.3 0.7 broadcast_bitcast_fusion.16
  6.6 1.4 %convolution_add_fusion.6 = f32[768,256]{1,0:T(8,128)S(1)} fusion(f32[768,256]{1,0:T(8,128)S(1)} %fusion.170, pred[768]{0:T(1024)(128)(4,1)S(1)} %get-tuple-element.52, bf16[768,512]{1,0:T(8,128)(2,1)S(1)} %get-tuple-element.5, f32[512,256]{1,0:T(8,128)} %param.5, f32[768,256]{1,0:T(8,128)S(1)} %copy-done), kind=kOutput, calls=%fused_computation.24 | convolution fusion | flops 101941248 | bytes 2688000 | tf_op jit(solution)/shard_map/dot_general | solution.py:69
  8.1 1.5 %convolution_add_fusion.5 = f32[768,256]{1,0:T(8,128)S(1)} fusion(f32[768,256]{1,0:T(8,128)S(1)} %convolution_add_fusion.6, pred[768]{0:T(1024)(128)(4,1)S(1)} %get-tuple-element.51, bf16[768,512]{1,0:T(8,128)(2,1)S(1)} %get-tuple-element.5, f32[512,256]{1,0:T(8,128)} %param.5, f32[768,256]{1,0:T(8,128)S(1)} %copy-done), kind=kOutput, calls=%fused_computation.23 | convolution fusion | flops 101941248 | bytes 2688000 | tf_op jit(solution)/shard_map/dot_general | solution.py:69
  9.6 2.3 %fusion.699 = (bf16[768,256]{1,0:T(8,128)(2,1)S(1)}, f32[768,256]{1,0:T(8,128)}) fusion(f32[768,256]{1,0:T(8,128)S(1)} %convolution_add_fusion.5, f32[512,256]{1,0:T(8,128)} %param.5, pred[768]{0:T(1024)(128)(4,1)} %get-tuple-element.50, bf16[768,512]{1,0:T(8,128)(2,1)S(1)} %get-tuple-element.5, f32[768,256]{1,0:T(8,128)S(1)} %copy-done), kind=kOutput, calls=%fused_computation.805 | convolution fusion | flops 102727680 | bytes 3867648 | tf_op jit(solution)/shard_map/dot_general | solution.py:69
  11.9 2.2 %fusion.172 = f32[128,256]{1,0:T(8,128)} fusion(bf16[768,256]{1,0:T(8,128)(2,1)S(1)} %get-tuple-element.32, pred[768]{0:T(1024)(128)(4,1)} %copy-done.26, bf16[768,512]{1,0:T(8,128)(2,1)S(1)} %get-tuple-element.5, f32[512,256]{1,0:T(8,128)} %param.5), kind=kOutput, calls=%fused_computation.219 | convolution fusion | flops 101679104 | bytes 1377280 | tf_op jit(solution)/shard_map/ij,ik->jk/dot_general | solution.py:76
  14.2 2.0 %collective-permute-start = (f32[128,256]{1,0:T(8,128)}, f32[128,256]{1,0:T(8,128)S(1)}, u32[]{:S(2)}, u32[]{:S(2)}) collective-permute-start(f32[128,256]{1,0:T(8,128)} %fusion.172), channel_id=1, source_target_pairs={{0,4},{4,8},{8,12},{12,16},{16,20},{20,24},{24,28},{28,32},{32,36}... | collective-permute-start | bytes 393224 | tf_op jit(solution)/shard_map/ppermute | solution.py:28
  16.2 2.2 %fusion.174 = f32[128,256]{1,0:T(8,128)} fusion(bf16[768,256]{1,0:T(8,128)(2,1)S(1)} %get-tuple-element.32, pred[768]{0:T(1024)(128)(4,1)S(1)} %copy-done.25, bf16[768,512]{1,0:T(8,128)(2,1)S(1)} %get-tuple-element.5, f32[512,256]{1,0:T(8,128)} %param.5), kind=kOutput, calls=%fused_computation.221 | convolution fusion | flops 101679104 | bytes 1377280 | tf_op jit(solution)/shard_map/ij,ik->jk/dot_general | solution.py:76
  18.4 1.3 collective-permute-start.1
  19.6 1.5 %fusion.178 = f32[128,256]{1,0:T(8,128)S(1)} fusion(bf16[768,256]{1,0:T(8,128)(2,1)S(1)} %get-tuple-element.32, pred[768]{0:T(1024)(128)(4,1)S(1)} %copy-done.27, bf16[768,512]{1,0:T(8,128)(2,1)S(1)} %get-tuple-element.5, f32[512,256]{1,0:T(8,128)} %param.5), kind=kOutput, calls=%fused_computation.225 | convolution fusion | flops 101679104 | bytes 1377280 | tf_op jit(solution)/shard_map/ij,ik->jk/dot_general | solution.py:76
  21.1 1.3 collective-permute-start.3
  22.4 1.5 %fusion.176 = f32[128,256]{1,0:T(8,128)S(1)} fusion(bf16[768,256]{1,0:T(8,128)(2,1)S(1)} %get-tuple-element.32, pred[768]{0:T(1024)(128)(4,1)S(1)} %copy-done.23, bf16[768,512]{1,0:T(8,128)(2,1)S(1)} %get-tuple-element.5, f32[512,256]{1,0:T(8,128)} %param.5), kind=kOutput, calls=%fused_computation.223 | convolution fusion | flops 101679104 | bytes 1377280 | tf_op jit(solution)/shard_map/ij,ik->jk/dot_general | solution.py:76
  24.0 1.3 %collective-permute-start.2 = (f32[128,256]{1,0:T(8,128)S(1)}, f32[128,256]{1,0:T(8,128)S(1)}, u32[]{:S(2)}, u32[]{:S(2)}) collective-permute-start(f32[128,256]{1,0:T(8,128)S(1)} %fusion.176), channel_id=1, source_target_pairs={{0,4},{4,8},{8,12},{12,16},{16,20},{20,24},{24,28},{28,32},{32,36}... | collective-permute-start | bytes 393224 | tf_op jit(solution)/shard_map/ppermute | solution.py:28
  25.3 0.6 broadcast_bitcast_fusion.3
  26.0 0.6 broadcast_bitcast_fusion
  26.7 0.7 broadcast_bitcast_fusion.6
  27.4 0.6 broadcast_bitcast_fusion.5
  28.0 0.6 broadcast_bitcast_fusion.4
  28.6 0.7 broadcast_bitcast_fusion.7
  29.3 0.7 broadcast_bitcast_fusion.11
  30.1 0.7 broadcast_bitcast_fusion.10
  31.0 0.6 broadcast_bitcast_fusion.15
  31.6 4.3 %collective-permute-done.2 = f32[128,256]{1,0:T(8,128)S(1)} collective-permute-done((f32[128,256]{1,0:T(8,128)S(1)}, f32[128,256]{1,0:T(8,128)S(1)}, u32[]{:S(2)}, u32[]{:S(2)}) %collective-permute-start.2) | collective-permute-done | bytes 131104 | tf_op jit(solution)/shard_map/ppermute | solution.py:28
  37.0 1.4 %fusion.167 = f32[768,256]{1,0:T(8,128)S(1)} fusion(bf16[768,256]{1,0:T(8,128)(2,1)S(1)} %get-tuple-element.32, pred[768]{0:T(1024)(128)(4,1)S(1)} %broadcast_bitcast_fusion.14, bf16[768,512]{1,0:T(8,128)(2,1)} %get-tuple-element.4, f32[128,256]{1,0:T(8,128)S(1)} %collective-permute-done.1), kind=kOutput, calls=%fused_computation.214 | convolution fusion | flops 101613568 | bytes 1639424 | tf_op jit(solution)/shard_map/dot_general | solution.py:69
  38.5 0.6 copy-done.7
  39.1 2.6 %fusion.700 = (bf16[768,256]{1,0:T(8,128)(2,1)S(1)}, f32[768,256]{1,0:T(8,128)}) fusion(f32[768,256]{1,0:T(8,128)S(1)} %fusion.163, f32[768,256]{1,0:T(8,128)S(1)} %fusion.165, f32[768,256]{1,0:T(8,128)S(1)} %fusion.167, f32[128,256]{1,0:T(8,128)S(1)} %collective-permute-done, bf16[768,256]{1,0:T(8,128)(2,1)S(1)} %get-tuple-element.32, ...), kind=kOutput, calls=%fused_computation.806 | convolution fusion | flops 102989824 | bytes 5178368 | tf_op jit(solution)/shard_map/dot_general | solution.py:69
  41.8 1.7 %multiply_add_fusion.15 = f32[128,256]{1,0:T(8,128)S(1)} fusion(f32[128,256]{1,0:T(8,128)} %copy-done.7, bf16[768,256]{1,0:T(8,128)(2,1)S(1)} %get-tuple-element.34, pred[768]{0:T(1024)(128)(4,1)} %broadcast_bitcast_fusion.15, bf16[768,512]{1,0:T(8,128)(2,1)} %get-tuple-element.4), kind=kOutput, calls=%fused_computation.523 | convolution fusion | flops 101679104 | bytes 1377280 | tf_op jit(solution)/shard_map/ij,ik->jk/dot_general | solution.py:76
  43.6 2.3 %multiply_add_fusion.14 = f32[128,256]{1,0:T(8,128)} fusion(f32[128,256]{1,0:T(8,128)} %copy-done.11, bf16[768,256]{1,0:T(8,128)(2,1)S(1)} %get-tuple-element.34, pred[768]{0:T(1024)(128)(4,1)} %copy-done.39, bf16[768,512]{1,0:T(8,128)(2,1)} %get-tuple-element.4), kind=kOutput, calls=%fused_computation.522 | convolution fusion | flops 101679104 | bytes 1377280 | tf_op jit(solution)/shard_map/ij,ik->jk/dot_general | solution.py:76
  45.9 1.6 %multiply_add_fusion.13 = f32[128,256]{1,0:T(8,128)S(1)} fusion(f32[128,256]{1,0:T(8,128)} %copy-done.12, bf16[768,256]{1,0:T(8,128)(2,1)S(1)} %get-tuple-element.34, pred[768]{0:T(1024)(128)(4,1)} %copy-done.38, bf16[768,512]{1,0:T(8,128)(2,1)} %get-tuple-element.4), kind=kOutput, calls=%fused_computation.521 | convolution fusion | flops 101679104 | bytes 1377280 | tf_op jit(solution)/shard_map/ij,ik->jk/dot_general | solution.py:76
  47.8 1.5 %multiply_add_fusion.12 = f32[128,256]{1,0:T(8,128)S(1)} fusion(f32[128,256]{1,0:T(8,128)S(1)} %copy-done.10, bf16[768,256]{1,0:T(8,128)(2,1)S(1)} %get-tuple-element.34, pred[768]{0:T(1024)(128)(4,1)S(1)} %copy-done.37, bf16[768,512]{1,0:T(8,128)(2,1)} %get-tuple-element.4), kind=kOutput, calls=%fused_computation.520 | convolution fusion | flops 101679104 | bytes 1377280 | tf_op jit(solution)/shard_map/ij,ik->jk/dot_general | solution.py:76
  49.6 8.3 %collective-permute-done.6 = f32[128,256]{1,0:T(8,128)S(1)} collective-permute-done((f32[128,256]{1,0:T(8,128)S(1)}, f32[128,256]{1,0:T(8,128)S(1)}, u32[]{:S(2)}, u32[]{:S(2)}) %collective-permute-start.6) | collective-permute-done | bytes 131104 | tf_op jit(solution)/shard_map/ppermute | solution.py:28
  58.4 2.3 %collective-permute-done.7 = f32[128,256]{1,0:T(8,128)S(1)} collective-permute-done((f32[128,256]{1,0:T(8,128)S(1)}, f32[128,256]{1,0:T(8,128)S(1)}, u32[]{:S(2)}, u32[]{:S(2)}) %collective-permute-start.7) | collective-permute-done | bytes 131104 | tf_op jit(solution)/shard_map/ppermute | solution.py:28
  61.2 1.4 %fusion.160 = f32[768,256]{1,0:T(8,128)S(1)} fusion(bf16[768,256]{1,0:T(8,128)(2,1)S(1)} %get-tuple-element.34, pred[768]{0:T(1024)(128)(4,1)S(1)} %copy-done.35, bf16[768,512]{1,0:T(8,128)(2,1)} %get-tuple-element.3, f32[128,256]{1,0:T(8,128)S(1)} %collective-permute-done.5), kind=kOutput, calls=%fused_computation.207 | convolution fusion | flops 101613568 | bytes 1639424 | tf_op jit(solution)/shard_map/dot_general | solution.py:69
  62.7 0.6 copy-done.8
  63.4 2.7 %fusion.703 = (bf16[768,256]{1,0:T(8,128)(2,1)S(1)}, f32[768,256]{1,0:T(8,128)}) fusion(f32[768,256]{1,0:T(8,128)S(1)} %fusion.156, f32[768,256]{1,0:T(8,128)S(1)} %fusion.158, f32[768,256]{1,0:T(8,128)S(1)} %fusion.160, f32[128,256]{1,0:T(8,128)S(1)} %collective-permute-done.4, bf16[768,256]{1,0:T(8,128)(2,1)S(1)} %get-tuple-element.34, ...), kind=kOutput, calls=%fused_computation.807 | convolution fusion | flops 102989824 | bytes 5178368 | tf_op jit(solution)/shard_map/dot_general | solution.py:69
  66.0 2.3 %multiply_add_fusion.11 = f32[128,256]{1,0:T(8,128)} fusion(f32[128,256]{1,0:T(8,128)} %copy-done.8, bf16[768,256]{1,0:T(8,128)(2,1)S(1)} %get-tuple-element.36, pred[768]{0:T(1024)(128)(4,1)} %broadcast_bitcast_fusion.11, bf16[768,512]{1,0:T(8,128)(2,1)} %get-tuple-element.3), kind=kOutput, calls=%fused_computation.519 | convolution fusion | flops 101679104 | bytes 1377280 | tf_op jit(solution)/shard_map/ij,ik->jk/dot_general | solution.py:76
  68.4 1.6 %multiply_add_fusion.10 = f32[128,256]{1,0:T(8,128)S(1)} fusion(f32[128,256]{1,0:T(8,128)} %copy-done.14, bf16[768,256]{1,0:T(8,128)(2,1)S(1)} %get-tuple-element.36, pred[768]{0:T(1024)(128)(4,1)} %broadcast_bitcast_fusion.10, bf16[768,512]{1,0:T(8,128)(2,1)} %get-tuple-element.3), kind=kOutput, calls=%fused_computation.518 | convolution fusion | flops 101679104 | bytes 1377280 | tf_op jit(solution)/shard_map/ij,ik->jk/dot_general | solution.py:76
  70.1 1.6 %multiply_add_fusion.9 = f32[128,256]{1,0:T(8,128)S(1)} fusion(f32[128,256]{1,0:T(8,128)} %copy-done.15, bf16[768,256]{1,0:T(8,128)(2,1)S(1)} %get-tuple-element.36, pred[768]{0:T(1024)(128)(4,1)} %copy-done.34, bf16[768,512]{1,0:T(8,128)(2,1)} %get-tuple-element.3), kind=kOutput, calls=%fused_computation.517 | convolution fusion | flops 101679104 | bytes 1377280 | tf_op jit(solution)/shard_map/ij,ik->jk/dot_general | solution.py:76
  71.8 1.5 %multiply_add_fusion.8 = f32[128,256]{1,0:T(8,128)S(1)} fusion(f32[128,256]{1,0:T(8,128)S(1)} %copy-done.17, bf16[768,256]{1,0:T(8,128)(2,1)S(1)} %get-tuple-element.36, pred[768]{0:T(1024)(128)(4,1)S(1)} %copy-done.33, bf16[768,512]{1,0:T(8,128)(2,1)} %get-tuple-element.3), kind=kOutput, calls=%fused_computation.516 | convolution fusion | flops 101679104 | bytes 1377280 | tf_op jit(solution)/shard_map/ij,ik->jk/dot_general | solution.py:76
  73.4 8.9 %collective-permute-done.10 = f32[128,256]{1,0:T(8,128)S(1)} collective-permute-done((f32[128,256]{1,0:T(8,128)S(1)}, f32[128,256]{1,0:T(8,128)S(1)}, u32[]{:S(2)}, u32[]{:S(2)}) %collective-permute-start.10) | collective-permute-done | bytes 131104 | tf_op jit(solution)/shard_map/ppermute | solution.py:28
  82.9 2.0 %collective-permute-done.11 = f32[128,256]{1,0:T(8,128)S(1)} collective-permute-done((f32[128,256]{1,0:T(8,128)S(1)}, f32[128,256]{1,0:T(8,128)S(1)}, u32[]{:S(2)}, u32[]{:S(2)}) %collective-permute-start.11) | collective-permute-done | bytes 131104 | tf_op jit(solution)/shard_map/ppermute | solution.py:28
  85.6 1.5 %fusion.153 = f32[768,256]{1,0:T(8,128)S(1)} fusion(bf16[768,256]{1,0:T(8,128)(2,1)S(1)} %get-tuple-element.36, pred[768]{0:T(1024)(128)(4,1)S(1)} %copy-done.31, bf16[768,512]{1,0:T(8,128)(2,1)S(1)} %copy-done.3, f32[128,256]{1,0:T(8,128)} %collective-permute-done.9), kind=kOutput, calls=%fused_computation.200 | convolution fusion | flops 101613568 | bytes 1639424 | tf_op jit(solution)/shard_map/dot_general | solution.py:69
  87.1 2.8 %fusion.706 = (bf16[768,256]{1,0:T(8,128)(2,1)S(1)}, f32[768,256]{1,0:T(8,128)}) fusion(f32[768,256]{1,0:T(8,128)S(1)} %fusion.149, f32[768,256]{1,0:T(8,128)S(1)} %fusion.151, f32[768,256]{1,0:T(8,128)S(1)} %fusion.153, f32[128,256]{1,0:T(8,128)} %collective-permute-done.8, bf16[768,256]{1,0:T(8,128)(2,1)S(1)} %get-tuple-element.36, ...), kind=kOutput, calls=%fused_computation.808 | convolution fusion | flops 102989824 | bytes 5178368 | tf_op jit(solution)/shard_map/dot_general | solution.py:69
  89.9 2.3 %multiply_add_fusion.7 = f32[128,256]{1,0:T(8,128)} fusion(f32[128,256]{1,0:T(8,128)} %collective-permute-done.8, bf16[768,256]{1,0:T(8,128)(2,1)S(1)} %get-tuple-element.38, pred[768]{0:T(1024)(128)(4,1)} %broadcast_bitcast_fusion.7, bf16[768,512]{1,0:T(8,128)(2,1)} %get-tuple-element.6), kind=kOutput, calls=%fused_computation.515 | convolution fusion | flops 101679104 | bytes 1377280 | tf_op jit(solution)/shard_map/ij,ik->jk/dot_general | solution.py:76
  92.2 4.6 %collective-permute-start.12 = (f32[128,256]{1,0:T(8,128)}, f32[128,256]{1,0:T(8,128)}, u32[]{:S(2)}, u32[]{:S(2)}) collective-permute-start(f32[128,256]{1,0:T(8,128)} %multiply_add_fusion.7), channel_id=1, source_target_pairs={{0,1},{1,2},{2,3},{3,0},{4,5},{5,6},{6,7},{7,4},{8,9},{9,10},{10,1... | collective-permute-start | bytes 393224 | tf_op jit(solution)/shard_map/ppermute | solution.py:28
  96.8 2.3 %multiply_add_fusion.6 = f32[128,256]{1,0:T(8,128)} fusion(f32[128,256]{1,0:T(8,128)} %collective-permute-done.9, bf16[768,256]{1,0:T(8,128)(2,1)S(1)} %get-tuple-element.38, pred[768]{0:T(1024)(128)(4,1)} %broadcast_bitcast_fusion.6, bf16[768,512]{1,0:T(8,128)(2,1)} %get-tuple-element.6), kind=kOutput, calls=%fused_computation.514 | convolution fusion | flops 101679104 | bytes 1377280 | tf_op jit(solution)/shard_map/ij,ik->jk/dot_general | solution.py:76
  99.0 1.7 %multiply_add_fusion.5 = f32[128,256]{1,0:T(8,128)S(1)} fusion(f32[128,256]{1,0:T(8,128)} %copy-done.18, bf16[768,256]{1,0:T(8,128)(2,1)S(1)} %get-tuple-element.38, pred[768]{0:T(1024)(128)(4,1)} %broadcast_bitcast_fusion.5, bf16[768,512]{1,0:T(8,128)(2,1)} %get-tuple-element.6), kind=kOutput, calls=%fused_computation.513 | convolution fusion | flops 101679104 | bytes 1377280 | tf_op jit(solution)/shard_map/ij,ik->jk/dot_general | solution.py:76
  100.7 1.1 collective-permute-start.14
  101.9 1.5 %multiply_add_fusion.4 = f32[128,256]{1,0:T(8,128)S(1)} fusion(f32[128,256]{1,0:T(8,128)S(1)} %copy-done.20, bf16[768,256]{1,0:T(8,128)(2,1)S(1)} %get-tuple-element.38, pred[768]{0:T(1024)(128)(4,1)S(1)} %copy-done.29, bf16[768,512]{1,0:T(8,128)(2,1)} %get-tuple-element.6), kind=kOutput, calls=%fused_computation.512 | convolution fusion | flops 101679104 | bytes 1377280 | tf_op jit(solution)/shard_map/ij,ik->jk/dot_general | solution.py:76
  104.5 1.0 collective-permute-done.15
  105.4 1.4 %fusion.142 = f32[768,256]{1,0:T(8,128)S(1)} fusion(bf16[768,256]{1,0:T(8,128)(2,1)S(1)} %get-tuple-element.38, pred[768]{0:T(1024)(128)(4,1)S(1)} %copy-done.28, bf16[768,512]{1,0:T(8,128)(2,1)S(1)} %copy-done.2, f32[128,256]{1,0:T(8,128)} %collective-permute-done.15), kind=kOutput, calls=%fused_computation.189 | convolution fusion | flops 101613568 | bytes 1639424 | tf_op jit(solution)/shard_map/dot_general | solution.py:69
  106.9 1.5 %fusion.146 = f32[768,256]{1,0:T(8,128)S(1)} fusion(bf16[768,256]{1,0:T(8,128)(2,1)S(1)} %get-tuple-element.38, pred[768]{0:T(1024)(128)(4,1)S(1)} %broadcast_bitcast_fusion.2, bf16[768,512]{1,0:T(8,128)(2,1)} %get-tuple-element.2, f32[128,256]{1,0:T(8,128)} %collective-permute-done.13), kind=kOutput, calls=%fused_computation.193 | convolution fusion | flops 101613568 | bytes 1639168 | tf_op jit(solution)/shard_map/dot_general | solution.py:69
  108.5 2.6 %fusion.709 = (bf16[768,256]{1,0:T(8,128)(2,1)}, f32[768,256]{1,0:T(8,128)}) fusion(f32[768,256]{1,0:T(8,128)S(1)} %fusion.142, f32[768,256]{1,0:T(8,128)S(1)} %fusion.144, f32[768,256]{1,0:T(8,128)S(1)} %fusion.146, f32[128,256]{1,0:T(8,128)} %collective-permute-done.12, bf16[768,256]{1,0:T(8,128)(2,1)S(1)} %get-tuple-element.38, ...), kind=kOutput, calls=%fused_computation.809 | convolution fusion | flops 102989824 | bytes 5178368 | tf_op jit(solution)/shard_map/dot_general | solution.py:69
  111.1 1.9 %multiply_add_fusion = f32[128,256]{1,0:T(8,128)S(1)} fusion(f32[128,256]{1,0:T(8,128)} %collective-permute-done.15, bf16[768,256]{1,0:T(8,128)(2,1)} %get-tuple-element.40, pred[768]{0:T(1024)(128)(4,1)S(1)} %copy-done.28, bf16[768,512]{1,0:T(8,128)(2,1)} %get-tuple-element.2), kind=kOutput, calls=%fused_computation.508 | convolution fusion | flops 101679104 | bytes 1377024 | tf_op jit(solution)/shard_map/ij,ik->jk/dot_general | solution.py:76
  112.9 4.4 %collective-permute-start.19 = (f32[128,256]{1,0:T(8,128)S(1)}, f32[128,256]{1,0:T(8,128)S(1)}, u32[]{:S(2)}, u32[]{:S(2)}) collective-permute-start(f32[128,256]{1,0:T(8,128)S(1)} %multiply_add_fusion), channel_id=1, source_target_pairs={{0,247},{1,244},{2,245},{3,246},{4,251},{5,248},{6,249},{7,250},{8... | collective-permute-start | bytes 393224 | tf_op jit(solution)/shard_map/ppermute | solution.py:28
  117.3 1.8 %multiply_add_fusion.3 = f32[128,256]{1,0:T(8,128)S(1)} fusion(f32[128,256]{1,0:T(8,128)} %collective-permute-done.12, bf16[768,256]{1,0:T(8,128)(2,1)} %get-tuple-element.40, pred[768]{0:T(1024)(128)(4,1)S(1)} %copy-done.40, bf16[768,512]{1,0:T(8,128)(2,1)} %get-tuple-element.2), kind=kOutput, calls=%fused_computation.511 | convolution fusion | flops 101679104 | bytes 1377024 | tf_op jit(solution)/shard_map/ij,ik->jk/dot_general | solution.py:76
  119.3 1.9 %multiply_add_fusion.1 = f32[128,256]{1,0:T(8,128)S(1)} fusion(f32[128,256]{1,0:T(8,128)} %copy-done.13, bf16[768,256]{1,0:T(8,128)(2,1)} %get-tuple-element.40, pred[768]{0:T(1024)(128)(4,1)S(1)} %broadcast_bitcast_fusion.1, bf16[768,512]{1,0:T(8,128)(2,1)} %get-tuple-element.2), kind=kOutput, calls=%fused_computation.509 | convolution fusion | flops 101679104 | bytes 1377024 | tf_op jit(solution)/shard_map/ij,ik->jk/dot_general | solution.py:76
  121.1 2.6 %collective-permute-start.18 = (f32[128,256]{1,0:T(8,128)S(1)}, f32[128,256]{1,0:T(8,128)S(1)}, u32[]{:S(2)}, u32[]{:S(2)}) collective-permute-start(f32[128,256]{1,0:T(8,128)S(1)} %multiply_add_fusion.1), channel_id=1, source_target_pairs={{0,247},{1,244},{2,245},{3,246},{4,251},{5,248},{6,249},{7,250},{8... | collective-permute-start | bytes 393224 | tf_op jit(solution)/shard_map/ppermute | solution.py:28
  123.8 1.6 %multiply_add_fusion.2 = f32[128,256]{1,0:T(8,128)S(1)} fusion(f32[128,256]{1,0:T(8,128)} %collective-permute-done.13, bf16[768,256]{1,0:T(8,128)(2,1)S(1)} %copy-done.21, pred[768]{0:T(1024)(128)(4,1)S(1)} %broadcast_bitcast_fusion.2, bf16[768,512]{1,0:T(8,128)(2,1)} %get-tuple-element.2), kind=kOutput, calls=%fused_computation.510 | convolution fusion | flops 101679104 | bytes 1377280 | tf_op jit(solution)/shard_map/ij,ik->jk/dot_general | solution.py:76
  125.5 1.1 collective-permute-done.16
  126.6 2.4 %collective-permute-done.18 = f32[128,256]{1,0:T(8,128)S(1)} collective-permute-done((f32[128,256]{1,0:T(8,128)S(1)}, f32[128,256]{1,0:T(8,128)S(1)}, u32[]{:S(2)}, u32[]{:S(2)}) %collective-permute-start.18) | collective-permute-done | bytes 131104 | tf_op jit(solution)/shard_map/ppermute | solution.py:28
  128.9 3.0 %collective-permute-done.17 = f32[128,256]{1,0:T(8,128)S(1)} collective-permute-done((f32[128,256]{1,0:T(8,128)S(1)}, f32[128,256]{1,0:T(8,128)S(1)}, u32[]{:S(2)}, u32[]{:S(2)}) %collective-permute-start.17) | collective-permute-done | bytes 131104 | tf_op jit(solution)/shard_map/ppermute | solution.py:28
  132.0 0.8 pad_maximum_fusion
  (122 shorter events, 6.8 us)
Async XLA Ops:
  1.4 4.7 %copy-start = (f32[768,256]{1,0:T(8,128)S(1)}, f32[768,256]{1,0:T(8,128)}, u32[]{:S(2)}) copy-start(f32[768,256]{1,0:T(8,128)} %param.4) | copy-start | bytes 2359300
  1.4 4.7 %copy-start.6 = (f32[512,256]{1,0:T(8,128)S(1)}, f32[512,256]{1,0:T(8,128)}, u32[]{:S(2)}) copy-start(f32[512,256]{1,0:T(8,128)} %param.5) | copy-start | bytes 1572868
  6.0 3.5 %copy-start.22 = (pred[768]{0:T(1024)(128)(4,1)}, pred[768]{0:T(1024)(128)(4,1)S(1)}, u32[]{:S(2)}) copy-start(pred[768]{0:T(1024)(128)(4,1)S(1)} %get-tuple-element.51) | copy-start | bytes 2308
  6.1 0.5 copy-start.26
  6.1 3.5 %copy-start.24 = (pred[768]{0:T(1024)(128)(4,1)}, pred[768]{0:T(1024)(128)(4,1)S(1)}, u32[]{:S(2)}) copy-start(pred[768]{0:T(1024)(128)(4,1)S(1)} %get-tuple-element.52) | copy-start | bytes 2308
  9.6 10.1 %copy-start.27 = (pred[768]{0:T(1024)(128)(4,1)S(1)}, pred[768]{0:T(1024)(128)(4,1)}, u32[]{:S(2)}) copy-start(pred[768]{0:T(1024)(128)(4,1)} %get-tuple-element.50) | copy-start | bytes 2308
  9.6 6.6 %copy-start.25 = (pred[768]{0:T(1024)(128)(4,1)S(1)}, pred[768]{0:T(1024)(128)(4,1)}, u32[]{:S(2)}) copy-start(pred[768]{0:T(1024)(128)(4,1)} %copy-done.24) | copy-start | bytes 2308
  11.9 10.5 %copy-start.23 = (pred[768]{0:T(1024)(128)(4,1)S(1)}, pred[768]{0:T(1024)(128)(4,1)}, u32[]{:S(2)}) copy-start(pred[768]{0:T(1024)(128)(4,1)} %copy-done.22) | copy-start | bytes 2308
  11.9 24.1 %copy-start.5 = (bf16[768,512]{1,0:T(8,128)(2,1)S(1)}, bf16[768,512]{1,0:T(8,128)(2,1)}, u32[]{:S(2)}) copy-start(bf16[768,512]{1,0:T(8,128)(2,1)} %get-tuple-element.4) | copy-start | bytes 2359300
  14.2 24.3 %collective-permute-start = (f32[128,256]{1,0:T(8,128)}, f32[128,256]{1,0:T(8,128)S(1)}, u32[]{:S(2)}, u32[]{:S(2)}) collective-permute-start(f32[128,256]{1,0:T(8,128)} %fusion.172), channel_id=1, source_target_pairs={{0,4},{4,8},{8,12},{12,16},{16,20},{20,24},{24,28},{28,32},{32,36}... | collective-permute-start | bytes 393224 | tf_op jit(solution)/shard_map/ppermute | solution.py:28
  18.4 18.6 %collective-permute-start.1 = (f32[128,256]{1,0:T(8,128)}, f32[128,256]{1,0:T(8,128)S(1)}, u32[]{:S(2)}, u32[]{:S(2)}) collective-permute-start(f32[128,256]{1,0:T(8,128)} %fusion.174), channel_id=1, source_target_pairs={{0,4},{4,8},{8,12},{12,16},{16,20},{20,24},{24,28},{28,32},{32,36}... | collective-permute-start | bytes 393224 | tf_op jit(solution)/shard_map/ppermute | solution.py:28
  21.1 15.3 %collective-permute-start.3 = (f32[128,256]{1,0:T(8,128)S(1)}, f32[128,256]{1,0:T(8,128)S(1)}, u32[]{:S(2)}, u32[]{:S(2)}) collective-permute-start(f32[128,256]{1,0:T(8,128)S(1)} %fusion.178), channel_id=1, source_target_pairs={{0,4},{4,8},{8,12},{12,16},{16,20},{20,24},{24,28},{28,32},{32,36}... | collective-permute-start | bytes 393224 | tf_op jit(solution)/shard_map/ppermute | solution.py:28
  24.0 12.0 %collective-permute-start.2 = (f32[128,256]{1,0:T(8,128)S(1)}, f32[128,256]{1,0:T(8,128)S(1)}, u32[]{:S(2)}, u32[]{:S(2)}) collective-permute-start(f32[128,256]{1,0:T(8,128)S(1)} %fusion.176), channel_id=1, source_target_pairs={{0,4},{4,8},{8,12},{12,16},{16,20},{20,24},{24,28},{28,32},{32,36}... | collective-permute-start | bytes 393224 | tf_op jit(solution)/shard_map/ppermute | solution.py:28
  30.1 30.7 %copy-start.32 = (pred[768]{0:T(1024)(128)(4,1)}, pred[768]{0:T(1024)(128)(4,1)S(1)}, u32[]{:S(2)}) copy-start(pred[768]{0:T(1024)(128)(4,1)S(1)} %broadcast_bitcast_fusion.8) | copy-start | bytes 2308
  30.1 27.8 %copy-start.34 = (pred[768]{0:T(1024)(128)(4,1)}, pred[768]{0:T(1024)(128)(4,1)S(1)}, u32[]{:S(2)}) copy-start(pred[768]{0:T(1024)(128)(4,1)S(1)} %broadcast_bitcast_fusion.9) | copy-start | bytes 2308
  30.9 7.6 %copy-start.39 = (pred[768]{0:T(1024)(128)(4,1)}, pred[768]{0:T(1024)(128)(4,1)S(1)}, u32[]{:S(2)}) copy-start(pred[768]{0:T(1024)(128)(4,1)S(1)} %broadcast_bitcast_fusion.14) | copy-start | bytes 2308
  30.9 7.5 %copy-start.38 = (pred[768]{0:T(1024)(128)(4,1)}, pred[768]{0:T(1024)(128)(4,1)S(1)}, u32[]{:S(2)}) copy-start(pred[768]{0:T(1024)(128)(4,1)S(1)} %broadcast_bitcast_fusion.13) | copy-start | bytes 2308
  31.0 7.4 %copy-start.36 = (pred[768]{0:T(1024)(128)(4,1)}, pred[768]{0:T(1024)(128)(4,1)S(1)}, u32[]{:S(2)}) copy-start(pred[768]{0:T(1024)(128)(4,1)S(1)} %broadcast_bitcast_fusion.12) | copy-start | bytes 2308
  36.0 2.5 %copy-start.12 = (f32[128,256]{1,0:T(8,128)}, f32[128,256]{1,0:T(8,128)S(1)}, u32[]{:S(2)}) copy-start(f32[128,256]{1,0:T(8,128)S(1)} %collective-permute-done.2) | copy-start | bytes 393220
  36.5 2.0 %copy-start.9 = (f32[128,256]{1,0:T(8,128)}, f32[128,256]{1,0:T(8,128)S(1)}, u32[]{:S(2)}) copy-start(f32[128,256]{1,0:T(8,128)S(1)} %collective-permute-done.3) | copy-start | bytes 393220
  37.0 1.5 %copy-start.11 = (f32[128,256]{1,0:T(8,128)}, f32[128,256]{1,0:T(8,128)S(1)}, u32[]{:S(2)}) copy-start(f32[128,256]{1,0:T(8,128)S(1)} %collective-permute-done.1) | copy-start | bytes 393220
  38.5 0.7 copy-start.7
  41.8 6.0 %copy-start.10 = (f32[128,256]{1,0:T(8,128)S(1)}, f32[128,256]{1,0:T(8,128)}, u32[]{:S(2)}) copy-start(f32[128,256]{1,0:T(8,128)} %copy-done.9) | copy-start | bytes 393220
  41.8 6.0 %copy-start.37 = (pred[768]{0:T(1024)(128)(4,1)S(1)}, pred[768]{0:T(1024)(128)(4,1)}, u32[]{:S(2)}) copy-start(pred[768]{0:T(1024)(128)(4,1)} %copy-done.36) | copy-start | bytes 2308
  41.8 16.1 %copy-start.4 = (bf16[768,512]{1,0:T(8,128)(2,1)S(1)}, bf16[768,512]{1,0:T(8,128)(2,1)}, u32[]{:S(2)}) copy-start(bf16[768,512]{1,0:T(8,128)(2,1)} %get-tuple-element.3) | copy-start | bytes 2359300
  43.5 17.7 %copy-start.35 = (pred[768]{0:T(1024)(128)(4,1)S(1)}, pred[768]{0:T(1024)(128)(4,1)}, u32[]{:S(2)}) copy-start(pred[768]{0:T(1024)(128)(4,1)} %broadcast_bitcast_fusion.10) | copy-start | bytes 2308
  43.5 19.2 %collective-permute-start.4 = (f32[128,256]{1,0:T(8,128)S(1)}, f32[128,256]{1,0:T(8,128)S(1)}, u32[]{:S(2)}, u32[]{:S(2)}) collective-permute-start(f32[128,256]{1,0:T(8,128)S(1)} %multiply_add_fusion.15), channel_id=1, source_target_pairs={{0,4},{4,8},{8,12},{12,16},{16,20},{20,24},{24,28},{28,32},{32,36}... | collective-permute-start | bytes 393224 | tf_op jit(solution)/shard_map/ppermute | solution.py:28
  45.8 15.4 %collective-permute-start.5 = (f32[128,256]{1,0:T(8,128)}, f32[128,256]{1,0:T(8,128)S(1)}, u32[]{:S(2)}, u32[]{:S(2)}) collective-permute-start(f32[128,256]{1,0:T(8,128)} %multiply_add_fusion.14), channel_id=1, source_target_pairs={{0,4},{4,8},{8,12},{12,16},{16,20},{20,24},{24,28},{28,32},{32,36}... | collective-permute-start | bytes 393224 | tf_op jit(solution)/shard_map/ppermute | solution.py:28
  47.5 10.5 %collective-permute-start.6 = (f32[128,256]{1,0:T(8,128)S(1)}, f32[128,256]{1,0:T(8,128)S(1)}, u32[]{:S(2)}, u32[]{:S(2)}) collective-permute-start(f32[128,256]{1,0:T(8,128)S(1)} %multiply_add_fusion.13), channel_id=1, source_target_pairs={{0,4},{4,8},{8,12},{12,16},{16,20},{20,24},{24,28},{28,32},{32,36}... | collective-permute-start | bytes 393224 | tf_op jit(solution)/shard_map/ppermute | solution.py:28
  49.2 11.5 %collective-permute-start.7 = (f32[128,256]{1,0:T(8,128)S(1)}, f32[128,256]{1,0:T(8,128)S(1)}, u32[]{:S(2)}, u32[]{:S(2)}) collective-permute-start(f32[128,256]{1,0:T(8,128)S(1)} %multiply_add_fusion.12), channel_id=1, source_target_pairs={{0,4},{4,8},{8,12},{12,16},{16,20},{20,24},{24,28},{28,32},{32,36}... | collective-permute-start | bytes 393224 | tf_op jit(solution)/shard_map/ppermute | solution.py:28
  57.9 4.8 %copy-start.15 = (f32[128,256]{1,0:T(8,128)}, f32[128,256]{1,0:T(8,128)S(1)}, u32[]{:S(2)}) copy-start(f32[128,256]{1,0:T(8,128)S(1)} %collective-permute-done.6) | copy-start | bytes 393220
  60.7 2.0 %copy-start.16 = (f32[128,256]{1,0:T(8,128)}, f32[128,256]{1,0:T(8,128)S(1)}, u32[]{:S(2)}) copy-start(f32[128,256]{1,0:T(8,128)S(1)} %collective-permute-done.7) | copy-start | bytes 393220
  61.2 1.5 %copy-start.14 = (f32[128,256]{1,0:T(8,128)}, f32[128,256]{1,0:T(8,128)S(1)}, u32[]{:S(2)}) copy-start(f32[128,256]{1,0:T(8,128)S(1)} %collective-permute-done.5) | copy-start | bytes 393220
  62.7 0.6 copy-start.8
  66.0 5.8 %copy-start.17 = (f32[128,256]{1,0:T(8,128)S(1)}, f32[128,256]{1,0:T(8,128)}, u32[]{:S(2)}) copy-start(f32[128,256]{1,0:T(8,128)} %copy-done.16) | copy-start | bytes 393220
  66.0 5.8 %copy-start.33 = (pred[768]{0:T(1024)(128)(4,1)S(1)}, pred[768]{0:T(1024)(128)(4,1)}, u32[]{:S(2)}) copy-start(pred[768]{0:T(1024)(128)(4,1)} %copy-done.32) | copy-start | bytes 2308
  66.0 16.2 %copy-start.3 = (bf16[768,512]{1,0:T(8,128)(2,1)S(1)}, bf16[768,512]{1,0:T(8,128)(2,1)}, u32[]{:S(2)}) copy-start(bf16[768,512]{1,0:T(8,128)(2,1)} %get-tuple-element.6) | copy-start | bytes 2359300
  66.0 16.2 %copy-start.30 = (pred[768]{0:T(1024)(128)(4,1)S(1)}, pred[768]{0:T(1024)(128)(4,1)}, u32[]{:S(2)}) copy-start(pred[768]{0:T(1024)(128)(4,1)} %broadcast_bitcast_fusion.5) | copy-start | bytes 2308
  66.0 18.9 %copy-start.29 = (pred[768]{0:T(1024)(128)(4,1)S(1)}, pred[768]{0:T(1024)(128)(4,1)}, u32[]{:S(2)}) copy-start(pred[768]{0:T(1024)(128)(4,1)} %broadcast_bitcast_fusion.4) | copy-start | bytes 2308
  68.4 17.3 %copy-start.31 = (pred[768]{0:T(1024)(128)(4,1)S(1)}, pred[768]{0:T(1024)(128)(4,1)}, u32[]{:S(2)}) copy-start(pred[768]{0:T(1024)(128)(4,1)} %broadcast_bitcast_fusion.6) | copy-start | bytes 2308
  68.4 18.7 %collective-permute-start.8 = (f32[128,256]{1,0:T(8,128)}, f32[128,256]{1,0:T(8,128)}, u32[]{:S(2)}, u32[]{:S(2)}) collective-permute-start(f32[128,256]{1,0:T(8,128)} %multiply_add_fusion.11), channel_id=1, source_target_pairs={{0,4},{4,8},{8,12},{12,16},{16,20},{20,24},{24,28},{28,32},{32,36}... | collective-permute-start | bytes 393224 | tf_op jit(solution)/shard_map/ppermute | solution.py:28
  70.0 15.6 %collective-permute-start.9 = (f32[128,256]{1,0:T(8,128)S(1)}, f32[128,256]{1,0:T(8,128)}, u32[]{:S(2)}, u32[]{:S(2)}) collective-permute-start(f32[128,256]{1,0:T(8,128)S(1)} %multiply_add_fusion.10), channel_id=1, source_target_pairs={{0,4},{4,8},{8,12},{12,16},{16,20},{20,24},{24,28},{28,32},{32,36}... | collective-permute-start | bytes 393224 | tf_op jit(solution)/shard_map/ppermute | solution.py:28
  71.7 10.6 %collective-permute-start.10 = (f32[128,256]{1,0:T(8,128)S(1)}, f32[128,256]{1,0:T(8,128)S(1)}, u32[]{:S(2)}, u32[]{:S(2)}) collective-permute-start(f32[128,256]{1,0:T(8,128)S(1)} %multiply_add_fusion.9), channel_id=1, source_target_pairs={{0,4},{4,8},{8,12},{12,16},{16,20},{20,24},{24,28},{28,32},{32,36}... | collective-permute-start | bytes 393224 | tf_op jit(solution)/shard_map/ppermute | solution.py:28
  73.3 11.7 %collective-permute-start.11 = (f32[128,256]{1,0:T(8,128)S(1)}, f32[128,256]{1,0:T(8,128)S(1)}, u32[]{:S(2)}, u32[]{:S(2)}) collective-permute-start(f32[128,256]{1,0:T(8,128)S(1)} %multiply_add_fusion.8), channel_id=1, source_target_pairs={{0,4},{4,8},{8,12},{12,16},{16,20},{20,24},{24,28},{28,32},{32,36}... | collective-permute-start | bytes 393224 | tf_op jit(solution)/shard_map/ppermute | solution.py:28
  82.3 0.7 copy-start.18
  85.0 0.7 copy-start.19
  89.8 12.0 %copy-start.20 = (f32[128,256]{1,0:T(8,128)S(1)}, f32[128,256]{1,0:T(8,128)}, u32[]{:S(2)}) copy-start(f32[128,256]{1,0:T(8,128)} %copy-done.19) | copy-start | bytes 393220
  89.8 14.0 %copy-start.2 = (bf16[768,512]{1,0:T(8,128)(2,1)S(1)}, bf16[768,512]{1,0:T(8,128)(2,1)}, u32[]{:S(2)}) copy-start(bf16[768,512]{1,0:T(8,128)(2,1)} %get-tuple-element.2) | copy-start | bytes 2359300
  89.9 15.6 %copy-start.28 = (pred[768]{0:T(1024)(128)(4,1)S(1)}, pred[768]{0:T(1024)(128)(4,1)}, u32[]{:S(2)}) copy-start(pred[768]{0:T(1024)(128)(4,1)} %broadcast_bitcast_fusion) | copy-start | bytes 2308
  92.2 16.3 %collective-permute-start.12 = (f32[128,256]{1,0:T(8,128)}, f32[128,256]{1,0:T(8,128)}, u32[]{:S(2)}, u32[]{:S(2)}) collective-permute-start(f32[128,256]{1,0:T(8,128)} %multiply_add_fusion.7), channel_id=1, source_target_pairs={{0,1},{1,2},{2,3},{3,0},{4,5},{5,6},{6,7},{7,4},{8,9},{9,10},{10,1... | collective-permute-start | bytes 393224 | tf_op jit(solution)/shard_map/ppermute | solution.py:28
  99.0 9.4 %copy-start.1 = (f32[768,256]{1,0:T(8,128)S(1)}, f32[768,256]{1,0:T(8,128)}, u32[]{:S(2)}) copy-start(f32[768,256]{1,0:T(8,128)} %get-tuple-element.39) | copy-start | bytes 2359300
  99.0 7.9 %collective-permute-start.13 = (f32[128,256]{1,0:T(8,128)}, f32[128,256]{1,0:T(8,128)}, u32[]{:S(2)}, u32[]{:S(2)}) collective-permute-start(f32[128,256]{1,0:T(8,128)} %multiply_add_fusion.6), channel_id=1, source_target_pairs={{0,1},{1,2},{2,3},{3,0},{4,5},{5,6},{6,7},{7,4},{8,9},{9,10},{10,1... | collective-permute-start | bytes 393224 | tf_op jit(solution)/shard_map/ppermute | solution.py:28
  100.7 3.1 %collective-permute-start.14 = (f32[128,256]{1,0:T(8,128)S(1)}, f32[128,256]{1,0:T(8,128)S(1)}, u32[]{:S(2)}, u32[]{:S(2)}) collective-permute-start(f32[128,256]{1,0:T(8,128)S(1)} %multiply_add_fusion.5), channel_id=1, source_target_pairs={{0,1},{1,2},{2,3},{3,0},{4,5},{5,6},{6,7},{7,4},{8,9},{9,10},{10,1... | collective-permute-start | bytes 393224 | tf_op jit(solution)/shard_map/ppermute | solution.py:28
  103.3 2.1 %collective-permute-start.15 = (f32[128,256]{1,0:T(8,128)S(1)}, f32[128,256]{1,0:T(8,128)}, u32[]{:S(2)}, u32[]{:S(2)}) collective-permute-start(f32[128,256]{1,0:T(8,128)S(1)} %multiply_add_fusion.4), channel_id=1, source_target_pairs={{0,1},{1,2},{2,3},{3,0},{4,5},{5,6},{6,7},{7,4},{8,9},{9,10},{10,1... | collective-permute-start | bytes 393224 | tf_op jit(solution)/shard_map/ppermute | solution.py:28
  103.8 0.7 copy-start.13
  106.9 10.4 %copy-start.40 = (pred[768]{0:T(1024)(128)(4,1)S(1)}, pred[768]{0:T(1024)(128)(4,1)}, u32[]{:S(2)}) copy-start(pred[768]{0:T(1024)(128)(4,1)} %broadcast_bitcast_fusion.3) | copy-start | bytes 2308
  111.1 12.7 %copy-start.21 = (bf16[768,256]{1,0:T(8,128)(2,1)S(1)}, bf16[768,256]{1,0:T(8,128)(2,1)}, u32[]{:S(2)}) copy-start(bf16[768,256]{1,0:T(8,128)(2,1)} %get-tuple-element.40) | copy-start | bytes 1179652
  112.9 12.6 %collective-permute-start.19 = (f32[128,256]{1,0:T(8,128)S(1)}, f32[128,256]{1,0:T(8,128)S(1)}, u32[]{:S(2)}, u32[]{:S(2)}) collective-permute-start(f32[128,256]{1,0:T(8,128)S(1)} %multiply_add_fusion), channel_id=1, source_target_pairs={{0,247},{1,244},{2,245},{3,246},{4,251},{5,248},{6,249},{7,250},{8... | collective-permute-start | bytes 393224 | tf_op jit(solution)/shard_map/ppermute | solution.py:28
  119.2 7.4 %collective-permute-start.16 = (f32[128,256]{1,0:T(8,128)S(1)}, f32[128,256]{1,0:T(8,128)S(1)}, u32[]{:S(2)}, u32[]{:S(2)}) collective-permute-start(f32[128,256]{1,0:T(8,128)S(1)} %multiply_add_fusion.3), channel_id=1, source_target_pairs={{0,247},{1,244},{2,245},{3,246},{4,251},{5,248},{6,249},{7,250},{8... | collective-permute-start | bytes 393224 | tf_op jit(solution)/shard_map/ppermute | solution.py:28
  121.1 7.8 %collective-permute-start.18 = (f32[128,256]{1,0:T(8,128)S(1)}, f32[128,256]{1,0:T(8,128)S(1)}, u32[]{:S(2)}, u32[]{:S(2)}) collective-permute-start(f32[128,256]{1,0:T(8,128)S(1)} %multiply_add_fusion.1), channel_id=1, source_target_pairs={{0,247},{1,244},{2,245},{3,246},{4,251},{5,248},{6,249},{7,250},{8... | collective-permute-start | bytes 393224 | tf_op jit(solution)/shard_map/ppermute | solution.py:28
  125.4 6.6 %collective-permute-start.17 = (f32[128,256]{1,0:T(8,128)S(1)}, f32[128,256]{1,0:T(8,128)S(1)}, u32[]{:S(2)}, u32[]{:S(2)}) collective-permute-start(f32[128,256]{1,0:T(8,128)S(1)} %multiply_add_fusion.2), channel_id=1, source_target_pairs={{0,247},{1,244},{2,245},{3,246},{4,251},{5,248},{6,249},{7,250},{8... | collective-permute-start | bytes 393224 | tf_op jit(solution)/shard_map/ppermute | solution.py:28

commit v2 on v1

v2 whole, which is shorter than its diff:
```python
import functools

import jax
import jax.numpy as jnp
from jax import lax
from jax.experimental import pallas as pl
from jax.experimental.pallas import tpu as pltpu
from jax.sharding import PartitionSpec as P

CLIP_LIMIT = 3.0
DECAY = 0.03
RATE = 4.0


def shift(block, axes, sizes, offsets):
    total = 1
    for size in sizes:
        total *= size
    route = []
    for src in range(total):
        coords = []
        rem = src
        for size in reversed(sizes):
            coords.append(rem % size)
            rem //= size
        coords = coords[::-1]
        dst = 0
        for c, size, off in zip(coords, sizes, offsets):
            dst = dst * size + (c + off) % size
        route.append((src, dst))
    return lax.ppermute(block, axes, route)


def tile_kernel(user_rate, item_rate, flags_ref, users_ref, items_ref, rates_ref, users_out, items_out, obs_ref):
    row_blocks, col_blocks = flags_ref.shape
    rows, cols = rates_ref.shape
    bs_r = rows // row_blocks
    bs_c = cols // col_blocks
    for r in range(row_blocks):
        for c in range(col_blocks):
            block = rates_ref[r * bs_r:(r + 1) * bs_r, c * bs_c:(c + 1) * bs_c]
            keep = jnp.logical_and(block != 0, flags_ref[r, c] > 0)
            obs_ref[r * bs_r:(r + 1) * bs_r, c * bs_c:(c + 1) * bs_c] = keep.astype(jnp.float32)
    observed = obs_ref[...] > 0
    rates = rates_ref[...].astype(jnp.float32)
    user_rows = users_ref[...]
    item_rows = items_ref[...]
    item_bf = item_rows.astype(jnp.bfloat16)
    user_bf = user_rows.astype(jnp.bfloat16)
    nt = (((1,), (1,)), ((), ()))
    predicted = lax.dot_general(user_bf, item_bf, nt, preferred_element_type=jnp.float32)
    misfit = jnp.where(observed, jnp.clip(rates - predicted, -CLIP_LIMIT, CLIP_LIMIT), 0.0).astype(jnp.bfloat16)
    gradient = jnp.dot(misfit, item_bf, preferred_element_type=jnp.float32)
    user_rows = (1.0 - DECAY) * user_rows + user_rate * gradient
    users_out[...] = user_rows
    user_bf = user_rows.astype(jnp.bfloat16)
    predicted = lax.dot_general(user_bf, item_bf, nt, preferred_element_type=jnp.float32)
    misfit = jnp.where(observed, jnp.clip(rates - predicted, -CLIP_LIMIT, CLIP_LIMIT), 0.0).astype(jnp.bfloat16)
    tn = (((0,), (0,)), ((), ()))
    gradient = lax.dot_general(misfit, user_bf, tn, preferred_element_type=jnp.float32)
    items_out[...] = (1.0 - DECAY) * item_rows + item_rate * gradient


def update_tile(user_rows, item_rows, tile_rates, tile_flags, user_rate, item_rate):
    rows, k = user_rows.shape
    cols = item_rows.shape[0]
    flops = 8 * rows * cols * k
    nbytes = 2 * (rows * k * 4 + cols * k * 4) + rows * cols * 2
    vmem = pl.BlockSpec(memory_space=pltpu.VMEM)
    return pl.pallas_call(
        functools.partial(tile_kernel, user_rate, item_rate),
        out_shape=(
            jax.ShapeDtypeStruct(user_rows.shape, jnp.float32),
            jax.ShapeDtypeStruct(item_rows.shape, jnp.float32),
        ),
        in_specs=[pl.BlockSpec(memory_space=pltpu.SMEM), vmem, vmem, vmem],
        out_specs=(vmem, vmem),
        scratch_shapes=[pltpu.VMEM((rows, cols), jnp.float32)],
        cost_estimate=pl.CostEstimate(flops=flops, bytes_accessed=nbytes, transcendentals=0),
    )(tile_flags, user_rows, item_rows, tile_rates)


def body(user_factors, item_factors, ratings, block_mask):
    row_count = user_factors.shape[0]
    item_count = item_factors.shape[0]
    strata = ratings.shape[1]
    user_rate = RATE / item_count
    item_rate = RATE / row_count
    n_blk = lax.axis_size("blk")
    n_hop = lax.axis_size("hop")
    user_rows = user_factors
    item_rows = item_factors
    for stratum in range(strata):
        tile_rates = ratings[:, stratum, :]
        tile_flags = block_mask[:, stratum, :]
        user_rows, item_rows = update_tile(user_rows, item_rows, tile_rates, tile_flags, user_rate, item_rate)
        if stratum < strata - 2:
            item_rows = shift(item_rows, "blk", (n_blk,), (1,))
        elif stratum == strata - 2:
            item_rows = shift(item_rows, "hop", (n_hop,), (1,))
    back = strata - 2
    returned = shift(item_rows, ("blk", "hop"), (n_blk, n_hop), (-back, -1))
    return (user_rows, returned)


def solution(mesh):
    in_specs = (
        P(("blk", "hop"), None),
        P(("blk", "hop"), None),
        P(("blk", "hop"), None, None),
        P(("blk", "hop"), None, None),
    )
    out_specs = (P(("blk", "hop"), None), P(("blk", "hop"), None))
    return jax.shard_map(body, mesh=mesh, in_specs=in_specs, out_specs=out_specs, check_vma=False)
```

time: 135 us -> 111 us (0.82); the launches traced: 133 us -> 111 us
  matrix products: 63.3 us -> 0 us
  waiting for transfers between devices: 33.7 us -> 72.4 us
  Pallas kernels: 0 us -> 19.2 us
  starting transfers between devices: 20 us -> 7.33 us
  local copies, waits for them, and re-layouts: 13.7 us -> 11.4 us
    dot_general x40 -> x0, matrix products: 63.3 us -> none  [the longest x20 36.3 us: body(): jnp.einsum('ij,ik->jk', misfit, user_bf, preferred_element_type=jnp.float32)]
    ppermute x20 -> x5, waiting for transfers between devices: 33.7 us -> 72.4 us  [shift(): return lax.ppermute(block, axes, route)]
    pallas_call x0 -> x5, Pallas kernels: none -> 19.2 us  [update_tile(): pl.pallas_call(functools.partial(tile_kernel, user_rate, item_rate), out_...]
    ppermute x20 -> x5, starting transfers between devices: 20 us -> 7.33 us  [shift(): return lax.ppermute(block, axes, route)]
    and x18 -> x0, local copies, waits for them, and re-layouts: 7.03 us -> none  [expand(): nonzero & (tile_flags[:, None, :, None] > 0)]
    squeeze x1 -> x6, local copies, waits for them, and re-layouts: 0.75 us -> 3.39 us  [body(): tile_flags = block_mask[:, stratum, :]]
    unnamed x82 -> x11, local copies, waits for them, and re-layouts: 1.98 us -> 3.97 us
  transfers between devices with their start and end apart: 20 -> 5, of which waited for: 10 -> 5; matrix products, arithmetic and copies ran while one was open for 32% -> 2% of each run, Pallas kernels for 0% -> 0%
where the time goes in v2:
time: 111 us
  waiting for transfers between devices  72.4 us (65%)
  Pallas kernels  19.2 us (17%)
  local copies, waits for them, and re-layouts  11.4 us (10%)
  starting transfers between devices  7.33 us (7%)
    ppermute x5, waiting for transfers between devices, shift(): return lax.ppermute(block, axes, route)  72.4 us
    pallas_call x5, Pallas kernels, update_tile(): pl.pallas_call(functools.partial(tile_kernel, user_rate, item_rate), out_...  19.2 us
    ppermute x5, starting transfers between devices, shift(): return lax.ppermute(block, axes, route)  7.33 us
    squeeze x1, local copies, waits for them, and re-layouts, body(): tile_rates = ratings[:, stratum, :]  4.09 us
    unnamed x11, local copies, waits for them, and re-layouts  3.97 us
    squeeze x6, local copies, waits for them, and re-layouts, body(): tile_flags = block_mask[:, stratum, :]  3.39 us
  transfers between devices with their start and end apart: 5, of which 5 were waited for; matrix products, arithmetic and copies ran while one was open for 2% of the time, Pallas kernels for 0%

profile of v2, /device:TPU:1, one launch (start us, length us, event | category | flops | bytes accessed | tf_op | source)
XLA Modules:
  0.0 111.1 jit_solution(18312857571395437481)
XLA Ops:
  0.6 0.0 copy-start
  0.6 4.1 %slice_bitcast_fusion = (bf16[768,512]{1,0:T(8,128)(2,1)}, bf16[768,512]{1,0:T(8,128)(2,1)}, bf16[768,512]{1,0:T(8,128)(2,1)}, bf16[768,512]{1,0:T(8,128)(2,1)}, bf16[768,512]{1,0:T(8,128)(2,1)}) fusion(bf16[768,5,512]{2,0,1:T(8,128)(2,1)} %param.6), kind=kLoop, calls=%fused_computation | loop fusion | bytes 7864320 | tf_op jit(solution)/shard_map/squeeze | solution.py:94
  4.7 0.0 copy-done
  4.7 0.7 copy.6.flags_ref
  5.4 3.8 %shard_map.59 = (f32[768,256]{1,0:T(8,128)}, f32[512,256]{1,0:T(8,128)}) custom-call(s32[6,4]{1,0:T(8,128)} %copy.6.flags_ref, f32[768,256]{1,0:T(8,128)} %users_ref.1, f32[512,256]{1,0:T(8,128)} %items_ref.1, bf16[768,512]{1,0:T(8,128)(2,1)} %get-tuple-element.25.rates_ref), custom_call_target="tpu_custom_call" | custom-call | flops 805306368 | bytes 3407872 | tf_op jit(solution)/shard_map/pallas_call | solution.py:70
  9.3 2.0 %collective-permute-start = (f32[512,256]{1,0:T(8,128)}, f32[512,256]{1,0:T(8,128)S(1)}, u32[]{:S(2)}, u32[]{:S(2)}) collective-permute-start(f32[512,256]{1,0:T(8,128)} %get-tuple-element.13), channel_id=1, source_target_pairs={{0,4},{4,8},{8,12},{12,16},{16,20},{20,24},{24,28},{28,32},{32,36}... | collective-permute-start | bytes 1572872 | tf_op jit(solution)/shard_map/ppermute | solution.py:31
  11.3 0.7 copy.7.flags_ref
  12.0 18.9 %collective-permute-done.items_ref = f32[512,256]{1,0:T(8,128)S(1)} collective-permute-done((f32[512,256]{1,0:T(8,128)}, f32[512,256]{1,0:T(8,128)S(1)}, u32[]{:S(2)}, u32[]{:S(2)}) %collective-permute-start) | collective-permute-done | bytes 524320 | tf_op jit(solution)/shard_map/ppermute | solution.py:31
  30.9 0.0 copy-start.2
  30.9 0.8 copy-done.2
  31.7 3.8 %shard_map.60 = (f32[768,256]{1,0:T(8,128)}, f32[512,256]{1,0:T(8,128)}) custom-call(s32[6,4]{1,0:T(8,128)} %copy.7.flags_ref, f32[768,256]{1,0:T(8,128)} %get-tuple-element.12.users_ref, f32[512,256]{1,0:T(8,128)} %copy-done.2, bf16[768,512]{1,0:T(8,128)(2,1)} %get-tuple-element.24.rates_ref), custom_call_target="tpu_custom_call" | custom-call | flops 805306368 | bytes 3407872 | tf_op jit(solution)/shard_map/pallas_call | solution.py:70
  35.5 0.0 collective-permute-start.1
  35.5 0.7 copy.8.flags_ref
  36.2 16.0 %collective-permute-done.1.items_ref = f32[512,256]{1,0:T(8,128)S(1)} collective-permute-done((f32[512,256]{1,0:T(8,128)}, f32[512,256]{1,0:T(8,128)S(1)}, u32[]{:S(2)}, u32[]{:S(2)}) %collective-permute-start.1) | collective-permute-done | bytes 524320 | tf_op jit(solution)/shard_map/ppermute | solution.py:31
  52.2 0.0 copy-start.3
  52.2 0.8 copy-done.3
  53.0 3.8 %shard_map.61 = (f32[768,256]{1,0:T(8,128)}, f32[512,256]{1,0:T(8,128)}) custom-call(s32[6,4]{1,0:T(8,128)} %copy.8.flags_ref, f32[768,256]{1,0:T(8,128)} %get-tuple-element.14.users_ref, f32[512,256]{1,0:T(8,128)} %copy-done.3, bf16[768,512]{1,0:T(8,128)(2,1)} %get-tuple-element.23.rates_ref), custom_call_target="tpu_custom_call" | custom-call | flops 805306368 | bytes 3407872 | tf_op jit(solution)/shard_map/pallas_call | solution.py:70
  56.8 0.0 collective-permute-start.2
  56.8 0.7 copy.9.flags_ref
  57.5 15.1 %collective-permute-done.2.items_ref = f32[512,256]{1,0:T(8,128)S(1)} collective-permute-done((f32[512,256]{1,0:T(8,128)}, f32[512,256]{1,0:T(8,128)S(1)}, u32[]{:S(2)}, u32[]{:S(2)}) %collective-permute-start.2) | collective-permute-done | bytes 524320 | tf_op jit(solution)/shard_map/ppermute | solution.py:31
  72.6 0.0 copy-start.4
  72.6 0.8 copy-done.4
  73.4 3.8 %shard_map.62 = (f32[768,256]{1,0:T(8,128)}, f32[512,256]{1,0:T(8,128)}) custom-call(s32[6,4]{1,0:T(8,128)} %copy.9.flags_ref, f32[768,256]{1,0:T(8,128)} %get-tuple-element.16.users_ref, f32[512,256]{1,0:T(8,128)} %copy-done.4, bf16[768,512]{1,0:T(8,128)(2,1)} %get-tuple-element.26.rates_ref), custom_call_target="tpu_custom_call" | custom-call | flops 805306368 | bytes 3407872 | tf_op jit(solution)/shard_map/pallas_call | solution.py:70
  77.2 5.3 %collective-permute-start.3 = (f32[512,256]{1,0:T(8,128)}, f32[512,256]{1,0:T(8,128)S(1)}, u32[]{:S(2)}, u32[]{:S(2)}) collective-permute-start(f32[512,256]{1,0:T(8,128)} %get-tuple-element.19), channel_id=1, source_target_pairs={{0,1},{1,2},{2,3},{3,0},{4,5},{5,6},{6,7},{7,4},{8,9},{9,10},{10,1... | collective-permute-start | bytes 1572872 | tf_op jit(solution)/shard_map/ppermute | solution.py:31
  82.5 0.7 copy.10.flags_ref
  83.2 8.5 %collective-permute-done.3.items_ref = f32[512,256]{1,0:T(8,128)S(1)} collective-permute-done((f32[512,256]{1,0:T(8,128)}, f32[512,256]{1,0:T(8,128)S(1)}, u32[]{:S(2)}, u32[]{:S(2)}) %collective-permute-start.3) | collective-permute-done | bytes 524320 | tf_op jit(solution)/shard_map/ppermute | solution.py:31
  91.7 0.0 copy-start.1
  91.7 0.8 copy-done.1
  92.5 3.9 %shard_map.63 = (f32[768,256]{1,0:T(8,128)}, f32[512,256]{1,0:T(8,128)}) custom-call(s32[6,4]{1,0:T(8,128)} %copy.10.flags_ref, f32[768,256]{1,0:T(8,128)} %get-tuple-element.18.users_ref, f32[512,256]{1,0:T(8,128)} %copy-done.1, bf16[768,512]{1,0:T(8,128)(2,1)} %get-tuple-element.22.rates_ref), custom_call_target="tpu_custom_call" | custom-call | flops 805306368 | bytes 3407872 | tf_op jit(solution)/shard_map/pallas_call | solution.py:70
  96.4 0.0 collective-permute-start.4
  96.4 13.9 %collective-permute-done.4 = f32[512,256]{1,0:T(8,128)S(1)} collective-permute-done((f32[512,256]{1,0:T(8,128)}, f32[512,256]{1,0:T(8,128)S(1)}, u32[]{:S(2)}, u32[]{:S(2)}) %collective-permute-start.4) | collective-permute-done | bytes 524320 | tf_op jit(solution)/shard_map/ppermute | solution.py:31
  110.3 0.8 copy.12
  (1 shorter events, 0.0 us)
Async XLA Ops:
  0.6 4.1 %copy-start = (s32[6,5,4]{0,2,1:T(4,128)S(1)}, s32[6,5,4]{0,2,1:T(4,128)}, u32[]{:S(2)}) copy-start(s32[6,5,4]{0,2,1:T(4,128)} %param.7) | copy-start | bytes 1444
  9.3 21.6 %collective-permute-start = (f32[512,256]{1,0:T(8,128)}, f32[512,256]{1,0:T(8,128)S(1)}, u32[]{:S(2)}, u32[]{:S(2)}) collective-permute-start(f32[512,256]{1,0:T(8,128)} %get-tuple-element.13), channel_id=1, source_target_pairs={{0,4},{4,8},{8,12},{12,16},{16,20},{20,24},{24,28},{28,32},{32,36}... | collective-permute-start | bytes 1572872 | tf_op jit(solution)/shard_map/ppermute | solution.py:31
  30.9 0.8 copy-start.2
  35.5 16.7 %collective-permute-start.1 = (f32[512,256]{1,0:T(8,128)}, f32[512,256]{1,0:T(8,128)S(1)}, u32[]{:S(2)}, u32[]{:S(2)}) collective-permute-start(f32[512,256]{1,0:T(8,128)} %get-tuple-element.15), channel_id=1, source_target_pairs={{0,4},{4,8},{8,12},{12,16},{16,20},{20,24},{24,28},{28,32},{32,36}... | collective-permute-start | bytes 1572872 | tf_op jit(solution)/shard_map/ppermute | solution.py:31
  52.2 0.8 copy-start.3
  56.8 15.8 %collective-permute-start.2 = (f32[512,256]{1,0:T(8,128)}, f32[512,256]{1,0:T(8,128)S(1)}, u32[]{:S(2)}, u32[]{:S(2)}) collective-permute-start(f32[512,256]{1,0:T(8,128)} %get-tuple-element.17), channel_id=1, source_target_pairs={{0,4},{4,8},{8,12},{12,16},{16,20},{20,24},{24,28},{28,32},{32,36}... | collective-permute-start | bytes 1572872 | tf_op jit(solution)/shard_map/ppermute | solution.py:31
  72.6 0.8 copy-start.4
  77.2 14.4 %collective-permute-start.3 = (f32[512,256]{1,0:T(8,128)}, f32[512,256]{1,0:T(8,128)S(1)}, u32[]{:S(2)}, u32[]{:S(2)}) collective-permute-start(f32[512,256]{1,0:T(8,128)} %get-tuple-element.19), channel_id=1, source_target_pairs={{0,1},{1,2},{2,3},{3,0},{4,5},{5,6},{6,7},{7,4},{8,9},{9,10},{10,1... | collective-permute-start | bytes 1572872 | tf_op jit(solution)/shard_map/ppermute | solution.py:31
  91.7 0.8 copy-start.1
  96.4 13.9 %collective-permute-start.4 = (f32[512,256]{1,0:T(8,128)}, f32[512,256]{1,0:T(8,128)S(1)}, u32[]{:S(2)}, u32[]{:S(2)}) collective-permute-start(f32[512,256]{1,0:T(8,128)} %get-tuple-element.21), channel_id=1, source_target_pairs={{0,247},{1,244},{2,245},{3,246},{4,251},{5,248},{6,249},{7,250},{8... | collective-permute-start | bytes 1572872 | tf_op jit(solution)/shard_map/ppermute | solution.py:31

commit v3 on v2

--- a/solution.py
+++ b/solution.py
@@ -91,8 +91,11 @@
     user_rows = user_factors
     item_rows = item_factors
     for stratum in range(strata):
-        tile_rates = ratings[:, stratum, :]
-        tile_flags = block_mask[:, stratum, :]
+        rates_src, flags_src = ratings, block_mask
+        if stratum > 0:
+            rates_src, flags_src, user_rows = lax.optimization_barrier((ratings, block_mask, user_rows))
+        tile_rates = rates_src[:, stratum, :]
+        tile_flags = flags_src[:, stratum, :]
         user_rows, item_rows = update_tile(user_rows, item_rows, tile_rates, tile_flags, user_rate, item_rate)
         if stratum < strata - 2:
             item_rows = shift(item_rows, "blk", (n_blk,), (1,))

time: 111 us -> 110 us (level)
  waiting for transfers between devices: 72.4 us -> 64.1 us
  local copies, waits for them, and re-layouts: 11.4 us -> 18.5 us
    ppermute x5, waiting for transfers between devices: 72.4 us -> 64.1 us  [shift(): return lax.ppermute(block, axes, route)]
    squeeze x7 -> x15, local copies, waits for them, and re-layouts: 7.48 us -> 14.5 us  [the longest x5 10.4 us: body(): tile_rates = rates_src[:, stratum, :]]
  transfers between devices with their start and end apart: 5 -> 5, of which waited for: 5 -> 5; matrix products, arithmetic and copies ran while one was open for 2% -> 10% of each run, Pallas kernels for 0% -> 0%
where the time goes in v3:
time: 110 us
  waiting for transfers between devices  64.1 us (58%)
  Pallas kernels  19.2 us (17%)
  local copies, waits for them, and re-layouts  18.5 us (17%)
  starting transfers between devices  7.33 us (7%)
    ppermute x5, waiting for transfers between devices, shift(): return lax.ppermute(block, axes, route)  64.1 us
    pallas_call x5, Pallas kernels, update_tile(): pl.pallas_call(functools.partial(tile_kernel, user_rate, item_rate), out_...  19.2 us
    squeeze x5, local copies, waits for them, and re-layouts, body(): tile_rates = rates_src[:, stratum, :]  10.4 us
    ppermute x5, starting transfers between devices, shift(): return lax.ppermute(block, axes, route)  7.33 us
    squeeze x10, local copies, waits for them, and re-layouts, body(): tile_flags = flags_src[:, stratum, :]  4.14 us
    unnamed x11, local copies, waits for them, and re-layouts  3.97 us
  transfers between devices with their start and end apart: 5, of which 5 were waited for; matrix products, arithmetic and copies ran while one was open for 10% of the time, Pallas kernels for 0%

profile of v3, /device:TPU:1, one launch (start us, length us, event | category | flops | bytes accessed | tf_op | source)
XLA Modules:
  0.0 109.8 jit_solution(13573511642451093345)
XLA Ops:
  0.6 0.0 copy-start
  0.6 0.7 slice_bitcast_fusion.9
  1.4 0.7 copy.6.flags_ref
  2.1 2.1 %slice_bitcast_fusion.4.rates_ref = bf16[768,512]{1,0:T(8,128)(2,1)} fusion(bf16[768,5,512]{2,0,1:T(8,128)(2,1)} %param.6), kind=kLoop, calls=%fused_computation.4 | loop fusion | bytes 1572864 | tf_op jit(solution)/shard_map/squeeze | solution.py:97
  4.1 3.8 %shard_map.59 = (f32[768,256]{1,0:T(8,128)}, f32[512,256]{1,0:T(8,128)}) custom-call(s32[6,4]{1,0:T(8,128)} %copy.6.flags_ref, f32[768,256]{1,0:T(8,128)} %users_ref.1, f32[512,256]{1,0:T(8,128)} %items_ref.1, bf16[768,512]{1,0:T(8,128)(2,1)} %slice_bitcast_fusion.4.rates_ref), custom_call_target="tpu_custom_call" | custom-call | flops 805306368 | bytes 3407872 | tf_op jit(solution)/shard_map/pallas_call | solution.py:70
  8.0 2.0 %collective-permute-start = (f32[512,256]{1,0:T(8,128)}, f32[512,256]{1,0:T(8,128)S(1)}, u32[]{:S(2)}, u32[]{:S(2)}) collective-permute-start(f32[512,256]{1,0:T(8,128)} %get-tuple-element.27), channel_id=1, source_target_pairs={{0,4},{4,8},{8,12},{12,16},{16,20},{20,24},{24,28},{28,32},{32,36}... | collective-permute-start | bytes 1572872 | tf_op jit(solution)/shard_map/ppermute | solution.py:31
  10.0 0.0 copy-done
  10.0 0.7 copy.7.flags_ref
  10.7 2.1 %slice_bitcast_fusion.3.rates_ref = bf16[768,512]{1,0:T(8,128)(2,1)} fusion(bf16[768,5,512]{2,0,1:T(8,128)(2,1)} %param.6), kind=kLoop, calls=%fused_computation.3 | loop fusion | bytes 1572864 | tf_op jit(solution)/shard_map/squeeze | solution.py:97
  12.7 16.8 %collective-permute-done.items_ref = f32[512,256]{1,0:T(8,128)S(1)} collective-permute-done((f32[512,256]{1,0:T(8,128)}, f32[512,256]{1,0:T(8,128)S(1)}, u32[]{:S(2)}, u32[]{:S(2)}) %collective-permute-start) | collective-permute-done | bytes 524320 | tf_op jit(solution)/shard_map/ppermute | solution.py:31
  29.6 0.0 copy-start.1
  29.6 0.8 copy-done.1
  30.4 3.8 %shard_map.60 = (f32[768,256]{1,0:T(8,128)}, f32[512,256]{1,0:T(8,128)}) custom-call(s32[6,4]{1,0:T(8,128)} %copy.7.flags_ref, f32[768,256]{1,0:T(8,128)} %get-tuple-element.26.users_ref, f32[512,256]{1,0:T(8,128)} %copy-done.1, bf16[768,512]{1,0:T(8,128)(2,1)} %slice_bitcast_fusion.3.rates_ref), custom_call_target="tpu_custom_call" | custom-call | flops 805306368 | bytes 3407872 | tf_op jit(solution)/shard_map/pallas_call | solution.py:70
  34.2 0.0 collective-permute-start.1
  34.2 0.7 copy.8.flags_ref
  34.9 2.1 %slice_bitcast_fusion.2.rates_ref = bf16[768,512]{1,0:T(8,128)(2,1)} fusion(bf16[768,5,512]{2,0,1:T(8,128)(2,1)} %param.6), kind=kLoop, calls=%fused_computation.2 | loop fusion | bytes 1572864 | tf_op jit(solution)/shard_map/squeeze | solution.py:97
  37.0 13.9 %collective-permute-done.1.items_ref = f32[512,256]{1,0:T(8,128)S(1)} collective-permute-done((f32[512,256]{1,0:T(8,128)}, f32[512,256]{1,0:T(8,128)S(1)}, u32[]{:S(2)}, u32[]{:S(2)}) %collective-permute-start.1) | collective-permute-done | bytes 524320 | tf_op jit(solution)/shard_map/ppermute | solution.py:31
  50.9 0.0 copy-start.2
  50.9 0.8 copy-done.2
  51.7 3.8 %shard_map.61 = (f32[768,256]{1,0:T(8,128)}, f32[512,256]{1,0:T(8,128)}) custom-call(s32[6,4]{1,0:T(8,128)} %copy.8.flags_ref, f32[768,256]{1,0:T(8,128)} %get-tuple-element.31.users_ref, f32[512,256]{1,0:T(8,128)} %copy-done.2, bf16[768,512]{1,0:T(8,128)(2,1)} %slice_bitcast_fusion.2.rates_ref), custom_call_target="tpu_custom_call" | custom-call | flops 805306368 | bytes 3407872 | tf_op jit(solution)/shard_map/pallas_call | solution.py:70
  55.5 0.0 collective-permute-start.2
  55.5 0.7 copy.9.flags_ref
  56.2 2.1 %slice_bitcast_fusion.1.rates_ref = bf16[768,512]{1,0:T(8,128)(2,1)} fusion(bf16[768,5,512]{2,0,1:T(8,128)(2,1)} %param.6), kind=kLoop, calls=%fused_computation.1 | loop fusion | bytes 1572864 | tf_op jit(solution)/shard_map/squeeze | solution.py:97
  58.3 13.1 %collective-permute-done.2.items_ref = f32[512,256]{1,0:T(8,128)S(1)} collective-permute-done((f32[512,256]{1,0:T(8,128)}, f32[512,256]{1,0:T(8,128)S(1)}, u32[]{:S(2)}, u32[]{:S(2)}) %collective-permute-start.2) | collective-permute-done | bytes 524320 | tf_op jit(solution)/shard_map/ppermute | solution.py:31
  71.3 0.0 copy-start.3
  71.3 0.8 copy-done.3
  72.1 3.8 %shard_map.62 = (f32[768,256]{1,0:T(8,128)}, f32[512,256]{1,0:T(8,128)}) custom-call(s32[6,4]{1,0:T(8,128)} %copy.9.flags_ref, f32[768,256]{1,0:T(8,128)} %get-tuple-element.36.users_ref, f32[512,256]{1,0:T(8,128)} %copy-done.3, bf16[768,512]{1,0:T(8,128)(2,1)} %slice_bitcast_fusion.1.rates_ref), custom_call_target="tpu_custom_call" | custom-call | flops 805306368 | bytes 3407872 | tf_op jit(solution)/shard_map/pallas_call | solution.py:70
  76.0 5.3 %collective-permute-start.3 = (f32[512,256]{1,0:T(8,128)}, f32[512,256]{1,0:T(8,128)S(1)}, u32[]{:S(2)}, u32[]{:S(2)}) collective-permute-start(f32[512,256]{1,0:T(8,128)} %get-tuple-element.42), channel_id=1, source_target_pairs={{0,1},{1,2},{2,3},{3,0},{4,5},{5,6},{6,7},{7,4},{8,9},{9,10},{10,1... | collective-permute-start | bytes 1572872 | tf_op jit(solution)/shard_map/ppermute | solution.py:31
  81.3 0.7 copy.10.flags_ref
  81.9 2.1 %slice_bitcast_fusion.rates_ref = bf16[768,512]{1,0:T(8,128)(2,1)} fusion(bf16[768,5,512]{2,0,1:T(8,128)(2,1)} %param.6), kind=kLoop, calls=%fused_computation | loop fusion | bytes 1572864 | tf_op jit(solution)/shard_map/squeeze | solution.py:97
  84.1 6.4 %collective-permute-done.3.items_ref = f32[512,256]{1,0:T(8,128)S(1)} collective-permute-done((f32[512,256]{1,0:T(8,128)}, f32[512,256]{1,0:T(8,128)S(1)}, u32[]{:S(2)}, u32[]{:S(2)}) %collective-permute-start.3) | collective-permute-done | bytes 524320 | tf_op jit(solution)/shard_map/ppermute | solution.py:31
  90.4 0.0 copy-start.4
  90.4 0.8 copy-done.4
  91.2 3.8 %shard_map.63 = (f32[768,256]{1,0:T(8,128)}, f32[512,256]{1,0:T(8,128)}) custom-call(s32[6,4]{1,0:T(8,128)} %copy.10.flags_ref, f32[768,256]{1,0:T(8,128)} %get-tuple-element.41.users_ref, f32[512,256]{1,0:T(8,128)} %copy-done.4, bf16[768,512]{1,0:T(8,128)(2,1)} %slice_bitcast_fusion.rates_ref), custom_call_target="tpu_custom_call" | custom-call | flops 805306368 | bytes 3407872 | tf_op jit(solution)/shard_map/pallas_call | solution.py:70
  95.1 0.0 collective-permute-start.4
  95.1 13.9 %collective-permute-done.4 = f32[512,256]{1,0:T(8,128)S(1)} collective-permute-done((f32[512,256]{1,0:T(8,128)}, f32[512,256]{1,0:T(8,128)S(1)}, u32[]{:S(2)}, u32[]{:S(2)}) %collective-permute-start.4) | collective-permute-done | bytes 524320 | tf_op jit(solution)/shard_map/ppermute | solution.py:31
  109.0 0.8 copy.12
  (4 shorter events, 0.0 us)
Async XLA Ops:
  0.6 9.4 %copy-start = (s32[6,5,4]{0,2,1:T(4,128)S(1)}, s32[6,5,4]{0,2,1:T(4,128)}, u32[]{:S(2)}) copy-start(s32[6,5,4]{0,2,1:T(4,128)} %param.7) | copy-start | bytes 1444
  8.0 21.6 %collective-permute-start = (f32[512,256]{1,0:T(8,128)}, f32[512,256]{1,0:T(8,128)S(1)}, u32[]{:S(2)}, u32[]{:S(2)}) collective-permute-start(f32[512,256]{1,0:T(8,128)} %get-tuple-element.27), channel_id=1, source_target_pairs={{0,4},{4,8},{8,12},{12,16},{16,20},{20,24},{24,28},{28,32},{32,36}... | collective-permute-start | bytes 1572872 | tf_op jit(solution)/shard_map/ppermute | solution.py:31
  29.6 0.8 copy-start.1
  34.2 16.7 %collective-permute-start.1 = (f32[512,256]{1,0:T(8,128)}, f32[512,256]{1,0:T(8,128)S(1)}, u32[]{:S(2)}, u32[]{:S(2)}) collective-permute-start(f32[512,256]{1,0:T(8,128)} %get-tuple-element.32), channel_id=1, source_target_pairs={{0,4},{4,8},{8,12},{12,16},{16,20},{20,24},{24,28},{28,32},{32,36}... | collective-permute-start | bytes 1572872 | tf_op jit(solution)/shard_map/ppermute | solution.py:31
  50.9 0.8 copy-start.2
  55.5 15.8 %collective-permute-start.2 = (f32[512,256]{1,0:T(8,128)}, f32[512,256]{1,0:T(8,128)S(1)}, u32[]{:S(2)}, u32[]{:S(2)}) collective-permute-start(f32[512,256]{1,0:T(8,128)} %get-tuple-element.37), channel_id=1, source_target_pairs={{0,4},{4,8},{8,12},{12,16},{16,20},{20,24},{24,28},{28,32},{32,36}... | collective-permute-start | bytes 1572872 | tf_op jit(solution)/shard_map/ppermute | solution.py:31
  71.3 0.8 copy-start.3
  76.0 14.5 %collective-permute-start.3 = (f32[512,256]{1,0:T(8,128)}, f32[512,256]{1,0:T(8,128)S(1)}, u32[]{:S(2)}, u32[]{:S(2)}) collective-permute-start(f32[512,256]{1,0:T(8,128)} %get-tuple-element.42), channel_id=1, source_target_pairs={{0,1},{1,2},{2,3},{3,0},{4,5},{5,6},{6,7},{7,4},{8,9},{9,10},{10,1... | collective-permute-start | bytes 1572872 | tf_op jit(solution)/shard_map/ppermute | solution.py:31
  90.4 0.8 copy-start.4
  95.1 13.9 %collective-permute-start.4 = (f32[512,256]{1,0:T(8,128)}, f32[512,256]{1,0:T(8,128)S(1)}, u32[]{:S(2)}, u32[]{:S(2)}) collective-permute-start(f32[512,256]{1,0:T(8,128)} %get-tuple-element.45), channel_id=1, source_target_pairs={{0,247},{1,244},{2,245},{3,246},{4,251},{5,248},{6,249},{7,250},{8... | collective-permute-start | bytes 1572872 | tf_op jit(solution)/shard_map/ppermute | solution.py:31

commit v4 on v3

--- a/solution.py
+++ b/solution.py
@@ -31,34 +31,38 @@
     return lax.ppermute(block, axes, route)
 
 
-def tile_kernel(user_rate, item_rate, flags_ref, users_ref, items_ref, rates_ref, users_out, items_out, obs_ref):
+def tile_kernel(user_rate, item_rate, flags_ref, users_ref, items_ref, rates_ref, users_out, items_out):
     row_blocks, col_blocks = flags_ref.shape
     rows, cols = rates_ref.shape
     bs_r = rows // row_blocks
     bs_c = cols // col_blocks
-    for r in range(row_blocks):
-        for c in range(col_blocks):
-            block = rates_ref[r * bs_r:(r + 1) * bs_r, c * bs_c:(c + 1) * bs_c]
-            keep = jnp.logical_and(block != 0, flags_ref[r, c] > 0)
-            obs_ref[r * bs_r:(r + 1) * bs_r, c * bs_c:(c + 1) * bs_c] = keep.astype(jnp.float32)
-    observed = obs_ref[...] > 0
-    rates = rates_ref[...].astype(jnp.float32)
-    user_rows = users_ref[...]
     item_rows = items_ref[...]
     item_bf = item_rows.astype(jnp.bfloat16)
-    user_bf = user_rows.astype(jnp.bfloat16)
     nt = (((1,), (1,)), ((), ()))
-    predicted = lax.dot_general(user_bf, item_bf, nt, preferred_element_type=jnp.float32)
-    misfit = jnp.where(observed, jnp.clip(rates - predicted, -CLIP_LIMIT, CLIP_LIMIT), 0.0).astype(jnp.bfloat16)
-    gradient = jnp.dot(misfit, item_bf, preferred_element_type=jnp.float32)
-    user_rows = (1.0 - DECAY) * user_rows + user_rate * gradient
-    users_out[...] = user_rows
-    user_bf = user_rows.astype(jnp.bfloat16)
-    predicted = lax.dot_general(user_bf, item_bf, nt, preferred_element_type=jnp.float32)
-    misfit = jnp.where(observed, jnp.clip(rates - predicted, -CLIP_LIMIT, CLIP_LIMIT), 0.0).astype(jnp.bfloat16)
     tn = (((0,), (0,)), ((), ()))
-    gradient = lax.dot_general(misfit, user_bf, tn, preferred_element_type=jnp.float32)
-    items_out[...] = (1.0 - DECAY) * item_rows + item_rate * gradient
+    column_block = lax.broadcasted_iota(jnp.int32, (1, cols), 1) // bs_c
+    total = None
+    for r in range(row_blocks):
+        lo, hi = r * bs_r, (r + 1) * bs_r
+        col_flag = jnp.zeros((1, cols), jnp.int32)
+        for c in range(col_blocks):
+            col_flag = jnp.where(column_block == c, flags_ref[r, c], col_flag)
+        block = rates_ref[lo:hi, :]
+        observed = jnp.logical_and(block != 0, col_flag > 0)
+        rates = block.astype(jnp.float32)
+        user_rows = users_ref[lo:hi, :]
+        user_bf = user_rows.astype(jnp.bfloat16)
+        predicted = lax.dot_general(user_bf, item_bf, nt, preferred_element_type=jnp.float32)
+        misfit = jnp.where(observed, jnp.clip(rates - predicted, -CLIP_LIMIT, CLIP_LIMIT), 0.0)
+        gradient = jnp.dot(misfit.astype(jnp.bfloat16), item_bf, preferred_element_type=jnp.float32)
+        user_rows = (1.0 - DECAY) * user_rows + user_rate * gradient
+        users_out[lo:hi, :] = user_rows
+        user_bf = user_rows.astype(jnp.bfloat16)
+        predicted = lax.dot_general(user_bf, item_bf, nt, preferred_element_type=jnp.float32)
+        misfit = jnp.where(observed, jnp.clip(rates - predicted, -CLIP_LIMIT, CLIP_LIMIT), 0.0)
+        part = lax.dot_general(misfit.astype(jnp.bfloat16), user_bf, tn, preferred_element_type=jnp.float32)
+        total = part if total is None else total + part
+    items_out[...] = (1.0 - DECAY) * item_rows + item_rate * total
 
 
 def update_tile(user_rows, item_rows, tile_rates, tile_flags, user_rate, item_rate):
@@ -75,7 +79,6 @@
         ),
         in_specs=[pl.BlockSpec(memory_space=pltpu.SMEM), vmem, vmem, vmem],
         out_specs=(vmem, vmem),
-        scratch_shapes=[pltpu.VMEM((rows, cols), jnp.float32)],
         cost_estimate=pl.CostEstimate(flops=flops, bytes_accessed=nbytes, transcendentals=0),
     )(tile_flags, user_rows, item_rows, tile_rates)
 

time: 110 us -> 117 us (1.064)
  Pallas kernels: 19.2 us -> 27.5 us
  waiting for transfers between devices: 64.1 us -> 62.5 us
    pallas_call x5, Pallas kernels: 19.2 us -> 27.5 us  [update_tile(): pl.pallas_call(functools.partial(tile_kernel, user_rate, item_rate), out_...]
    ppermute x5, waiting for transfers between devices: 64.1 us -> 62.5 us  [shift(): return lax.ppermute(block, axes, route)]
  transfers between devices with their start and end apart: 5 -> 5, of which waited for: 5 -> 5; matrix products, arithmetic and copies ran while one was open for 10% -> 9% of each run, Pallas kernels for 0% -> 0%
where the time goes in v4:
time: 117 us; the launch traced here: 116 us
  waiting for transfers between devices  62.5 us (53%)
  Pallas kernels  27.5 us (24%)
  local copies, waits for them, and re-layouts  18.5 us (16%)
  starting transfers between devices  7.36 us (6%)
    ppermute x5, waiting for transfers between devices, shift(): return lax.ppermute(block, axes, route)  62.5 us
    pallas_call x5, Pallas kernels, update_tile(): pl.pallas_call(functools.partial(tile_kernel, user_rate, item_rate), out_...  27.5 us
    squeeze x5, local copies, waits for them, and re-layouts, body(): tile_rates = rates_src[:, stratum, :]  10.4 us
    ppermute x5, starting transfers between devices, shift(): return lax.ppermute(block, axes, route)  7.36 us
    squeeze x10, local copies, waits for them, and re-layouts, body(): tile_flags = flags_src[:, stratum, :]  4.14 us
    unnamed x11, local copies, waits for them, and re-layouts  3.97 us
  transfers between devices with their start and end apart: 5, of which 5 were waited for; matrix products, arithmetic and copies ran while one was open for 9% of the time, Pallas kernels for 0%

profile of v4, /device:TPU:1, one launch (start us, length us, event | category | flops | bytes accessed | tf_op | source)
XLA Modules:
  0.0 116.5 jit_solution(6700030192256060572)
XLA Ops:
  0.6 0.0 copy-start
  0.6 0.7 slice_bitcast_fusion.9
  1.4 0.7 copy.6.flags_ref
  2.1 2.1 %slice_bitcast_fusion.4.rates_ref = bf16[768,512]{1,0:T(8,128)(2,1)} fusion(bf16[768,5,512]{2,0,1:T(8,128)(2,1)} %param.6), kind=kLoop, calls=%fused_computation.4 | loop fusion | bytes 1572864 | tf_op jit(solution)/shard_map/squeeze | solution.py:100
  4.1 5.5 %shard_map.59 = (f32[768,256]{1,0:T(8,128)}, f32[512,256]{1,0:T(8,128)}) custom-call(s32[6,4]{1,0:T(8,128)} %copy.6.flags_ref, f32[768,256]{1,0:T(8,128)} %users_ref.1, f32[512,256]{1,0:T(8,128)} %items_ref.1, bf16[768,512]{1,0:T(8,128)(2,1)} %slice_bitcast_fusion.4.rates_ref), custom_call_target="tpu_custom_call" | custom-call | flops 805306368 | bytes 3407872 | tf_op jit(solution)/shard_map/pallas_call | solution.py:74
  9.6 2.0 %collective-permute-start = (f32[512,256]{1,0:T(8,128)}, f32[512,256]{1,0:T(8,128)S(1)}, u32[]{:S(2)}, u32[]{:S(2)}) collective-permute-start(f32[512,256]{1,0:T(8,128)} %get-tuple-element.27), channel_id=1, source_target_pairs={{0,4},{4,8},{8,12},{12,16},{16,20},{20,24},{24,28},{28,32},{32,36}... | collective-permute-start | bytes 1572872 | tf_op jit(solution)/shard_map/ppermute | solution.py:31
  11.7 0.0 copy-done
  11.7 0.7 copy.7.flags_ref
  12.3 2.1 %slice_bitcast_fusion.3.rates_ref = bf16[768,512]{1,0:T(8,128)(2,1)} fusion(bf16[768,5,512]{2,0,1:T(8,128)(2,1)} %param.6), kind=kLoop, calls=%fused_computation.3 | loop fusion | bytes 1572864 | tf_op jit(solution)/shard_map/squeeze | solution.py:100
  14.4 16.8 %collective-permute-done.items_ref = f32[512,256]{1,0:T(8,128)S(1)} collective-permute-done((f32[512,256]{1,0:T(8,128)}, f32[512,256]{1,0:T(8,128)S(1)}, u32[]{:S(2)}, u32[]{:S(2)}) %collective-permute-start) | collective-permute-done | bytes 524320 | tf_op jit(solution)/shard_map/ppermute | solution.py:31
  31.2 0.0 copy-start.1
  31.2 0.8 copy-done.1
  32.0 5.5 %shard_map.60 = (f32[768,256]{1,0:T(8,128)}, f32[512,256]{1,0:T(8,128)}) custom-call(s32[6,4]{1,0:T(8,128)} %copy.7.flags_ref, f32[768,256]{1,0:T(8,128)} %get-tuple-element.26.users_ref, f32[512,256]{1,0:T(8,128)} %copy-done.1, bf16[768,512]{1,0:T(8,128)(2,1)} %slice_bitcast_fusion.3.rates_ref), custom_call_target="tpu_custom_call" | custom-call | flops 805306368 | bytes 3407872 | tf_op jit(solution)/shard_map/pallas_call | solution.py:74
  37.5 0.0 collective-permute-start.1
  37.5 0.7 copy.8.flags_ref
  38.2 2.1 %slice_bitcast_fusion.2.rates_ref = bf16[768,512]{1,0:T(8,128)(2,1)} fusion(bf16[768,5,512]{2,0,1:T(8,128)(2,1)} %param.6), kind=kLoop, calls=%fused_computation.2 | loop fusion | bytes 1572864 | tf_op jit(solution)/shard_map/squeeze | solution.py:100
  40.3 13.9 %collective-permute-done.1.items_ref = f32[512,256]{1,0:T(8,128)S(1)} collective-permute-done((f32[512,256]{1,0:T(8,128)}, f32[512,256]{1,0:T(8,128)S(1)}, u32[]{:S(2)}, u32[]{:S(2)}) %collective-permute-start.1) | collective-permute-done | bytes 524320 | tf_op jit(solution)/shard_map/ppermute | solution.py:31
  54.2 0.0 copy-start.2
  54.2 0.8 copy-done.2
  55.0 5.5 %shard_map.61 = (f32[768,256]{1,0:T(8,128)}, f32[512,256]{1,0:T(8,128)}) custom-call(s32[6,4]{1,0:T(8,128)} %copy.8.flags_ref, f32[768,256]{1,0:T(8,128)} %get-tuple-element.31.users_ref, f32[512,256]{1,0:T(8,128)} %copy-done.2, bf16[768,512]{1,0:T(8,128)(2,1)} %slice_bitcast_fusion.2.rates_ref), custom_call_target="tpu_custom_call" | custom-call | flops 805306368 | bytes 3407872 | tf_op jit(solution)/shard_map/pallas_call | solution.py:74
  60.5 0.0 collective-permute-start.2
  60.5 0.7 copy.9.flags_ref
  61.1 2.1 %slice_bitcast_fusion.1.rates_ref = bf16[768,512]{1,0:T(8,128)(2,1)} fusion(bf16[768,5,512]{2,0,1:T(8,128)(2,1)} %param.6), kind=kLoop, calls=%fused_computation.1 | loop fusion | bytes 1572864 | tf_op jit(solution)/shard_map/squeeze | solution.py:100
  63.2 13.1 %collective-permute-done.2.items_ref = f32[512,256]{1,0:T(8,128)S(1)} collective-permute-done((f32[512,256]{1,0:T(8,128)}, f32[512,256]{1,0:T(8,128)S(1)}, u32[]{:S(2)}, u32[]{:S(2)}) %collective-permute-start.2) | collective-permute-done | bytes 524320 | tf_op jit(solution)/shard_map/ppermute | solution.py:31
  76.3 0.0 copy-start.3
  76.3 0.8 copy-done.3
  77.1 5.5 %shard_map.62 = (f32[768,256]{1,0:T(8,128)}, f32[512,256]{1,0:T(8,128)}) custom-call(s32[6,4]{1,0:T(8,128)} %copy.9.flags_ref, f32[768,256]{1,0:T(8,128)} %get-tuple-element.36.users_ref, f32[512,256]{1,0:T(8,128)} %copy-done.3, bf16[768,512]{1,0:T(8,128)(2,1)} %slice_bitcast_fusion.1.rates_ref), custom_call_target="tpu_custom_call" | custom-call | flops 805306368 | bytes 3407872 | tf_op jit(solution)/shard_map/pallas_call | solution.py:74
  82.6 5.3 %collective-permute-start.3 = (f32[512,256]{1,0:T(8,128)}, f32[512,256]{1,0:T(8,128)S(1)}, u32[]{:S(2)}, u32[]{:S(2)}) collective-permute-start(f32[512,256]{1,0:T(8,128)} %get-tuple-element.42), channel_id=1, source_target_pairs={{0,1},{1,2},{2,3},{3,0},{4,5},{5,6},{6,7},{7,4},{8,9},{9,10},{10,1... | collective-permute-start | bytes 1572872 | tf_op jit(solution)/shard_map/ppermute | solution.py:31
  87.9 0.7 copy.10.flags_ref
  88.6 2.1 %slice_bitcast_fusion.rates_ref = bf16[768,512]{1,0:T(8,128)(2,1)} fusion(bf16[768,5,512]{2,0,1:T(8,128)(2,1)} %param.6), kind=kLoop, calls=%fused_computation | loop fusion | bytes 1572864 | tf_op jit(solution)/shard_map/squeeze | solution.py:100
  90.7 3.9 %collective-permute-done.3.items_ref = f32[512,256]{1,0:T(8,128)S(1)} collective-permute-done((f32[512,256]{1,0:T(8,128)}, f32[512,256]{1,0:T(8,128)S(1)}, u32[]{:S(2)}, u32[]{:S(2)}) %collective-permute-start.3) | collective-permute-done | bytes 524320 | tf_op jit(solution)/shard_map/ppermute | solution.py:31
  94.5 0.0 copy-start.4
  94.5 0.8 copy-done.4
  95.3 5.5 %shard_map.63 = (f32[768,256]{1,0:T(8,128)}, f32[512,256]{1,0:T(8,128)}) custom-call(s32[6,4]{1,0:T(8,128)} %copy.10.flags_ref, f32[768,256]{1,0:T(8,128)} %get-tuple-element.41.users_ref, f32[512,256]{1,0:T(8,128)} %copy-done.4, bf16[768,512]{1,0:T(8,128)(2,1)} %slice_bitcast_fusion.rates_ref), custom_call_target="tpu_custom_call" | custom-call | flops 805306368 | bytes 3407872 | tf_op jit(solution)/shard_map/pallas_call | solution.py:74
  100.8 0.0 collective-permute-start.4
  100.8 14.9 %collective-permute-done.4 = f32[512,256]{1,0:T(8,128)S(1)} collective-permute-done((f32[512,256]{1,0:T(8,128)}, f32[512,256]{1,0:T(8,128)S(1)}, u32[]{:S(2)}, u32[]{:S(2)}) %collective-permute-start.4) | collective-permute-done | bytes 524320 | tf_op jit(solution)/shard_map/ppermute | solution.py:31
  115.7 0.8 copy.12
  (4 shorter events, 0.0 us)
Async XLA Ops:
  0.6 11.0 %copy-start = (s32[6,5,4]{0,2,1:T(4,128)S(1)}, s32[6,5,4]{0,2,1:T(4,128)}, u32[]{:S(2)}) copy-start(s32[6,5,4]{0,2,1:T(4,128)} %param.7) | copy-start | bytes 1444
  9.6 21.6 %collective-permute-start = (f32[512,256]{1,0:T(8,128)}, f32[512,256]{1,0:T(8,128)S(1)}, u32[]{:S(2)}, u32[]{:S(2)}) collective-permute-start(f32[512,256]{1,0:T(8,128)} %get-tuple-element.27), channel_id=1, source_target_pairs={{0,4},{4,8},{8,12},{12,16},{16,20},{20,24},{24,28},{28,32},{32,36}... | collective-permute-start | bytes 1572872 | tf_op jit(solution)/shard_map/ppermute | solution.py:31
  31.2 0.8 copy-start.1
  37.5 16.7 %collective-permute-start.1 = (f32[512,256]{1,0:T(8,128)}, f32[512,256]{1,0:T(8,128)S(1)}, u32[]{:S(2)}, u32[]{:S(2)}) collective-permute-start(f32[512,256]{1,0:T(8,128)} %get-tuple-element.32), channel_id=1, source_target_pairs={{0,4},{4,8},{8,12},{12,16},{16,20},{20,24},{24,28},{28,32},{32,36}... | collective-permute-start | bytes 1572872 | tf_op jit(solution)/shard_map/ppermute | solution.py:31
  54.2 0.8 copy-start.2
  60.5 15.8 %collective-permute-start.2 = (f32[512,256]{1,0:T(8,128)}, f32[512,256]{1,0:T(8,128)S(1)}, u32[]{:S(2)}, u32[]{:S(2)}) collective-permute-start(f32[512,256]{1,0:T(8,128)} %get-tuple-element.37), channel_id=1, source_target_pairs={{0,4},{4,8},{8,12},{12,16},{16,20},{20,24},{24,28},{28,32},{32,36}... | collective-permute-start | bytes 1572872 | tf_op jit(solution)/shard_map/ppermute | solution.py:31
  76.3 0.8 copy-start.3
  82.6 12.0 %collective-permute-start.3 = (f32[512,256]{1,0:T(8,128)}, f32[512,256]{1,0:T(8,128)S(1)}, u32[]{:S(2)}, u32[]{:S(2)}) collective-permute-start(f32[512,256]{1,0:T(8,128)} %get-tuple-element.42), channel_id=1, source_target_pairs={{0,1},{1,2},{2,3},{3,0},{4,5},{5,6},{6,7},{7,4},{8,9},{9,10},{10,1... | collective-permute-start | bytes 1572872 | tf_op jit(solution)/shard_map/ppermute | solution.py:31
  94.5 0.8 copy-start.4
  100.8 14.9 %collective-permute-start.4 = (f32[512,256]{1,0:T(8,128)}, f32[512,256]{1,0:T(8,128)S(1)}, u32[]{:S(2)}, u32[]{:S(2)}) collective-permute-start(f32[512,256]{1,0:T(8,128)} %get-tuple-element.45), channel_id=1, source_target_pairs={{0,247},{1,244},{2,245},{3,246},{4,251},{5,248},{6,249},{7,250},{8... | collective-permute-start | bytes 1572872 | tf_op jit(solution)/shard_map/ppermute | solution.py:31

commit v5 on v3

--- a/solution.py
+++ b/solution.py
@@ -31,41 +31,42 @@
     return lax.ppermute(block, axes, route)
 
 
-def tile_kernel(user_rate, item_rate, flags_ref, users_ref, items_ref, rates_ref, users_out, items_out, obs_ref):
-    row_blocks, col_blocks = flags_ref.shape
-    rows, cols = rates_ref.shape
-    bs_r = rows // row_blocks
-    bs_c = cols // col_blocks
-    for r in range(row_blocks):
-        for c in range(col_blocks):
-            block = rates_ref[r * bs_r:(r + 1) * bs_r, c * bs_c:(c + 1) * bs_c]
-            keep = jnp.logical_and(block != 0, flags_ref[r, c] > 0)
-            obs_ref[r * bs_r:(r + 1) * bs_r, c * bs_c:(c + 1) * bs_c] = keep.astype(jnp.float32)
-    observed = obs_ref[...] > 0
-    rates = rates_ref[...].astype(jnp.float32)
+def tile_kernel(user_rate, item_rate, users_ref, items_ref, rates_ref, seen_ref, users_out, items_out):
+    rates = rates_ref[...]
+    seen = seen_ref[...]
     user_rows = users_ref[...]
     item_rows = items_ref[...]
     item_bf = item_rows.astype(jnp.bfloat16)
     user_bf = user_rows.astype(jnp.bfloat16)
     nt = (((1,), (1,)), ((), ()))
     predicted = lax.dot_general(user_bf, item_bf, nt, preferred_element_type=jnp.float32)
-    misfit = jnp.where(observed, jnp.clip(rates - predicted, -CLIP_LIMIT, CLIP_LIMIT), 0.0).astype(jnp.bfloat16)
+    misfit = (jnp.clip(rates - predicted, -CLIP_LIMIT, CLIP_LIMIT) * seen).astype(jnp.bfloat16)
     gradient = jnp.dot(misfit, item_bf, preferred_element_type=jnp.float32)
     user_rows = (1.0 - DECAY) * user_rows + user_rate * gradient
     users_out[...] = user_rows
     user_bf = user_rows.astype(jnp.bfloat16)
     predicted = lax.dot_general(user_bf, item_bf, nt, preferred_element_type=jnp.float32)
-    misfit = jnp.where(observed, jnp.clip(rates - predicted, -CLIP_LIMIT, CLIP_LIMIT), 0.0).astype(jnp.bfloat16)
+    misfit = (jnp.clip(rates - predicted, -CLIP_LIMIT, CLIP_LIMIT) * seen).astype(jnp.bfloat16)
     tn = (((0,), (0,)), ((), ()))
     gradient = lax.dot_general(misfit, user_bf, tn, preferred_element_type=jnp.float32)
     items_out[...] = (1.0 - DECAY) * item_rows + item_rate * gradient
 
 
+def expand(tile_rates, tile_flags):
+    row_blocks, col_blocks = tile_flags.shape
+    block_rows = tile_rates.shape[0] // row_blocks
+    block_cols = tile_rates.shape[1] // col_blocks
+    nonzero = tile_rates.reshape(row_blocks, block_rows, col_blocks, block_cols) != 0
+    return (nonzero & (tile_flags[:, None, :, None] > 0)).reshape(tile_rates.shape)
+
+
 def update_tile(user_rows, item_rows, tile_rates, tile_flags, user_rate, item_rate):
     rows, k = user_rows.shape
     cols = item_rows.shape[0]
+    seen = expand(tile_rates, tile_flags).astype(jnp.float32)
+    rates = tile_rates.astype(jnp.float32)
     flops = 8 * rows * cols * k
-    nbytes = 2 * (rows * k * 4 + cols * k * 4) + rows * cols * 2
+    nbytes = 2 * (rows * k * 4 + cols * k * 4) + 2 * rows * cols * 4
     vmem = pl.BlockSpec(memory_space=pltpu.VMEM)
     return pl.pallas_call(
         functools.partial(tile_kernel, user_rate, item_rate),
@@ -73,11 +74,10 @@
             jax.ShapeDtypeStruct(user_rows.shape, jnp.float32),
             jax.ShapeDtypeStruct(item_rows.shape, jnp.float32),
         ),
-        in_specs=[pl.BlockSpec(memory_space=pltpu.SMEM), vmem, vmem, vmem],
+        in_specs=[vmem, vmem, vmem, vmem],
         out_specs=(vmem, vmem),
-        scratch_shapes=[pltpu.VMEM((rows, cols), jnp.float32)],
         cost_estimate=pl.CostEstimate(flops=flops, bytes_accessed=nbytes, transcendentals=0),
-    )(tile_flags, user_rows, item_rows, tile_rates)
+    )(user_rows, item_rows, rates, seen)
 
 
 def body(user_factors, item_factors, ratings, block_mask):
@@ -93,7 +93,7 @@
     for stratum in range(strata):
         rates_src, flags_src = ratings, block_mask
         if stratum > 0:
-            rates_src, flags_src, user_rows = lax.optimization_barrier((ratings, block_mask, user_rows))
+            rates_src, user_rows = lax.optimization_barrier((ratings, user_rows))
         tile_rates = rates_src[:, stratum, :]
         tile_flags = flags_src[:, stratum, :]
         user_rows, item_rows = update_tile(user_rows, item_rows, tile_rates, tile_flags, user_rate, item_rate)

time: 110 us -> 116 us (1.055)
  other arithmetic: 0 us -> 26.4 us
  local copies, waits for them, and re-layouts: 18.5 us -> 5.86 us
  waiting for transfers between devices: 64.1 us -> 52.7 us
  Pallas kernels: 19.2 us -> 22.5 us
    convert_element_type x0 -> x10, other arithmetic: none -> 25.6 us  [the longest x5 13 us: update_tile(): seen = expand(tile_rates, tile_flags).astype(jnp.float32)]
    squeeze x15 -> x0, local copies, waits for them, and re-layouts: 14.5 us -> none  [the longest x5 10.4 us: body(): tile_rates = rates_src[:, stratum, :]]
    ppermute x5, waiting for transfers between devices: 64.1 us -> 52.7 us  [shift(): return lax.ppermute(block, axes, route)]
    pallas_call x5, Pallas kernels: 19.2 us -> 22.5 us  [update_tile(): pl.pallas_call(functools.partial(tile_kernel, user_rate, item_rate), out_...]
    and x0 -> x5, local copies, waits for them, and re-layouts: none -> 1.36 us  [expand(): nonzero & (tile_flags[:, None, :, None] > 0)]
    unnamed x11 -> x9, local copies, waits for them, and re-layouts: 3.97 us -> 3.96 us
  transfers between devices with their start and end apart: 5 -> 5, of which waited for: 5 -> 5; matrix products, arithmetic and copies ran while one was open for 10% -> 19% of each run, Pallas kernels for 0% -> 0%
where the time goes in v5:
time: 116 us; the launch traced here: 115 us
  waiting for transfers between devices  52.7 us (45%)
  other arithmetic  26.4 us (23%)
  Pallas kernels  22.5 us (19%)
  starting transfers between devices  7.33 us (6%)
  local copies, waits for them, and re-layouts  5.86 us (5%)
    ppermute x5, waiting for transfers between devices, shift(): return lax.ppermute(block, axes, route)  52.7 us
    pallas_call x5, Pallas kernels, update_tile(): pl.pallas_call(functools.partial(tile_kernel, user_rate, item_rate), out_...  22.5 us
    convert_element_type x5, other arithmetic, update_tile(): seen = expand(tile_rates, tile_flags).astype(jnp.float32)  13 us
    convert_element_type x5, other arithmetic, update_tile(): rates = tile_rates.astype(jnp.float32)  12.6 us
    ppermute x5, starting transfers between devices, shift(): return lax.ppermute(block, axes, route)  7.33 us
    unnamed x9, local copies, waits for them, and re-layouts  3.96 us
  transfers between devices with their start and end apart: 5, of which 5 were waited for; matrix products, arithmetic and copies ran while one was open for 19% of the time, Pallas kernels for 0%

profile of v5, /device:TPU:1, one launch (start us, length us, event | category | flops | bytes accessed | tf_op | source)
XLA Modules:
  0.0 115.5 jit_solution(12180506184431249695)
XLA Ops:
  0.6 0.8 fusion.9
  1.4 0.1 copy.6
  1.5 2.5 %bitcast_convert_fusion.4.rates_ref = f32[768,512]{1,0:T(8,128)} fusion(bf16[768,5,512]{2,0,1:T(8,128)(2,1)} %param.6), kind=kLoop, calls=%fused_computation.14 | loop fusion | flops 393216 | bytes 2359296 | tf_op jit(solution)/shard_map/convert_element_type | solution.py:67
  4.0 0.3 and.55
  4.3 2.6 %fusion.4.seen_ref = f32[768,512]{1,0:T(8,128)} fusion(pred[96,8,4,128]{3,2,1,0:T(4,128)(4,1)S(1)} %bitcast.65, bf16[768,5,512]{2,0,1:T(8,128)(2,1)} %param.6), kind=kLoop, calls=%fused_computation.9 | loop fusion | flops 1966080 | bytes 2752512 | tf_op jit(solution)/shard_map/convert_element_type | solution.py:66
  6.9 4.5 %shard_map.59 = (f32[768,256]{1,0:T(8,128)}, f32[512,256]{1,0:T(8,128)}) custom-call(f32[768,256]{1,0:T(8,128)} %users_ref.1, f32[512,256]{1,0:T(8,128)} %items_ref.1, f32[768,512]{1,0:T(8,128)} %bitcast_convert_fusion.4.rates_ref, f32[768,512]{1,0:T(8,128)} %fusion.4.seen_ref), custom_call_target="tpu_custom_call" | custom-call | flops 805306368 | bytes 5767168 | tf_op jit(solution)/shard_map/pallas_call | solution.py:71
  11.4 2.0 %collective-permute-start = (f32[512,256]{1,0:T(8,128)}, f32[512,256]{1,0:T(8,128)S(1)}, u32[]{:S(2)}, u32[]{:S(2)}) collective-permute-start(f32[512,256]{1,0:T(8,128)} %get-tuple-element.22), channel_id=1, source_target_pairs={{0,4},{4,8},{8,12},{12,16},{16,20},{20,24},{24,28},{28,32},{32,36}... | collective-permute-start | bytes 1572872 | tf_op jit(solution)/shard_map/ppermute | solution.py:31
  13.4 0.1 copy.7
  13.5 0.1 copy.8
  13.6 0.1 copy.9
  13.7 0.1 copy.10
  13.8 2.5 %bitcast_convert_fusion.3.rates_ref = f32[768,512]{1,0:T(8,128)} fusion(bf16[768,5,512]{2,0,1:T(8,128)(2,1)} %param.6), kind=kLoop, calls=%fused_computation.13 | loop fusion | flops 393216 | bytes 2359296 | tf_op jit(solution)/shard_map/convert_element_type | solution.py:67
  16.4 0.3 and.58
  16.6 2.6 %fusion.3.seen_ref = f32[768,512]{1,0:T(8,128)} fusion(pred[96,8,4,128]{3,2,1,0:T(4,128)(4,1)S(1)} %bitcast.66, bf16[768,5,512]{2,0,1:T(8,128)(2,1)} %param.6), kind=kLoop, calls=%fused_computation.7 | loop fusion | flops 1966080 | bytes 2752512 | tf_op jit(solution)/shard_map/convert_element_type | solution.py:66
  19.3 13.7 %collective-permute-done.items_ref = f32[512,256]{1,0:T(8,128)S(1)} collective-permute-done((f32[512,256]{1,0:T(8,128)}, f32[512,256]{1,0:T(8,128)S(1)}, u32[]{:S(2)}, u32[]{:S(2)}) %collective-permute-start) | collective-permute-done | bytes 524320 | tf_op jit(solution)/shard_map/ppermute | solution.py:31
  33.0 0.0 copy-start
  33.0 0.8 copy-done
  33.8 4.5 %shard_map.60 = (f32[768,256]{1,0:T(8,128)}, f32[512,256]{1,0:T(8,128)}) custom-call(f32[768,256]{1,0:T(8,128)} %get-tuple-element.21.users_ref, f32[512,256]{1,0:T(8,128)} %copy-done, f32[768,512]{1,0:T(8,128)} %bitcast_convert_fusion.3.rates_ref, f32[768,512]{1,0:T(8,128)} %fusion.3.seen_ref), custom_call_target="tpu_custom_call" | custom-call | flops 805306368 | bytes 5767168 | tf_op jit(solution)/shard_map/pallas_call | solution.py:71
  38.3 0.0 collective-permute-start.1
  38.3 2.5 %bitcast_convert_fusion.2.rates_ref = f32[768,512]{1,0:T(8,128)} fusion(bf16[768,5,512]{2,0,1:T(8,128)(2,1)} %param.6), kind=kLoop, calls=%fused_computation.12 | loop fusion | flops 393216 | bytes 2359296 | tf_op jit(solution)/shard_map/convert_element_type | solution.py:67
  40.8 0.3 and.61
  41.1 2.6 %fusion.2.seen_ref = f32[768,512]{1,0:T(8,128)} fusion(pred[96,8,4,128]{3,2,1,0:T(4,128)(4,1)S(1)} %bitcast.67, bf16[768,5,512]{2,0,1:T(8,128)(2,1)} %param.6), kind=kLoop, calls=%fused_computation.5 | loop fusion | flops 1966080 | bytes 2752512 | tf_op jit(solution)/shard_map/convert_element_type | solution.py:66
  43.7 11.3 %collective-permute-done.1.items_ref = f32[512,256]{1,0:T(8,128)S(1)} collective-permute-done((f32[512,256]{1,0:T(8,128)}, f32[512,256]{1,0:T(8,128)S(1)}, u32[]{:S(2)}, u32[]{:S(2)}) %collective-permute-start.1) | collective-permute-done | bytes 524320 | tf_op jit(solution)/shard_map/ppermute | solution.py:31
  55.0 0.0 copy-start.1
  55.0 0.8 copy-done.1
  55.7 4.5 %shard_map.61 = (f32[768,256]{1,0:T(8,128)}, f32[512,256]{1,0:T(8,128)}) custom-call(f32[768,256]{1,0:T(8,128)} %get-tuple-element.25.users_ref, f32[512,256]{1,0:T(8,128)} %copy-done.1, f32[768,512]{1,0:T(8,128)} %bitcast_convert_fusion.2.rates_ref, f32[768,512]{1,0:T(8,128)} %fusion.2.seen_ref), custom_call_target="tpu_custom_call" | custom-call | flops 805306368 | bytes 5767168 | tf_op jit(solution)/shard_map/pallas_call | solution.py:71
  60.2 0.0 collective-permute-start.2
  60.2 2.5 %bitcast_convert_fusion.1.rates_ref = f32[768,512]{1,0:T(8,128)} fusion(bf16[768,5,512]{2,0,1:T(8,128)(2,1)} %param.6), kind=kLoop, calls=%fused_computation.11 | loop fusion | flops 393216 | bytes 2359296 | tf_op jit(solution)/shard_map/convert_element_type | solution.py:67
  62.8 0.3 and.64
  63.0 2.6 %fusion.1.seen_ref = f32[768,512]{1,0:T(8,128)} fusion(pred[96,8,4,128]{3,2,1,0:T(4,128)(4,1)S(1)} %bitcast.68, bf16[768,5,512]{2,0,1:T(8,128)(2,1)} %param.6), kind=kLoop, calls=%fused_computation.3 | loop fusion | flops 1966080 | bytes 2752512 | tf_op jit(solution)/shard_map/convert_element_type | solution.py:66
  65.7 10.4 %collective-permute-done.2.items_ref = f32[512,256]{1,0:T(8,128)S(1)} collective-permute-done((f32[512,256]{1,0:T(8,128)}, f32[512,256]{1,0:T(8,128)S(1)}, u32[]{:S(2)}, u32[]{:S(2)}) %collective-permute-start.2) | collective-permute-done | bytes 524320 | tf_op jit(solution)/shard_map/ppermute | solution.py:31
  76.1 0.0 copy-start.2
  76.1 0.8 copy-done.2
  76.8 4.5 %shard_map.62 = (f32[768,256]{1,0:T(8,128)}, f32[512,256]{1,0:T(8,128)}) custom-call(f32[768,256]{1,0:T(8,128)} %get-tuple-element.29.users_ref, f32[512,256]{1,0:T(8,128)} %copy-done.2, f32[768,512]{1,0:T(8,128)} %bitcast_convert_fusion.1.rates_ref, f32[768,512]{1,0:T(8,128)} %fusion.1.seen_ref), custom_call_target="tpu_custom_call" | custom-call | flops 805306368 | bytes 5767168 | tf_op jit(solution)/shard_map/pallas_call | solution.py:71
  81.3 5.3 %collective-permute-start.3 = (f32[512,256]{1,0:T(8,128)}, f32[512,256]{1,0:T(8,128)S(1)}, u32[]{:S(2)}, u32[]{:S(2)}) collective-permute-start(f32[512,256]{1,0:T(8,128)} %get-tuple-element.34), channel_id=1, source_target_pairs={{0,1},{1,2},{2,3},{3,0},{4,5},{5,6},{6,7},{7,4},{8,9},{9,10},{10,1... | collective-permute-start | bytes 1572872 | tf_op jit(solution)/shard_map/ppermute | solution.py:31
  86.6 2.5 %bitcast_convert_fusion.rates_ref = f32[768,512]{1,0:T(8,128)} fusion(bf16[768,5,512]{2,0,1:T(8,128)(2,1)} %param.6), kind=kLoop, calls=%fused_computation.10 | loop fusion | flops 393216 | bytes 2359296 | tf_op jit(solution)/shard_map/convert_element_type | solution.py:67
  89.2 0.3 and.67
  89.4 2.6 %fusion.seen_ref = f32[768,512]{1,0:T(8,128)} fusion(pred[96,8,4,128]{3,2,1,0:T(4,128)(4,1)S(1)} %bitcast.69, bf16[768,5,512]{2,0,1:T(8,128)(2,1)} %param.6), kind=kLoop, calls=%fused_computation.1 | loop fusion | flops 1966080 | bytes 2752512 | tf_op jit(solution)/shard_map/convert_element_type | solution.py:66
  92.0 3.1 %collective-permute-done.3.items_ref = f32[512,256]{1,0:T(8,128)S(1)} collective-permute-done((f32[512,256]{1,0:T(8,128)}, f32[512,256]{1,0:T(8,128)S(1)}, u32[]{:S(2)}, u32[]{:S(2)}) %collective-permute-start.3) | collective-permute-done | bytes 524320 | tf_op jit(solution)/shard_map/ppermute | solution.py:31
  95.2 0.0 copy-start.3
  95.2 0.8 copy-done.3
  95.9 4.5 %shard_map.63 = (f32[768,256]{1,0:T(8,128)}, f32[512,256]{1,0:T(8,128)}) custom-call(f32[768,256]{1,0:T(8,128)} %get-tuple-element.33.users_ref, f32[512,256]{1,0:T(8,128)} %copy-done.3, f32[768,512]{1,0:T(8,128)} %bitcast_convert_fusion.rates_ref, f32[768,512]{1,0:T(8,128)} %fusion.seen_ref), custom_call_target="tpu_custom_call" | custom-call | flops 805306368 | bytes 5767168 | tf_op jit(solution)/shard_map/pallas_call | solution.py:71
  100.4 0.0 collective-permute-start.4
  100.4 14.2 %collective-permute-done.4 = f32[512,256]{1,0:T(8,128)S(1)} collective-permute-done((f32[512,256]{1,0:T(8,128)}, f32[512,256]{1,0:T(8,128)S(1)}, u32[]{:S(2)}, u32[]{:S(2)}) %collective-permute-start.4) | collective-permute-done | bytes 524320 | tf_op jit(solution)/shard_map/ppermute | solution.py:31
  114.7 0.8 copy.22
Async XLA Ops:
  11.4 21.6 %collective-permute-start = (f32[512,256]{1,0:T(8,128)}, f32[512,256]{1,0:T(8,128)S(1)}, u32[]{:S(2)}, u32[]{:S(2)}) collective-permute-start(f32[512,256]{1,0:T(8,128)} %get-tuple-element.22), channel_id=1, source_target_pairs={{0,4},{4,8},{8,12},{12,16},{16,20},{20,24},{24,28},{28,32},{32,36}... | collective-permute-start | bytes 1572872 | tf_op jit(solution)/shard_map/ppermute | solution.py:31
  33.0 0.8 copy-start
  38.3 16.7 %collective-permute-start.1 = (f32[512,256]{1,0:T(8,128)}, f32[512,256]{1,0:T(8,128)S(1)}, u32[]{:S(2)}, u32[]{:S(2)}) collective-permute-start(f32[512,256]{1,0:T(8,128)} %get-tuple-element.26), channel_id=1, source_target_pairs={{0,4},{4,8},{8,12},{12,16},{16,20},{20,24},{24,28},{28,32},{32,36}... | collective-permute-start | bytes 1572872 | tf_op jit(solution)/shard_map/ppermute | solution.py:31
  55.0 0.8 copy-start.1
  60.2 15.8 %collective-permute-start.2 = (f32[512,256]{1,0:T(8,128)}, f32[512,256]{1,0:T(8,128)S(1)}, u32[]{:S(2)}, u32[]{:S(2)}) collective-permute-start(f32[512,256]{1,0:T(8,128)} %get-tuple-element.30), channel_id=1, source_target_pairs={{0,4},{4,8},{8,12},{12,16},{16,20},{20,24},{24,28},{28,32},{32,36}... | collective-permute-start | bytes 1572872 | tf_op jit(solution)/shard_map/ppermute | solution.py:31
  76.1 0.8 copy-start.2
  81.3 13.8 %collective-permute-start.3 = (f32[512,256]{1,0:T(8,128)}, f32[512,256]{1,0:T(8,128)S(1)}, u32[]{:S(2)}, u32[]{:S(2)}) collective-permute-start(f32[512,256]{1,0:T(8,128)} %get-tuple-element.34), channel_id=1, source_target_pairs={{0,1},{1,2},{2,3},{3,0},{4,5},{5,6},{6,7},{7,4},{8,9},{9,10},{10,1... | collective-permute-start | bytes 1572872 | tf_op jit(solution)/shard_map/ppermute | solution.py:31
  95.2 0.8 copy-start.3
  100.4 14.2 %collective-permute-start.4 = (f32[512,256]{1,0:T(8,128)}, f32[512,256]{1,0:T(8,128)S(1)}, u32[]{:S(2)}, u32[]{:S(2)}) collective-permute-start(f32[512,256]{1,0:T(8,128)} %get-tuple-element.37), channel_id=1, source_target_pairs={{0,247},{1,244},{2,245},{3,246},{4,251},{5,248},{6,249},{7,250},{8... | collective-permute-start | bytes 1572872 | tf_op jit(solution)/shard_map/ppermute | solution.py:31

commit v6 on v5

--- a/solution.py
+++ b/solution.py
@@ -31,42 +31,42 @@
     return lax.ppermute(block, axes, route)
 
 
-def tile_kernel(user_rate, item_rate, users_ref, items_ref, rates_ref, seen_ref, users_out, items_out):
-    rates = rates_ref[...]
-    seen = seen_ref[...]
+def tile_kernel(user_rate, item_rate, users_ref, items_ref, rates_ref, users_out, items_out):
+    rates = rates_ref[...].astype(jnp.float32)
+    observed = rates != 0
     user_rows = users_ref[...]
     item_rows = items_ref[...]
     item_bf = item_rows.astype(jnp.bfloat16)
     user_bf = user_rows.astype(jnp.bfloat16)
     nt = (((1,), (1,)), ((), ()))
     predicted = lax.dot_general(user_bf, item_bf, nt, preferred_element_type=jnp.float32)
-    misfit = (jnp.clip(rates - predicted, -CLIP_LIMIT, CLIP_LIMIT) * seen).astype(jnp.bfloat16)
+    misfit = jnp.where(observed, jnp.clip(rates - predicted, -CLIP_LIMIT, CLIP_LIMIT), 0.0).astype(jnp.bfloat16)
     gradient = jnp.dot(misfit, item_bf, preferred_element_type=jnp.float32)
     user_rows = (1.0 - DECAY) * user_rows + user_rate * gradient
     users_out[...] = user_rows
     user_bf = user_rows.astype(jnp.bfloat16)
     predicted = lax.dot_general(user_bf, item_bf, nt, preferred_element_type=jnp.float32)
-    misfit = (jnp.clip(rates - predicted, -CLIP_LIMIT, CLIP_LIMIT) * seen).astype(jnp.bfloat16)
+    misfit = jnp.where(observed, jnp.clip(rates - predicted, -CLIP_LIMIT, CLIP_LIMIT), 0.0).astype(jnp.bfloat16)
     tn = (((0,), (0,)), ((), ()))
     gradient = lax.dot_general(misfit, user_bf, tn, preferred_element_type=jnp.float32)
     items_out[...] = (1.0 - DECAY) * item_rows + item_rate * gradient
 
 
-def expand(tile_rates, tile_flags):
+def mask_blocks(tile_rates, tile_flags):
     row_blocks, col_blocks = tile_flags.shape
     block_rows = tile_rates.shape[0] // row_blocks
     block_cols = tile_rates.shape[1] // col_blocks
-    nonzero = tile_rates.reshape(row_blocks, block_rows, col_blocks, block_cols) != 0
-    return (nonzero & (tile_flags[:, None, :, None] > 0)).reshape(tile_rates.shape)
+    blocks = tile_rates.reshape(row_blocks, block_rows, col_blocks, block_cols)
+    kept = jnp.where(tile_flags[:, None, :, None] > 0, blocks, jnp.zeros_like(blocks))
+    return kept.reshape(tile_rates.shape)
 
 
 def update_tile(user_rows, item_rows, tile_rates, tile_flags, user_rate, item_rate):
     rows, k = user_rows.shape
     cols = item_rows.shape[0]
-    seen = expand(tile_rates, tile_flags).astype(jnp.float32)
-    rates = tile_rates.astype(jnp.float32)
+    rates = mask_blocks(tile_rates, tile_flags)
     flops = 8 * rows * cols * k
-    nbytes = 2 * (rows * k * 4 + cols * k * 4) + 2 * rows * cols * 4
+    nbytes = 2 * (rows * k * 4 + cols * k * 4) + rows * cols * 2
     vmem = pl.BlockSpec(memory_space=pltpu.VMEM)
     return pl.pallas_call(
         functools.partial(tile_kernel, user_rate, item_rate),
@@ -74,10 +74,10 @@
             jax.ShapeDtypeStruct(user_rows.shape, jnp.float32),
             jax.ShapeDtypeStruct(item_rows.shape, jnp.float32),
         ),
-        in_specs=[vmem, vmem, vmem, vmem],
+        in_specs=[vmem, vmem, vmem],
         out_specs=(vmem, vmem),
         cost_estimate=pl.CostEstimate(flops=flops, bytes_accessed=nbytes, transcendentals=0),
-    )(user_rows, item_rows, rates, seen)
+    )(user_rows, item_rows, rates)
 
 
 def body(user_factors, item_factors, ratings, block_mask):

time: 116 us -> 110 us (0.948)
  other arithmetic: 26.4 us -> 11.9 us
  waiting for transfers between devices: 52.7 us -> 64.8 us
  Pallas kernels: 22.5 us -> 18.7 us
    convert_element_type x10 -> x0, other arithmetic: 25.6 us -> none  [the longest x5 13 us: update_tile(): seen = expand(tile_rates, tile_flags).astype(jnp.float32)]
    ppermute x5, waiting for transfers between devices: 52.7 us -> 64.8 us  [shift(): return lax.ppermute(block, axes, route)]
    select_n x0 -> x5, other arithmetic: none -> 11.2 us  [mask_blocks(): jnp.where(tile_flags[:, None, :, None] > 0, blocks, jnp.zeros_like(blocks))]
    pallas_call x5, Pallas kernels: 22.5 us -> 18.7 us  [update_tile(): pl.pallas_call(functools.partial(tile_kernel, user_rate, item_rate), out_...]
    broadcast_in_dim x0 -> x5, local copies, waits for them, and re-layouts: none -> 1.37 us  [mask_blocks(): jnp.where(tile_flags[:, None, :, None] > 0, blocks, jnp.zeros_like(blocks))]
    and x5 -> x0, local copies, waits for them, and re-layouts: 1.36 us -> none  [expand(): nonzero & (tile_flags[:, None, :, None] > 0)]
  transfers between devices with their start and end apart: 5 -> 5, of which waited for: 5 -> 5; matrix products, arithmetic and copies ran while one was open for 19% -> 10% of each run, Pallas kernels for 0% -> 0%
where the time goes in v6:
time: 110 us; the launch traced here: 109 us
  waiting for transfers between devices  64.8 us (59%)
  Pallas kernels  18.7 us (17%)
  other arithmetic  11.9 us (11%)
  starting transfers between devices  7.34 us (7%)
  local copies, waits for them, and re-layouts  5.87 us (5%)
    ppermute x5, waiting for transfers between devices, shift(): return lax.ppermute(block, axes, route)  64.8 us
    pallas_call x5, Pallas kernels, update_tile(): pl.pallas_call(functools.partial(tile_kernel, user_rate, item_rate), out_...  18.7 us
    select_n x5, other arithmetic, mask_blocks(): jnp.where(tile_flags[:, None, :, None] > 0, blocks, jnp.zeros_like(blocks))  11.2 us
    ppermute x5, starting transfers between devices, shift(): return lax.ppermute(block, axes, route)  7.34 us
    unnamed x9, local copies, waits for them, and re-layouts  3.96 us
  transfers between devices with their start and end apart: 5, of which 5 were waited for; matrix products, arithmetic and copies ran while one was open for 10% of the time, Pallas kernels for 0%

profile of v6, /device:TPU:1, one launch (start us, length us, event | category | flops | bytes accessed | tf_op | source)
XLA Modules:
  0.0 109.3 jit_solution(7358223244076493569)
XLA Ops:
  0.6 0.8 fusion.4
  1.4 0.1 copy.6
  1.5 0.3 broadcast_in_dim.38
  1.8 2.2 %bitcast_select_fusion.4.rates_ref = bf16[768,512]{1,0:T(8,128)(2,1)} fusion(pred[96,8,4,128]{3,2,1,0:T(4,128)(4,1)S(1)} %bitcast.40, bf16[768,5,512]{2,0,1:T(8,128)(2,1)} %param.6), kind=kLoop, calls=%fused_computation.4 | loop fusion | flops 393216 | bytes 1966080 | tf_op jit(solution)/shard_map/jit(_where)/select_n | solution.py:60
  4.0 3.7 %shard_map.59 = (f32[768,256]{1,0:T(8,128)}, f32[512,256]{1,0:T(8,128)}) custom-call(f32[768,256]{1,0:T(8,128)} %users_ref.1, f32[512,256]{1,0:T(8,128)} %items_ref.1, bf16[768,512]{1,0:T(8,128)(2,1)} %bitcast_select_fusion.4.rates_ref), custom_call_target="tpu_custom_call" | custom-call | flops 805306368 | bytes 3407872 | tf_op jit(solution)/shard_map/pallas_call | solution.py:71
  7.7 2.0 %collective-permute-start = (f32[512,256]{1,0:T(8,128)}, f32[512,256]{1,0:T(8,128)S(1)}, u32[]{:S(2)}, u32[]{:S(2)}) collective-permute-start(f32[512,256]{1,0:T(8,128)} %get-tuple-element.22), channel_id=1, source_target_pairs={{0,4},{4,8},{8,12},{12,16},{16,20},{20,24},{24,28},{28,32},{32,36}... | collective-permute-start | bytes 1572872 | tf_op jit(solution)/shard_map/ppermute | solution.py:31
  9.8 0.1 copy.7
  9.9 0.3 broadcast_in_dim.40
  10.1 2.2 %bitcast_select_fusion.3.rates_ref = bf16[768,512]{1,0:T(8,128)(2,1)} fusion(pred[96,8,4,128]{3,2,1,0:T(4,128)(4,1)S(1)} %bitcast.41, bf16[768,5,512]{2,0,1:T(8,128)(2,1)} %param.6), kind=kLoop, calls=%fused_computation.3 | loop fusion | flops 393216 | bytes 1966080 | tf_op jit(solution)/shard_map/jit(_where)/select_n | solution.py:60
  12.4 17.0 %collective-permute-done.items_ref = f32[512,256]{1,0:T(8,128)S(1)} collective-permute-done((f32[512,256]{1,0:T(8,128)}, f32[512,256]{1,0:T(8,128)S(1)}, u32[]{:S(2)}, u32[]{:S(2)}) %collective-permute-start) | collective-permute-done | bytes 524320 | tf_op jit(solution)/shard_map/ppermute | solution.py:31
  29.3 0.0 copy-start.1
  29.3 0.8 copy-done.1
  30.1 3.7 %shard_map.60 = (f32[768,256]{1,0:T(8,128)}, f32[512,256]{1,0:T(8,128)}) custom-call(f32[768,256]{1,0:T(8,128)} %get-tuple-element.21.users_ref, f32[512,256]{1,0:T(8,128)} %copy-done.1, bf16[768,512]{1,0:T(8,128)(2,1)} %bitcast_select_fusion.3.rates_ref), custom_call_target="tpu_custom_call" | custom-call | flops 805306368 | bytes 3407872 | tf_op jit(solution)/shard_map/pallas_call | solution.py:71
  33.9 0.0 collective-permute-start.1
  33.9 0.1 copy.8
  34.0 0.3 broadcast_in_dim.42
  34.3 2.2 %bitcast_select_fusion.2.rates_ref = bf16[768,512]{1,0:T(8,128)(2,1)} fusion(pred[96,8,4,128]{3,2,1,0:T(4,128)(4,1)S(1)} %bitcast.42, bf16[768,5,512]{2,0,1:T(8,128)(2,1)} %param.6), kind=kLoop, calls=%fused_computation.2 | loop fusion | flops 393216 | bytes 1966080 | tf_op jit(solution)/shard_map/jit(_where)/select_n | solution.py:60
  36.5 14.0 %collective-permute-done.1.items_ref = f32[512,256]{1,0:T(8,128)S(1)} collective-permute-done((f32[512,256]{1,0:T(8,128)}, f32[512,256]{1,0:T(8,128)S(1)}, u32[]{:S(2)}, u32[]{:S(2)}) %collective-permute-start.1) | collective-permute-done | bytes 524320 | tf_op jit(solution)/shard_map/ppermute | solution.py:31
  50.5 0.0 copy-start.2
  50.5 0.8 copy-done.2
  51.3 3.7 %shard_map.61 = (f32[768,256]{1,0:T(8,128)}, f32[512,256]{1,0:T(8,128)}) custom-call(f32[768,256]{1,0:T(8,128)} %get-tuple-element.25.users_ref, f32[512,256]{1,0:T(8,128)} %copy-done.2, bf16[768,512]{1,0:T(8,128)(2,1)} %bitcast_select_fusion.2.rates_ref), custom_call_target="tpu_custom_call" | custom-call | flops 805306368 | bytes 3407872 | tf_op jit(solution)/shard_map/pallas_call | solution.py:71
  55.1 0.0 collective-permute-start.2
  55.1 0.1 copy.9
  55.2 0.3 broadcast_in_dim.44
  55.4 2.2 %bitcast_select_fusion.1.rates_ref = bf16[768,512]{1,0:T(8,128)(2,1)} fusion(pred[96,8,4,128]{3,2,1,0:T(4,128)(4,1)S(1)} %bitcast.43, bf16[768,5,512]{2,0,1:T(8,128)(2,1)} %param.6), kind=kLoop, calls=%fused_computation.1 | loop fusion | flops 393216 | bytes 1966080 | tf_op jit(solution)/shard_map/jit(_where)/select_n | solution.py:60
  57.7 13.2 %collective-permute-done.2.items_ref = f32[512,256]{1,0:T(8,128)S(1)} collective-permute-done((f32[512,256]{1,0:T(8,128)}, f32[512,256]{1,0:T(8,128)S(1)}, u32[]{:S(2)}, u32[]{:S(2)}) %collective-permute-start.2) | collective-permute-done | bytes 524320 | tf_op jit(solution)/shard_map/ppermute | solution.py:31
  70.9 0.0 copy-start.3
  70.9 0.8 copy-done.3
  71.7 3.7 %shard_map.62 = (f32[768,256]{1,0:T(8,128)}, f32[512,256]{1,0:T(8,128)}) custom-call(f32[768,256]{1,0:T(8,128)} %get-tuple-element.29.users_ref, f32[512,256]{1,0:T(8,128)} %copy-done.3, bf16[768,512]{1,0:T(8,128)(2,1)} %bitcast_select_fusion.1.rates_ref), custom_call_target="tpu_custom_call" | custom-call | flops 805306368 | bytes 3407872 | tf_op jit(solution)/shard_map/pallas_call | solution.py:71
  75.4 5.3 %collective-permute-start.3 = (f32[512,256]{1,0:T(8,128)}, f32[512,256]{1,0:T(8,128)S(1)}, u32[]{:S(2)}, u32[]{:S(2)}) collective-permute-start(f32[512,256]{1,0:T(8,128)} %get-tuple-element.34), channel_id=1, source_target_pairs={{0,1},{1,2},{2,3},{3,0},{4,5},{5,6},{6,7},{7,4},{8,9},{9,10},{10,1... | collective-permute-start | bytes 1572872 | tf_op jit(solution)/shard_map/ppermute | solution.py:31
  80.7 0.1 copy.10
  80.8 0.3 broadcast_in_dim.46
  81.1 2.3 %bitcast_select_fusion.rates_ref = bf16[768,512]{1,0:T(8,128)(2,1)} fusion(pred[96,8,4,128]{3,2,1,0:T(4,128)(4,1)S(1)} %bitcast.44, bf16[768,5,512]{2,0,1:T(8,128)(2,1)} %param.6), kind=kLoop, calls=%fused_computation | loop fusion | flops 393216 | bytes 1966080 | tf_op jit(solution)/shard_map/jit(_where)/select_n | solution.py:60
  83.4 6.6 %collective-permute-done.3.items_ref = f32[512,256]{1,0:T(8,128)S(1)} collective-permute-done((f32[512,256]{1,0:T(8,128)}, f32[512,256]{1,0:T(8,128)S(1)}, u32[]{:S(2)}, u32[]{:S(2)}) %collective-permute-start.3) | collective-permute-done | bytes 524320 | tf_op jit(solution)/shard_map/ppermute | solution.py:31
  90.0 0.0 copy-start
  90.0 0.8 copy-done
  90.8 3.7 %shard_map.63 = (f32[768,256]{1,0:T(8,128)}, f32[512,256]{1,0:T(8,128)}) custom-call(f32[768,256]{1,0:T(8,128)} %get-tuple-element.33.users_ref, f32[512,256]{1,0:T(8,128)} %copy-done, bf16[768,512]{1,0:T(8,128)(2,1)} %bitcast_select_fusion.rates_ref), custom_call_target="tpu_custom_call" | custom-call | flops 805306368 | bytes 3407872 | tf_op jit(solution)/shard_map/pallas_call | solution.py:71
  94.5 0.0 collective-permute-start.4
  94.5 13.9 %collective-permute-done.4 = f32[512,256]{1,0:T(8,128)S(1)} collective-permute-done((f32[512,256]{1,0:T(8,128)}, f32[512,256]{1,0:T(8,128)S(1)}, u32[]{:S(2)}, u32[]{:S(2)}) %collective-permute-start.4) | collective-permute-done | bytes 524320 | tf_op jit(solution)/shard_map/ppermute | solution.py:31
  108.5 0.8 copy.22
Async XLA Ops:
  7.7 21.6 %collective-permute-start = (f32[512,256]{1,0:T(8,128)}, f32[512,256]{1,0:T(8,128)S(1)}, u32[]{:S(2)}, u32[]{:S(2)}) collective-permute-start(f32[512,256]{1,0:T(8,128)} %get-tuple-element.22), channel_id=1, source_target_pairs={{0,4},{4,8},{8,12},{12,16},{16,20},{20,24},{24,28},{28,32},{32,36}... | collective-permute-start | bytes 1572872 | tf_op jit(solution)/shard_map/ppermute | solution.py:31
  29.3 0.8 copy-start.1
  33.9 16.7 %collective-permute-start.1 = (f32[512,256]{1,0:T(8,128)}, f32[512,256]{1,0:T(8,128)S(1)}, u32[]{:S(2)}, u32[]{:S(2)}) collective-permute-start(f32[512,256]{1,0:T(8,128)} %get-tuple-element.26), channel_id=1, source_target_pairs={{0,4},{4,8},{8,12},{12,16},{16,20},{20,24},{24,28},{28,32},{32,36}... | collective-permute-start | bytes 1572872 | tf_op jit(solution)/shard_map/ppermute | solution.py:31
  50.5 0.8 copy-start.2
  55.1 15.8 %collective-permute-start.2 = (f32[512,256]{1,0:T(8,128)}, f32[512,256]{1,0:T(8,128)S(1)}, u32[]{:S(2)}, u32[]{:S(2)}) collective-permute-start(f32[512,256]{1,0:T(8,128)} %get-tuple-element.30), channel_id=1, source_target_pairs={{0,4},{4,8},{8,12},{12,16},{16,20},{20,24},{24,28},{28,32},{32,36}... | collective-permute-start | bytes 1572872 | tf_op jit(solution)/shard_map/ppermute | solution.py:31
  70.9 0.8 copy-start.3
  75.4 14.6 %collective-permute-start.3 = (f32[512,256]{1,0:T(8,128)}, f32[512,256]{1,0:T(8,128)S(1)}, u32[]{:S(2)}, u32[]{:S(2)}) collective-permute-start(f32[512,256]{1,0:T(8,128)} %get-tuple-element.34), channel_id=1, source_target_pairs={{0,1},{1,2},{2,3},{3,0},{4,5},{5,6},{6,7},{7,4},{8,9},{9,10},{10,1... | collective-permute-start | bytes 1572872 | tf_op jit(solution)/shard_map/ppermute | solution.py:31
  90.0 0.8 copy-start
  94.5 13.9 %collective-permute-start.4 = (f32[512,256]{1,0:T(8,128)}, f32[512,256]{1,0:T(8,128)S(1)}, u32[]{:S(2)}, u32[]{:S(2)}) collective-permute-start(f32[512,256]{1,0:T(8,128)} %get-tuple-element.37), channel_id=1, source_target_pairs={{0,247},{1,244},{2,245},{3,246},{4,251},{5,248},{6,249},{7,250},{8... | collective-permute-start | bytes 1572872 | tf_op jit(solution)/shard_map/ppermute | solution.py:31

commit v7 on v6

--- a/solution.py
+++ b/solution.py
@@ -31,10 +31,13 @@
     return lax.ppermute(block, axes, route)
 
 
-def tile_kernel(user_rate, item_rate, users_ref, items_ref, rates_ref, users_out, items_out):
+def tile_kernel(user_rate, item_rate, users_ref, items_hbm, rates_ref, users_out, items_out, items_ref, sem):
+    fetch = pltpu.make_async_copy(items_hbm, items_ref, sem)
+    fetch.start()
     rates = rates_ref[...].astype(jnp.float32)
     observed = rates != 0
     user_rows = users_ref[...]
+    fetch.wait()
     item_rows = items_ref[...]
     item_bf = item_rows.astype(jnp.bfloat16)
     user_bf = user_rows.astype(jnp.bfloat16)
@@ -74,9 +77,11 @@
             jax.ShapeDtypeStruct(user_rows.shape, jnp.float32),
             jax.ShapeDtypeStruct(item_rows.shape, jnp.float32),
         ),
-        in_specs=[vmem, vmem, vmem],
+        in_specs=[vmem, pl.BlockSpec(memory_space=pl.ANY), vmem],
         out_specs=(vmem, vmem),
+        scratch_shapes=[pltpu.VMEM(item_rows.shape, jnp.float32), pltpu.SemaphoreType.DMA],
         cost_estimate=pl.CostEstimate(flops=flops, bytes_accessed=nbytes, transcendentals=0),
+        compiler_params=pltpu.CompilerParams(vmem_limit_bytes=64 * 1024 * 1024),
     )(user_rows, item_rows, rates)
 
 

time: 110 us -> 113 us (1.027)
  Pallas kernels: 18.7 us -> 23.1 us
  waiting for transfers between devices: 64.8 us -> 62.2 us
    pallas_call x5, Pallas kernels: 18.7 us -> 23.1 us  [update_tile(): pl.pallas_call(functools.partial(tile_kernel, user_rate, item_rate), out_...]
    unnamed x9 -> x1, local copies, waits for them, and re-layouts: 3.96 us -> 0.79 us
    ppermute x5, waiting for transfers between devices: 64.8 us -> 62.2 us  [shift(): return lax.ppermute(block, axes, route)]
    gt x5, local copies, waits for them, and re-layouts: 0.54 us -> 3.04 us  [mask_blocks(): tile_flags[:, None, :, None] > 0]
  transfers between devices with their start and end apart: 5 -> 5, of which waited for: 5 -> 5; matrix products, arithmetic and copies ran while one was open for 10% -> 12% of each run, Pallas kernels for 0% -> 0%
where the time goes in v7:
time: 113 us; the launch traced here: 112 us
  waiting for transfers between devices  62.2 us (55%)
  Pallas kernels  23.1 us (20%)
  other arithmetic  12.5 us (11%)
  starting transfers between devices  7.93 us (7%)
  local copies, waits for them, and re-layouts  5.2 us (5%)
    ppermute x5, waiting for transfers between devices, shift(): return lax.ppermute(block, axes, route)  62.2 us
    pallas_call x5, Pallas kernels, update_tile(): pl.pallas_call(functools.partial(tile_kernel, user_rate, item_rate), out_...  23.1 us
    select_n x5, other arithmetic, mask_blocks(): jnp.where(tile_flags[:, None, :, None] > 0, blocks, jnp.zeros_like(blocks))  11.1 us
    ppermute x5, starting transfers between devices, shift(): return lax.ppermute(block, axes, route)  7.93 us
    gt x5, local copies, waits for them, and re-layouts, mask_blocks(): tile_flags[:, None, :, None] > 0  3.04 us
  transfers between devices with their start and end apart: 5, of which 5 were waited for; matrix products, arithmetic and copies ran while one was open for 12% of the time, Pallas kernels for 0%

profile of v7, /device:TPU:1, one launch (start us, length us, event | category | flops | bytes accessed | tf_op | source)
XLA Modules:
  0.0 111.7 jit_solution(11774623014689542883)
XLA Ops:
  0.6 1.3 %fusion.4 = (pred[6,4]{0,1:T(4,128)(4,1)}, pred[6,4]{0,1:T(4,128)(4,1)}, pred[6,4]{0,1:T(4,128)(4,1)}, pred[6,4]{0,1:T(4,128)(4,1)S(1)}, pred[6,4]{0,1:T(4,128)(4,1)}) fusion(s32[6,5,4]{0,2,1:T(4,128)} %param.7), kind=kLoop, calls=%fused_computation.14 | loop fusion | flops 120 | bytes 600 | tf_op jit(solution)/shard_map/gt | solution.py:63
  2.0 0.1 copy.6
  2.1 0.3 broadcast_in_dim.38
  2.4 2.2 %bitcast_select_fusion.4.rates_ref = bf16[768,512]{1,0:T(8,128)(2,1)} fusion(pred[96,8,4,128]{3,2,1,0:T(4,128)(4,1)S(1)} %bitcast.40, bf16[768,5,512]{2,0,1:T(8,128)(2,1)} %param.6), kind=kLoop, calls=%fused_computation.4 | loop fusion | flops 393216 | bytes 1966080 | tf_op jit(solution)/shard_map/jit(_where)/select_n | solution.py:63
  4.6 4.6 %shard_map.59 = (f32[768,256]{1,0:T(8,128)}, f32[512,256]{1,0:T(8,128)}) custom-call(f32[768,256]{1,0:T(8,128)} %users_ref.1, f32[512,256]{1,0:T(8,128)} %items_hbm.1, bf16[768,512]{1,0:T(8,128)(2,1)} %bitcast_select_fusion.4.rates_ref), custom_call_target="tpu_custom_call" | custom-call | flops 805306368 | bytes 3407872 | tf_op jit(solution)/shard_map/pallas_call | solution.py:74
  9.2 2.1 %collective-permute-start = (f32[512,256]{1,0:T(8,128)}, f32[512,256]{1,0:T(8,128)}, u32[]{:S(2)}, u32[]{:S(2)}) collective-permute-start(f32[512,256]{1,0:T(8,128)} %get-tuple-element.22), channel_id=1, source_target_pairs={{0,4},{4,8},{8,12},{12,16},{16,20},{20,24},{24,28},{28,32},{32,36}... | collective-permute-start | bytes 1572872 | tf_op jit(solution)/shard_map/ppermute | solution.py:31
  11.3 0.7 copy.7
  12.0 0.3 broadcast_in_dim.40
  12.3 2.2 %bitcast_select_fusion.3.rates_ref = bf16[768,512]{1,0:T(8,128)(2,1)} fusion(pred[96,8,4,128]{3,2,1,0:T(4,128)(4,1)S(1)} %bitcast.41, bf16[768,5,512]{2,0,1:T(8,128)(2,1)} %param.6), kind=kLoop, calls=%fused_computation.3 | loop fusion | flops 393216 | bytes 1966080 | tf_op jit(solution)/shard_map/jit(_where)/select_n | solution.py:63
  14.5 16.5 %collective-permute-done.items_hbm = f32[512,256]{1,0:T(8,128)} collective-permute-done((f32[512,256]{1,0:T(8,128)}, f32[512,256]{1,0:T(8,128)}, u32[]{:S(2)}, u32[]{:S(2)}) %collective-permute-start) | collective-permute-done | bytes 524320 | tf_op jit(solution)/shard_map/ppermute | solution.py:31
  31.0 4.6 %shard_map.60 = (f32[768,256]{1,0:T(8,128)}, f32[512,256]{1,0:T(8,128)}) custom-call(f32[768,256]{1,0:T(8,128)} %get-tuple-element.21.users_ref, f32[512,256]{1,0:T(8,128)} %collective-permute-done.items_hbm, bf16[768,512]{1,0:T(8,128)(2,1)} %bitcast_select_fusion.3.rates_ref), custom_call_target="tpu_custom_call" | custom-call | flops 805306368 | bytes 3407872 | tf_op jit(solution)/shard_map/pallas_call | solution.py:74
  35.6 0.1 collective-permute-start.1
  35.7 0.7 copy.8
  36.4 0.3 broadcast_in_dim.42
  36.7 2.2 %bitcast_select_fusion.2.rates_ref = bf16[768,512]{1,0:T(8,128)(2,1)} fusion(pred[96,8,4,128]{3,2,1,0:T(4,128)(4,1)S(1)} %bitcast.42, bf16[768,5,512]{2,0,1:T(8,128)(2,1)} %param.6), kind=kLoop, calls=%fused_computation.2 | loop fusion | flops 393216 | bytes 1966080 | tf_op jit(solution)/shard_map/jit(_where)/select_n | solution.py:63
  38.9 13.6 %collective-permute-done.1.items_hbm = f32[512,256]{1,0:T(8,128)} collective-permute-done((f32[512,256]{1,0:T(8,128)}, f32[512,256]{1,0:T(8,128)}, u32[]{:S(2)}, u32[]{:S(2)}) %collective-permute-start.1) | collective-permute-done | bytes 524320 | tf_op jit(solution)/shard_map/ppermute | solution.py:31
  52.5 4.6 %shard_map.61 = (f32[768,256]{1,0:T(8,128)}, f32[512,256]{1,0:T(8,128)}) custom-call(f32[768,256]{1,0:T(8,128)} %get-tuple-element.25.users_ref, f32[512,256]{1,0:T(8,128)} %collective-permute-done.1.items_hbm, bf16[768,512]{1,0:T(8,128)(2,1)} %bitcast_select_fusion.2.rates_ref), custom_call_target="tpu_custom_call" | custom-call | flops 805306368 | bytes 3407872 | tf_op jit(solution)/shard_map/pallas_call | solution.py:74
  57.1 0.1 collective-permute-start.2
  57.2 0.8 copy.9
  57.9 0.3 broadcast_in_dim.44
  58.2 2.2 %bitcast_select_fusion.1.rates_ref = bf16[768,512]{1,0:T(8,128)(2,1)} fusion(pred[96,8,4,128]{3,2,1,0:T(4,128)(4,1)S(1)} %bitcast.43, bf16[768,5,512]{2,0,1:T(8,128)(2,1)} %param.6), kind=kLoop, calls=%fused_computation.1 | loop fusion | flops 393216 | bytes 1966080 | tf_op jit(solution)/shard_map/jit(_where)/select_n | solution.py:63
  60.5 12.6 %collective-permute-done.2.items_hbm = f32[512,256]{1,0:T(8,128)} collective-permute-done((f32[512,256]{1,0:T(8,128)}, f32[512,256]{1,0:T(8,128)}, u32[]{:S(2)}, u32[]{:S(2)}) %collective-permute-start.2) | collective-permute-done | bytes 524320 | tf_op jit(solution)/shard_map/ppermute | solution.py:31
  73.1 4.6 %shard_map.62 = (f32[768,256]{1,0:T(8,128)}, f32[512,256]{1,0:T(8,128)}) custom-call(f32[768,256]{1,0:T(8,128)} %get-tuple-element.29.users_ref, f32[512,256]{1,0:T(8,128)} %collective-permute-done.2.items_hbm, bf16[768,512]{1,0:T(8,128)(2,1)} %bitcast_select_fusion.1.rates_ref), custom_call_target="tpu_custom_call" | custom-call | flops 805306368 | bytes 3407872 | tf_op jit(solution)/shard_map/pallas_call | solution.py:74
  77.7 5.6 %collective-permute-start.3 = (f32[512,256]{1,0:T(8,128)}, f32[512,256]{1,0:T(8,128)}, u32[]{:S(2)}, u32[]{:S(2)}) collective-permute-start(f32[512,256]{1,0:T(8,128)} %get-tuple-element.34), channel_id=1, source_target_pairs={{0,1},{1,2},{2,3},{3,0},{4,5},{5,6},{6,7},{7,4},{8,9},{9,10},{10,1... | collective-permute-start | bytes 1572872 | tf_op jit(solution)/shard_map/ppermute | solution.py:31
  83.3 0.8 copy.10
  84.0 0.3 broadcast_in_dim.46
  84.3 2.3 %bitcast_select_fusion.rates_ref = bf16[768,512]{1,0:T(8,128)(2,1)} fusion(pred[96,8,4,128]{3,2,1,0:T(4,128)(4,1)S(1)} %bitcast.44, bf16[768,5,512]{2,0,1:T(8,128)(2,1)} %param.6), kind=kLoop, calls=%fused_computation | loop fusion | flops 393216 | bytes 1966080 | tf_op jit(solution)/shard_map/jit(_where)/select_n | solution.py:63
  86.6 5.8 %collective-permute-done.3.items_hbm = f32[512,256]{1,0:T(8,128)} collective-permute-done((f32[512,256]{1,0:T(8,128)}, f32[512,256]{1,0:T(8,128)}, u32[]{:S(2)}, u32[]{:S(2)}) %collective-permute-start.3) | collective-permute-done | bytes 524320 | tf_op jit(solution)/shard_map/ppermute | solution.py:31
  92.4 4.6 %shard_map.63 = (f32[768,256]{1,0:T(8,128)}, f32[512,256]{1,0:T(8,128)}) custom-call(f32[768,256]{1,0:T(8,128)} %get-tuple-element.33.users_ref, f32[512,256]{1,0:T(8,128)} %collective-permute-done.3.items_hbm, bf16[768,512]{1,0:T(8,128)(2,1)} %bitcast_select_fusion.rates_ref), custom_call_target="tpu_custom_call" | custom-call | flops 805306368 | bytes 3407872 | tf_op jit(solution)/shard_map/pallas_call | solution.py:74
  97.0 0.1 collective-permute-start.4
  97.1 13.8 %collective-permute-done.4 = f32[512,256]{1,0:T(8,128)S(1)} collective-permute-done((f32[512,256]{1,0:T(8,128)}, f32[512,256]{1,0:T(8,128)S(1)}, u32[]{:S(2)}, u32[]{:S(2)}) %collective-permute-start.4) | collective-permute-done | bytes 524320 | tf_op jit(solution)/shard_map/ppermute | solution.py:31
  110.9 0.8 copy.22
Async XLA Ops:
  9.2 21.8 %collective-permute-start = (f32[512,256]{1,0:T(8,128)}, f32[512,256]{1,0:T(8,128)}, u32[]{:S(2)}, u32[]{:S(2)}) collective-permute-start(f32[512,256]{1,0:T(8,128)} %get-tuple-element.22), channel_id=1, source_target_pairs={{0,4},{4,8},{8,12},{12,16},{16,20},{20,24},{24,28},{28,32},{32,36}... | collective-permute-start | bytes 1572872 | tf_op jit(solution)/shard_map/ppermute | solution.py:31
  35.6 16.8 %collective-permute-start.1 = (f32[512,256]{1,0:T(8,128)}, f32[512,256]{1,0:T(8,128)}, u32[]{:S(2)}, u32[]{:S(2)}) collective-permute-start(f32[512,256]{1,0:T(8,128)} %get-tuple-element.26), channel_id=1, source_target_pairs={{0,4},{4,8},{8,12},{12,16},{16,20},{20,24},{24,28},{28,32},{32,36}... | collective-permute-start | bytes 1572872 | tf_op jit(solution)/shard_map/ppermute | solution.py:31
  57.1 16.0 %collective-permute-start.2 = (f32[512,256]{1,0:T(8,128)}, f32[512,256]{1,0:T(8,128)}, u32[]{:S(2)}, u32[]{:S(2)}) collective-permute-start(f32[512,256]{1,0:T(8,128)} %get-tuple-element.30), channel_id=1, source_target_pairs={{0,4},{4,8},{8,12},{12,16},{16,20},{20,24},{24,28},{28,32},{32,36}... | collective-permute-start | bytes 1572872 | tf_op jit(solution)/shard_map/ppermute | solution.py:31
  77.7 14.7 %collective-permute-start.3 = (f32[512,256]{1,0:T(8,128)}, f32[512,256]{1,0:T(8,128)}, u32[]{:S(2)}, u32[]{:S(2)}) collective-permute-start(f32[512,256]{1,0:T(8,128)} %get-tuple-element.34), channel_id=1, source_target_pairs={{0,1},{1,2},{2,3},{3,0},{4,5},{5,6},{6,7},{7,4},{8,9},{9,10},{10,1... | collective-permute-start | bytes 1572872 | tf_op jit(solution)/shard_map/ppermute | solution.py:31
  97.0 13.9 %collective-permute-start.4 = (f32[512,256]{1,0:T(8,128)}, f32[512,256]{1,0:T(8,128)S(1)}, u32[]{:S(2)}, u32[]{:S(2)}) collective-permute-start(f32[512,256]{1,0:T(8,128)} %get-tuple-element.37), channel_id=1, source_target_pairs={{0,247},{1,244},{2,245},{3,246},{4,251},{5,248},{6,249},{7,250},{8... | collective-permute-start | bytes 1572872 | tf_op jit(solution)/shard_map/ppermute | solution.py:31

commit v8 on v6

v8 whole, which is shorter than its diff:
```python
import functools

import jax
import jax.numpy as jnp
from jax import lax
from jax.experimental import pallas as pl
from jax.experimental.pallas import tpu as pltpu
from jax.sharding import PartitionSpec as P


CLIP_LIMIT = 3.0
DECAY = 0.03
RATE = 4.0


def shift(block, axes, sizes, offsets):
    total = 1
    for size in sizes:
        total *= size
    route = []
    for src in range(total):
        coords = []
        rem = src
        for size in reversed(sizes):
            coords.append(rem % size)
            rem //= size
        coords = coords[::-1]
        dst = 0
        for c, size, off in zip(coords, sizes, offsets):
            dst = dst * size + (c + off) % size
        route.append((src, dst))
    return lax.ppermute(block, axes, route)


NT = (((1,), (1,)), ((), ()))
TN = (((0,), (0,)), ((), ()))


def misfit_of(user_bf, item_bf, rates):
    predicted = lax.dot_general(user_bf, item_bf, NT, preferred_element_type=jnp.float32)
    misfit = jnp.where(rates != 0, jnp.clip(rates - predicted, -CLIP_LIMIT, CLIP_LIMIT), 0.0)
    return misfit.astype(jnp.bfloat16)


def user_part(users_ref, items_ref, rates_ref):
    item_bf = items_ref[...].astype(jnp.bfloat16)
    user_bf = users_ref[...].astype(jnp.bfloat16)
    misfit = misfit_of(user_bf, item_bf, rates_ref[...].astype(jnp.float32))
    return jnp.dot(misfit, item_bf, preferred_element_type=jnp.float32)


def item_part(item_rate, user_bf, items_ref, rates_ref):
    item_rows = items_ref[...]
    misfit = misfit_of(user_bf, item_rows.astype(jnp.bfloat16), rates_ref[...].astype(jnp.float32))
    gradient = lax.dot_general(misfit, user_bf, TN, preferred_element_type=jnp.float32)
    return (1.0 - DECAY) * item_rows + item_rate * gradient


def first_kernel(users_ref, items_ref, rates_ref, partial_out):
    partial_out[...] = user_part(users_ref, items_ref, rates_ref)


def middle_kernel(user_rate, item_rate, users_ref, partial_ref, items1_ref, rates1_ref, items0_ref, rates0_ref,
                  users_out, items0_out):
    gradient = partial_ref[...] + user_part(users_ref, items1_ref, rates1_ref)
    user_rows = (1.0 - DECAY) * users_ref[...] + user_rate * gradient
    users_out[...] = user_rows
    items0_out[...] = item_part(item_rate, user_rows.astype(jnp.bfloat16), items0_ref, rates0_ref)


def last_kernel(item_rate, users_ref, items_ref, rates_ref, items_out):
    items_out[...] = item_part(item_rate, users_ref[...].astype(jnp.bfloat16), items_ref, rates_ref)


def call(kernel, outs, args, flops):
    vmem = pl.BlockSpec(memory_space=pltpu.VMEM)
    nbytes = sum(a.size * a.dtype.itemsize for a in args) + sum(o.size * o.dtype.itemsize for o in outs)
    return pl.pallas_call(
        kernel,
        out_shape=tuple(outs),
        in_specs=[vmem] * len(args),
        out_specs=tuple([vmem] * len(outs)),
        cost_estimate=pl.CostEstimate(flops=flops, bytes_accessed=nbytes, transcendentals=0),
    )(*args)


def mask_blocks(tile_rates, tile_flags):
    row_blocks, col_blocks = tile_flags.shape
    block_rows = tile_rates.shape[0] // row_blocks
    block_cols = tile_rates.shape[1] // col_blocks
    blocks = tile_rates.reshape(row_blocks, block_rows, col_blocks, block_cols)
    kept = jnp.where(tile_flags[:, None, :, None] > 0, blocks, jnp.zeros_like(blocks))
    return kept.reshape(tile_rates.shape)


def body(user_factors, item_factors, ratings, block_mask):
    row_count, k = user_factors.shape
    item_count = item_factors.shape[0]
    strata = ratings.shape[1]
    user_rate = RATE / item_count
    item_rate = RATE / row_count
    n_blk = lax.axis_size("blk")
    n_hop = lax.axis_size("hop")
    half = item_count // 2
    user_rows = user_factors
    chunks = [item_factors[:half], item_factors[half:]]
    users_t = jax.ShapeDtypeStruct(user_factors.shape, jnp.float32)
    chunk_t = jax.ShapeDtypeStruct((half, k), jnp.float32)
    unit = 2 * row_count * half * k
    for stratum in range(strata):
      rates_src = ratings
      if stratum > 0:
          rates_src, user_rows = lax.optimization_barrier((ratings, user_rows))
      rates = mask_blocks(rates_src[:, stratum, :], block_mask[:, stratum, :])
      rates0, rates1 = rates[:, :half], rates[:, half:]
      (partial,) = call(first_kernel, [users_t], [user_rows, chunks[0], rates0], 2 * unit)
      user_rows, new0 = call(
          functools.partial(middle_kernel, user_rate, item_rate),
          [users_t, chunk_t],
          [user_rows, partial, chunks[1], rates1, chunks[0], rates0],
          4 * unit,
      )
      if stratum < strata - 2:
          move = functools.partial(shift, axes="blk", sizes=(n_blk,), offsets=(1,))
      elif stratum == strata - 2:
          move = functools.partial(shift, axes="hop", sizes=(n_hop,), offsets=(1,))
      else:
          move = functools.partial(shift, axes=("blk", "hop"), sizes=(n_blk, n_hop), offsets=(-(strata - 2), -1))
      new0 = move(new0)
      (new1,) = call(functools.partial(last_kernel, item_rate), [chunk_t], [user_rows, chunks[1], rates1], 2 * unit)
      new1 = move(new1)
      chunks = [new0, new1]
    return (user_rows, jnp.concatenate(chunks, axis=0))


def solution(mesh):
    in_specs = (
        P(("blk", "hop"), None),
        P(("blk", "hop"), None),
        P(("blk", "hop"), None, None),
        P(("blk", "hop"), None, None),
    )
    out_specs = (P(("blk", "hop"), None), P(("blk", "hop"), None))
    return jax.shard_map(body, mesh=mesh, in_specs=in_specs, out_specs=out_specs, check_vma=False)
```

time: 110 us -> 131 us (1.19)
  Pallas kernels: 18.7 us -> 43.8 us
  waiting for transfers between devices: 64.8 us -> 55.3 us
  local copies, waits for them, and re-layouts: 5.87 us -> 13.2 us
  other arithmetic: 11.9 us -> 8.35 us
    pallas_call x5 -> x15, Pallas kernels: 18.7 us -> 43.8 us  [call(): pl.pallas_call(kernel, out_shape=tuple(outs), in_specs=[vmem] * len(args)...]
    ppermute x5 -> x10, waiting for transfers between devices: 64.8 us -> 55.3 us  [shift(): return lax.ppermute(block, axes, route)]
    slice x0 -> x6, local copies, waits for them, and re-layouts: none -> 5.61 us  [the longest x5 4.78 us: body(): rates0, rates1 = (rates[:, :half], rates[:, half:])]
    select_n x5, other arithmetic: 11.2 us -> 6.71 us  [mask_blocks(): jnp.where(tile_flags[:, None, :, None] > 0, blocks, jnp.zeros_like(blocks))]
    unnamed x9 -> x18, local copies, waits for them, and re-layouts: 3.96 us -> 5.7 us
    ppermute x5 -> x10, starting transfers between devices: 7.34 us -> 8.63 us  [shift(): return lax.ppermute(block, axes, route)]
  transfers between devices with their start and end apart: 5 -> 10, of which waited for: 5 -> 7; matrix products, arithmetic and copies ran while one was open for 10% -> 8% of each run, Pallas kernels for 0% -> 10%
where the time goes in v8:
time: 131 us; the launch traced here: 130 us
  waiting for transfers between devices  55.3 us (42%)
  Pallas kernels  43.8 us (33%)
  local copies, waits for them, and re-layouts  13.2 us (10%)
  starting transfers between devices  8.63 us (7%)
  other arithmetic  8.35 us (6%)
    ppermute x10, waiting for transfers between devices, shift(): return lax.ppermute(block, axes, route)  55.3 us
    pallas_call x15, Pallas kernels, call(): pl.pallas_call(kernel, out_shape=tuple(outs), in_specs=[vmem] * len(args)...  43.8 us
    ppermute x10, starting transfers between devices, shift(): return lax.ppermute(block, axes, route)  8.63 us
    select_n x5, other arithmetic, mask_blocks(): jnp.where(tile_flags[:, None, :, None] > 0, blocks, jnp.zeros_like(blocks))  6.71 us
    unnamed x18, local copies, waits for them, and re-layouts  5.7 us
    slice x5, local copies, waits for them, and re-layouts, body(): rates0, rates1 = (rates[:, :half], rates[:, half:])  4.78 us
  transfers between devices with their start and end apart: 10, of which 7 were waited for; matrix products, arithmetic and copies ran while one was open for 8% of the time, Pallas kernels for 10%

profile of v8, /device:TPU:1, one launch (start us, length us, event | category | flops | bytes accessed | tf_op | source)
XLA Modules:
  0.0 129.9 jit_solution(6515908048909256234)
XLA Ops:
  0.6 0.8 fusion.4
  1.5 0.1 copy.6
  1.6 0.3 broadcast_in_dim.38
  1.8 1.3 %bitcast_select_fusion.4 = bf16[768,512]{1,0:T(8,128)(2,1)S(1)} fusion(pred[96,8,4,128]{3,2,1,0:T(4,128)(4,1)S(1)} %bitcast.40, bf16[768,5,512]{2,0,1:T(8,128)(2,1)} %param.6), kind=kLoop, calls=%fused_computation.4 | loop fusion | flops 393216 | bytes 1966080 | tf_op jit(solution)/shard_map/jit(_where)/select_n | solution.py:92
  3.2 0.9 fusion.9
  4.1 0.8 fusion.10
  5.0 2.7 %shard_map.59.partial_ref = f32[768,256]{1,0:T(8,128)} custom-call(f32[768,256]{1,0:T(8,128)} %users_ref.3, f32[256,256]{1,0:T(8,128)} %get-tuple-element.49.items_ref.items0_ref, bf16[768,256]{1,0:T(8,128)(2,1)} %get-tuple-element.47.rates_ref.rates0_ref), custom_call_target="tpu_custom_call" | custom-call | flops 201326592 | bytes 2228224 | tf_op jit(solution)/shard_map/pallas_call | solution.py:78
  7.7 3.4 %shard_map.60 = (f32[768,256]{1,0:T(8,128)}, f32[256,256]{1,0:T(8,128)}) custom-call(f32[768,256]{1,0:T(8,128)} %users_ref.3, f32[768,256]{1,0:T(8,128)} %shard_map.59.partial_ref, f32[256,256]{1,0:T(8,128)} %get-tuple-element.48.items1_ref.items_ref, bf16[768,256]{1,0:T(8,128)(2,1)} %get-tuple-element.46.rates1_ref.rates_ref, ...), custom_call_target="tpu_custom_call" | custom-call | flops 402653184 | bytes 3932160 | tf_op jit(solution)/shard_map/pallas_call | solution.py:78
  11.1 2.0 %collective-permute-start = (f32[256,256]{1,0:T(8,128)}, f32[256,256]{1,0:T(8,128)S(1)}, u32[]{:S(2)}, u32[]{:S(2)}) collective-permute-start(f32[256,256]{1,0:T(8,128)} %get-tuple-element.22), channel_id=1, source_target_pairs={{0,4},{4,8},{8,12},{12,16},{16,20},{20,24},{24,28},{28,32},{32,36}... | collective-permute-start | bytes 786440 | tf_op jit(solution)/shard_map/ppermute | solution.py:32
  13.1 2.6 %shard_map.62 = f32[256,256]{1,0:T(8,128)} custom-call(f32[768,256]{1,0:T(8,128)} %get-tuple-element.21.users_ref, f32[256,256]{1,0:T(8,128)} %get-tuple-element.48.items1_ref.items_ref, bf16[768,256]{1,0:T(8,128)(2,1)} %get-tuple-element.46.rates1_ref.rates_ref), custom_call_target="tpu_custom_call" | custom-call | flops 201326592 | bytes 1703936 | tf_op jit(solution)/shard_map/pallas_call | solution.py:78
  15.7 1.3 collective-permute-start.1
  17.0 0.1 copy.7
  17.1 0.3 broadcast_in_dim.40
  17.4 1.3 %bitcast_select_fusion.3 = bf16[768,512]{1,0:T(8,128)(2,1)S(1)} fusion(pred[96,8,4,128]{3,2,1,0:T(4,128)(4,1)S(1)} %bitcast.41, bf16[768,5,512]{2,0,1:T(8,128)(2,1)} %param.6), kind=kLoop, calls=%fused_computation.3 | loop fusion | flops 393216 | bytes 1966080 | tf_op jit(solution)/shard_map/jit(_where)/select_n | solution.py:92
  18.7 0.1 copy.8
  18.8 0.1 copy.9
  18.9 0.1 copy.10
  19.1 1.0 fusion.8
  20.0 7.0 %collective-permute-done.items_ref.items0_ref = f32[256,256]{1,0:T(8,128)S(1)} collective-permute-done((f32[256,256]{1,0:T(8,128)}, f32[256,256]{1,0:T(8,128)S(1)}, u32[]{:S(2)}, u32[]{:S(2)}) %collective-permute-start) | collective-permute-done | bytes 262176 | tf_op jit(solution)/shard_map/ppermute | solution.py:32
  27.1 0.7 copy-done
  27.8 2.7 %shard_map.61.partial_ref = f32[768,256]{1,0:T(8,128)} custom-call(f32[768,256]{1,0:T(8,128)} %get-tuple-element.21.users_ref, f32[256,256]{1,0:T(8,128)} %copy-done, bf16[768,256]{1,0:T(8,128)(2,1)} %get-tuple-element.45.rates_ref.rates0_ref), custom_call_target="tpu_custom_call" | custom-call | flops 201326592 | bytes 2228224 | tf_op jit(solution)/shard_map/pallas_call | solution.py:78
  30.5 2.2 %collective-permute-done.1.items1_ref.items_ref = f32[256,256]{1,0:T(8,128)S(1)} collective-permute-done((f32[256,256]{1,0:T(8,128)}, f32[256,256]{1,0:T(8,128)S(1)}, u32[]{:S(2)}, u32[]{:S(2)}) %collective-permute-start.1) | collective-permute-done | bytes 262176 | tf_op jit(solution)/shard_map/ppermute | solution.py:32
  32.7 0.7 copy-done.4
  33.4 3.4 %shard_map.63 = (f32[768,256]{1,0:T(8,128)}, f32[256,256]{1,0:T(8,128)}) custom-call(f32[768,256]{1,0:T(8,128)} %get-tuple-element.21.users_ref, f32[768,256]{1,0:T(8,128)} %shard_map.61.partial_ref, f32[256,256]{1,0:T(8,128)} %copy-done.4, bf16[768,256]{1,0:T(8,128)(2,1)} %get-tuple-element.44.rates1_ref.rates_ref, f32[256,256]{1,0:T(8,128)} %copy-done, ...), custom_call_target="tpu_custom_call" | custom-call | flops 402653184 | bytes 3932160 | tf_op jit(solution)/shard_map/pallas_call | solution.py:78
  36.8 2.6 %shard_map.65 = f32[256,256]{1,0:T(8,128)} custom-call(f32[768,256]{1,0:T(8,128)} %get-tuple-element.25.users_ref, f32[256,256]{1,0:T(8,128)} %copy-done.4, bf16[768,256]{1,0:T(8,128)(2,1)} %get-tuple-element.44.rates1_ref.rates_ref), custom_call_target="tpu_custom_call" | custom-call | flops 201326592 | bytes 1703936 | tf_op jit(solution)/shard_map/pallas_call | solution.py:78
  39.5 0.0 collective-permute-start.3
  39.5 0.3 broadcast_in_dim.42
  39.7 1.3 %bitcast_select_fusion.2 = bf16[768,512]{1,0:T(8,128)(2,1)S(1)} fusion(pred[96,8,4,128]{3,2,1,0:T(4,128)(4,1)S(1)} %bitcast.42, bf16[768,5,512]{2,0,1:T(8,128)(2,1)} %param.6), kind=kLoop, calls=%fused_computation.2 | loop fusion | flops 393216 | bytes 1966080 | tf_op jit(solution)/shard_map/jit(_where)/select_n | solution.py:92
  41.1 1.0 fusion.7
  42.1 14.1 %collective-permute-done.2.items_ref.items0_ref = f32[256,256]{1,0:T(8,128)S(1)} collective-permute-done((f32[256,256]{1,0:T(8,128)}, f32[256,256]{1,0:T(8,128)S(1)}, u32[]{:S(2)}, u32[]{:S(2)}) %collective-permute-start.2) | collective-permute-done | bytes 262176 | tf_op jit(solution)/shard_map/ppermute | solution.py:32
  56.1 0.7 copy-done.1
  56.8 2.7 %shard_map.64.partial_ref = f32[768,256]{1,0:T(8,128)} custom-call(f32[768,256]{1,0:T(8,128)} %get-tuple-element.25.users_ref, f32[256,256]{1,0:T(8,128)} %copy-done.1, bf16[768,256]{1,0:T(8,128)(2,1)} %get-tuple-element.43.rates_ref.rates0_ref), custom_call_target="tpu_custom_call" | custom-call | flops 201326592 | bytes 2228224 | tf_op jit(solution)/shard_map/pallas_call | solution.py:78
  59.5 0.0 collective-permute-done.3.items1_ref.items_ref
  59.5 0.7 copy-done.5
  60.3 3.4 %shard_map.66 = (f32[768,256]{1,0:T(8,128)}, f32[256,256]{1,0:T(8,128)}) custom-call(f32[768,256]{1,0:T(8,128)} %get-tuple-element.25.users_ref, f32[768,256]{1,0:T(8,128)} %shard_map.64.partial_ref, f32[256,256]{1,0:T(8,128)} %copy-done.5, bf16[768,256]{1,0:T(8,128)(2,1)} %get-tuple-element.42.rates1_ref.rates_ref, f32[256,256]{1,0:T(8,128)} %copy-done.1, ...), custom_call_target="tpu_custom_call" | custom-call | flops 402653184 | bytes 3932160 | tf_op jit(solution)/shard_map/pallas_call | solution.py:78
  63.7 2.6 %shard_map.68 = f32[256,256]{1,0:T(8,128)} custom-call(f32[768,256]{1,0:T(8,128)} %get-tuple-element.29.users_ref, f32[256,256]{1,0:T(8,128)} %copy-done.5, bf16[768,256]{1,0:T(8,128)(2,1)} %get-tuple-element.42.rates1_ref.rates_ref), custom_call_target="tpu_custom_call" | custom-call | flops 201326592 | bytes 1703936 | tf_op jit(solution)/shard_map/pallas_call | solution.py:78
  66.3 0.0 collective-permute-start.4
  66.3 0.3 broadcast_in_dim.44
  66.6 1.3 %bitcast_select_fusion.1 = bf16[768,512]{1,0:T(8,128)(2,1)S(1)} fusion(pred[96,8,4,128]{3,2,1,0:T(4,128)(4,1)S(1)} %bitcast.43, bf16[768,5,512]{2,0,1:T(8,128)(2,1)} %param.6), kind=kLoop, calls=%fused_computation.1 | loop fusion | flops 393216 | bytes 1966080 | tf_op jit(solution)/shard_map/jit(_where)/select_n | solution.py:92
  67.9 1.0 fusion.6
  68.9 13.2 %collective-permute-done.4.items_ref.items0_ref = f32[256,256]{1,0:T(8,128)S(1)} collective-permute-done((f32[256,256]{1,0:T(8,128)}, f32[256,256]{1,0:T(8,128)S(1)}, u32[]{:S(2)}, u32[]{:S(2)}) %collective-permute-start.4) | collective-permute-done | bytes 262176 | tf_op jit(solution)/shard_map/ppermute | solution.py:32
  82.1 0.7 copy-done.2
  82.8 2.7 %shard_map.67.partial_ref = f32[768,256]{1,0:T(8,128)} custom-call(f32[768,256]{1,0:T(8,128)} %get-tuple-element.29.users_ref, f32[256,256]{1,0:T(8,128)} %copy-done.2, bf16[768,256]{1,0:T(8,128)(2,1)} %get-tuple-element.41.rates_ref.rates0_ref), custom_call_target="tpu_custom_call" | custom-call | flops 201326592 | bytes 2228224 | tf_op jit(solution)/shard_map/pallas_call | solution.py:78
  85.5 0.0 collective-permute-done.5.items1_ref.items_ref
  85.5 0.7 copy-done.6
  86.2 3.4 %shard_map.69 = (f32[768,256]{1,0:T(8,128)}, f32[256,256]{1,0:T(8,128)}) custom-call(f32[768,256]{1,0:T(8,128)} %get-tuple-element.29.users_ref, f32[768,256]{1,0:T(8,128)} %shard_map.67.partial_ref, f32[256,256]{1,0:T(8,128)} %copy-done.6, bf16[768,256]{1,0:T(8,128)(2,1)} %get-tuple-element.40.rates1_ref.rates_ref, f32[256,256]{1,0:T(8,128)} %copy-done.2, ...), custom_call_target="tpu_custom_call" | custom-call | flops 402653184 | bytes 3932160 | tf_op jit(solution)/shard_map/pallas_call | solution.py:78
  89.6 2.6 %shard_map.71 = f32[256,256]{1,0:T(8,128)} custom-call(f32[768,256]{1,0:T(8,128)} %get-tuple-element.33.users_ref, f32[256,256]{1,0:T(8,128)} %copy-done.6, bf16[768,256]{1,0:T(8,128)(2,1)} %get-tuple-element.40.rates1_ref.rates_ref), custom_call_target="tpu_custom_call" | custom-call | flops 201326592 | bytes 1703936 | tf_op jit(solution)/shard_map/pallas_call | solution.py:78
  92.3 5.3 %collective-permute-start.7 = (f32[256,256]{1,0:T(8,128)}, f32[256,256]{1,0:T(8,128)S(1)}, u32[]{:S(2)}, u32[]{:S(2)}) collective-permute-start(f32[256,256]{1,0:T(8,128)} %shard_map.71), channel_id=1, source_target_pairs={{0,1},{1,2},{2,3},{3,0},{4,5},{5,6},{6,7},{7,4},{8,9},{9,10},{10,1... | collective-permute-start | bytes 786440 | tf_op jit(solution)/shard_map/ppermute | solution.py:32
  97.6 0.0 collective-permute-start.6
  97.6 0.3 broadcast_in_dim.46
  97.9 1.3 %bitcast_select_fusion = bf16[768,512]{1,0:T(8,128)(2,1)S(1)} fusion(pred[96,8,4,128]{3,2,1,0:T(4,128)(4,1)S(1)} %bitcast.44, bf16[768,5,512]{2,0,1:T(8,128)(2,1)} %param.6), kind=kLoop, calls=%fused_computation | loop fusion | flops 393216 | bytes 1966080 | tf_op jit(solution)/shard_map/jit(_where)/select_n | solution.py:92
  99.2 1.0 fusion.5
  100.2 3.8 %collective-permute-done.6.items_ref.items0_ref = f32[256,256]{1,0:T(8,128)S(1)} collective-permute-done((f32[256,256]{1,0:T(8,128)}, f32[256,256]{1,0:T(8,128)S(1)}, u32[]{:S(2)}, u32[]{:S(2)}) %collective-permute-start.6) | collective-permute-done | bytes 262176 | tf_op jit(solution)/shard_map/ppermute | solution.py:32
  104.0 0.7 copy-done.3
  104.7 2.8 %shard_map.70.partial_ref = f32[768,256]{1,0:T(8,128)} custom-call(f32[768,256]{1,0:T(8,128)} %get-tuple-element.33.users_ref, f32[256,256]{1,0:T(8,128)} %copy-done.3, bf16[768,256]{1,0:T(8,128)(2,1)} %get-tuple-element.39.rates_ref.rates0_ref), custom_call_target="tpu_custom_call" | custom-call | flops 201326592 | bytes 2228224 | tf_op jit(solution)/shard_map/pallas_call | solution.py:78
  107.5 0.0 collective-permute-done.7.items1_ref.items_ref
  107.5 0.7 copy-done.7
  108.2 3.4 %shard_map.72 = (f32[768,256]{1,0:T(8,128)}, f32[256,256]{1,0:T(8,128)}) custom-call(f32[768,256]{1,0:T(8,128)} %get-tuple-element.33.users_ref, f32[768,256]{1,0:T(8,128)} %shard_map.70.partial_ref, f32[256,256]{1,0:T(8,128)} %copy-done.7, bf16[768,256]{1,0:T(8,128)(2,1)} %get-tuple-element.38.rates1_ref.rates_ref, f32[256,256]{1,0:T(8,128)} %copy-done.3, ...), custom_call_target="tpu_custom_call" | custom-call | flops 402653184 | bytes 3932160 | tf_op jit(solution)/shard_map/pallas_call | solution.py:78
  111.6 2.6 %shard_map.73 = f32[256,256]{1,0:T(8,128)} custom-call(f32[768,256]{1,0:T(8,128)} %get-tuple-element.18.users_ref, f32[256,256]{1,0:T(8,128)} %copy-done.7, bf16[768,256]{1,0:T(8,128)(2,1)} %get-tuple-element.38.rates1_ref.rates_ref), custom_call_target="tpu_custom_call" | custom-call | flops 201326592 | bytes 1703936 | tf_op jit(solution)/shard_map/pallas_call | solution.py:78
  114.2 0.0 collective-permute-start.9
  114.3 0.0 collective-permute-start.8
  114.3 10.2 %collective-permute-done.9 = f32[256,256]{1,0:T(8,128)S(1)} collective-permute-done((f32[256,256]{1,0:T(8,128)}, f32[256,256]{1,0:T(8,128)S(1)}, u32[]{:S(2)}, u32[]{:S(2)}) %collective-permute-start.9) | collective-permute-done | bytes 262176 | tf_op jit(solution)/shard_map/ppermute | solution.py:32
  124.5 4.6 %collective-permute-done.8 = f32[256,256]{1,0:T(8,128)S(1)} collective-permute-done((f32[256,256]{1,0:T(8,128)}, f32[256,256]{1,0:T(8,128)S(1)}, u32[]{:S(2)}, u32[]{:S(2)}) %collective-permute-start.8) | collective-permute-done | bytes 262176 | tf_op jit(solution)/shard_map/ppermute | solution.py:32
  129.1 0.8 pad_maximum_fusion
  (12 shorter events, 0.0 us)
Async XLA Ops:
  0.6 3.5 %copy-start.8 = (f32[512,256]{1,0:T(8,128)S(1)}, f32[512,256]{1,0:T(8,128)}, u32[]{:S(2)}) copy-start(f32[512,256]{1,0:T(8,128)} %param.5) | copy-start | bytes 1572868
  11.1 16.0 %collective-permute-start = (f32[256,256]{1,0:T(8,128)}, f32[256,256]{1,0:T(8,128)S(1)}, u32[]{:S(2)}, u32[]{:S(2)}) collective-permute-start(f32[256,256]{1,0:T(8,128)} %get-tuple-element.22), channel_id=1, source_target_pairs={{0,4},{4,8},{8,12},{12,16},{16,20},{20,24},{24,28},{28,32},{32,36}... | collective-permute-start | bytes 786440 | tf_op jit(solution)/shard_map/ppermute | solution.py:32
  15.7 16.9 %collective-permute-start.1 = (f32[256,256]{1,0:T(8,128)}, f32[256,256]{1,0:T(8,128)S(1)}, u32[]{:S(2)}, u32[]{:S(2)}) collective-permute-start(f32[256,256]{1,0:T(8,128)} %shard_map.62), channel_id=1, source_target_pairs={{0,4},{4,8},{8,12},{12,16},{16,20},{20,24},{24,28},{28,32},{32,36}... | collective-permute-start | bytes 786440 | tf_op jit(solution)/shard_map/ppermute | solution.py:32
  27.1 0.7 copy-start
  32.7 0.7 copy-start.4
  39.5 20.1 %collective-permute-start.3 = (f32[256,256]{1,0:T(8,128)}, f32[256,256]{1,0:T(8,128)S(1)}, u32[]{:S(2)}, u32[]{:S(2)}) collective-permute-start(f32[256,256]{1,0:T(8,128)} %shard_map.65), channel_id=1, source_target_pairs={{0,4},{4,8},{8,12},{12,16},{16,20},{20,24},{24,28},{28,32},{32,36}... | collective-permute-start | bytes 786440 | tf_op jit(solution)/shard_map/ppermute | solution.py:32
  39.5 16.7 %collective-permute-start.2 = (f32[256,256]{1,0:T(8,128)}, f32[256,256]{1,0:T(8,128)S(1)}, u32[]{:S(2)}, u32[]{:S(2)}) collective-permute-start(f32[256,256]{1,0:T(8,128)} %get-tuple-element.26), channel_id=1, source_target_pairs={{0,4},{4,8},{8,12},{12,16},{16,20},{20,24},{24,28},{28,32},{32,36}... | collective-permute-start | bytes 786440 | tf_op jit(solution)/shard_map/ppermute | solution.py:32
  56.1 0.7 copy-start.1
  59.5 0.7 copy-start.5
  66.3 19.2 %collective-permute-start.5 = (f32[256,256]{1,0:T(8,128)}, f32[256,256]{1,0:T(8,128)S(1)}, u32[]{:S(2)}, u32[]{:S(2)}) collective-permute-start(f32[256,256]{1,0:T(8,128)} %shard_map.68), channel_id=1, source_target_pairs={{0,4},{4,8},{8,12},{12,16},{16,20},{20,24},{24,28},{28,32},{32,36}... | collective-permute-start | bytes 786440 | tf_op jit(solution)/shard_map/ppermute | solution.py:32
  66.3 15.8 %collective-permute-start.4 = (f32[256,256]{1,0:T(8,128)}, f32[256,256]{1,0:T(8,128)S(1)}, u32[]{:S(2)}, u32[]{:S(2)}) collective-permute-start(f32[256,256]{1,0:T(8,128)} %get-tuple-element.30), channel_id=1, source_target_pairs={{0,4},{4,8},{8,12},{12,16},{16,20},{20,24},{24,28},{28,32},{32,36}... | collective-permute-start | bytes 786440 | tf_op jit(solution)/shard_map/ppermute | solution.py:32
  82.1 0.7 copy-start.2
  85.5 0.7 copy-start.6
  92.3 15.2 %collective-permute-start.7 = (f32[256,256]{1,0:T(8,128)}, f32[256,256]{1,0:T(8,128)S(1)}, u32[]{:S(2)}, u32[]{:S(2)}) collective-permute-start(f32[256,256]{1,0:T(8,128)} %shard_map.71), channel_id=1, source_target_pairs={{0,1},{1,2},{2,3},{3,0},{4,5},{5,6},{6,7},{7,4},{8,9},{9,10},{10,1... | collective-permute-start | bytes 786440 | tf_op jit(solution)/shard_map/ppermute | solution.py:32
  97.6 6.4 %collective-permute-start.6 = (f32[256,256]{1,0:T(8,128)}, f32[256,256]{1,0:T(8,128)S(1)}, u32[]{:S(2)}, u32[]{:S(2)}) collective-permute-start(f32[256,256]{1,0:T(8,128)} %get-tuple-element.34), channel_id=1, source_target_pairs={{0,1},{1,2},{2,3},{3,0},{4,5},{5,6},{6,7},{7,4},{8,9},{9,10},{10,1... | collective-permute-start | bytes 786440 | tf_op jit(solution)/shard_map/ppermute | solution.py:32
  104.0 0.7 copy-start.3
  107.5 0.7 copy-start.7
  114.2 10.2 %collective-permute-start.9 = (f32[256,256]{1,0:T(8,128)}, f32[256,256]{1,0:T(8,128)S(1)}, u32[]{:S(2)}, u32[]{:S(2)}) collective-permute-start(f32[256,256]{1,0:T(8,128)} %shard_map.73), channel_id=1, source_target_pairs={{0,247},{1,244},{2,245},{3,246},{4,251},{5,248},{6,249},{7,250},{8... | collective-permute-start | bytes 786440 | tf_op jit(solution)/shard_map/ppermute | solution.py:32
  114.3 14.9 %collective-permute-start.8 = (f32[256,256]{1,0:T(8,128)}, f32[256,256]{1,0:T(8,128)S(1)}, u32[]{:S(2)}, u32[]{:S(2)}) collective-permute-start(f32[256,256]{1,0:T(8,128)} %get-tuple-element.37), channel_id=1, source_target_pairs={{0,247},{1,244},{2,245},{3,246},{4,251},{5,248},{6,249},{7,250},{8... | collective-permute-start | bytes 786440 | tf_op jit(solution)/shard_map/ppermute | solution.py:32
